TPU v7x, 32 devices: a whole 2x2x4 slice. The times are simulated.
32 devices in a mesh: fsdp: 2 (over y), ctx: 4 (over z), tp: 4 (over x, core).
Axes of the slice: x: 2, y: 2, z: 4, core: 2. Of those that a mesh axis runs over, the one named last changes fastest.
Arguments:
- block_input: bfloat16 [4096, 768], P(('fsdp', 'ctx')), may hold values from -6 to 6
- cotangent: bfloat16 [4096, 768], P(('fsdp', 'ctx')), may hold values from -6 to 6
- route_perm: int32 [4096], P('fsdp'), may hold values from 0 to 4095, as said below
- doc_lengths: int32 [2, 4], P('fsdp'), may hold values from 1 to 1024, 2048 in all within a row
- norm_gain: float32 [768], replicated, may hold values from 0.5 to 1.5
- in_proj: float32 [1536, 2, 768], P(('tp', 'fsdp', 'ctx')), may hold values from -0.21875 to 0.21875
- conv_weight: float32 [4, 1536], replicated, may hold values from -3 to 3
- conv_bias: float32 [1536], replicated, may hold values from -3 to 3
- x_proj: float32 [1536, 80], P(('tp', 'fsdp', 'ctx')), may hold values from -0.15625 to 0.15625
- dt_proj: float32 [1536, 48], P(('tp', 'fsdp', 'ctx')), may hold values from -0.875 to 0.875
- dt_bias: float32 [1536], replicated, may hold values from -6.9 to -2.3
- a_log: float32 [16, 1536], replicated, may hold values from -1 to 2.8
- skip_gain: float32 [1536], replicated, may hold values from 0.5 to 1.5
- out_proj: float32 [1536, 768], P(('tp', 'fsdp', 'ctx')), may hold values from -0.15625 to 0.15625
- in_momentum: float32 [1536, 2, 768], P(('tp', 'fsdp', 'ctx')), may hold values from -20 to 20
- x_momentum: float32 [1536, 80], P(('tp', 'fsdp', 'ctx')), may hold values from -20 to 20
- dt_momentum: float32 [1536, 48], P(('tp', 'fsdp', 'ctx')), may hold values from -20 to 20
- out_momentum: float32 [1536, 768], P(('tp', 'fsdp', 'ctx')), may hold values from -20 to 20
- adam_first: float32 [36096], replicated, may hold values from -6 to 6
- adam_second: float32 [36096], replicated, may hold values from 0.1024 to 10.24
- adam_step: int32 [1], replicated, may hold values from 1 to 20
Outputs:
- block_out: bfloat16 [4096, 768], P(('fsdp', 'ctx'))
- input_grad: bfloat16 [4096, 768], P(('fsdp', 'ctx'))
- grad_gain: float32 [768], replicated
- grad_in_proj: float32 [1536, 2, 768], P(('tp', 'fsdp', 'ctx'))
- grad_conv_weight: float32 [4, 1536], replicated
- grad_conv_bias: float32 [1536], replicated
- grad_x_proj: float32 [1536, 80], P(('tp', 'fsdp', 'ctx'))
- grad_dt_proj: float32 [1536, 48], P(('tp', 'fsdp', 'ctx'))
- grad_dt_bias: float32 [1536], replicated
- grad_a_log: float32 [16, 1536], replicated
- grad_skip: float32 [1536], replicated
- grad_out_proj: float32 [1536, 768], P(('tp', 'fsdp', 'ctx'))
- new_gain: float32 [768], replicated
- new_in_proj: float32 [1536, 2, 768], P(('tp', 'fsdp', 'ctx'))
- new_conv_weight: float32 [4, 1536], replicated
- new_conv_bias: float32 [1536], replicated
- new_x_proj: float32 [1536, 80], P(('tp', 'fsdp', 'ctx'))
- new_dt_proj: float32 [1536, 48], P(('tp', 'fsdp', 'ctx'))
- new_dt_bias: float32 [1536], replicated
- new_a_log: float32 [16, 1536], replicated
- new_skip: float32 [1536], replicated
- new_out_proj: float32 [1536, 768], P(('tp', 'fsdp', 'ctx'))
- new_in_momentum: float32 [1536, 2, 768], P(('tp', 'fsdp', 'ctx'))
- new_x_momentum: float32 [1536, 80], P(('tp', 'fsdp', 'ctx'))
- new_dt_momentum: float32 [1536, 48], P(('tp', 'fsdp', 'ctx'))
- new_out_momentum: float32 [1536, 768], P(('tp', 'fsdp', 'ctx'))
- new_adam_first: float32 [36096], replicated
- new_adam_second: float32 [36096], replicated
Inputs may be any that keep to these rules, and one draw needn't show every extreme that they name: route_perm is a permutation of 0 .. 4095 that maps the arrival rows of stream r onto positions of stream r; each aligned block of 512 arrival rows sends exactly 128 rows to each aligned block of 512 positions of its stream. `doc_lengths`: each row sums to 2048; its longest document has exactly 1024 positions.
All inputs are finite; a program needn't handle non-finite values.
Results may differ from a plain program's by a relative error of at most 0.006.
The roundings to bfloat16 on the way count: a program that leaves them out, or rounds other values in their place, can miss the bound.
Values may be sent and summed in bfloat16 or wider, within the bound.
No kernel may reach another device: no remote copies, remote signals or barrier semaphores. Data moves between devices by JAX's collectives and lax.ppermute only.
A program may use at most 256 MiB of HBM per device.

v0:
```python
import math

import jax
import jax.numpy as jnp
from jax import lax
from jax.experimental import pallas as pl
from jax.experimental.pallas import tpu as pltpu
from jax.sharding import PartitionSpec as P

F32 = jnp.float32
BF = jnp.bfloat16
LANES = 128
RESET = 1e5
LOG2E = 1.4426950408889634
VMEM_LIMIT = 60 * 1024 * 1024
NS_A = 3.4445
NS_B = -4.775
NS_C = 2.0315
MOMENTUM = 0.95
MUON_RATE = 0.1
ADAM_RATE = 0.25
BETA_ONE = 0.9
BETA_TWO = 0.95
ADAM_EPS = 1e-08
DECAY_RATE = 0.01
NORM_EPS = 1e-05


def dot_nn(a, b):
    return lax.dot_general(a, b, (((1,), (0,)), ((), ())), preferred_element_type=F32)


def dot_nt(a, b):
    return lax.dot_general(a, b, (((1,), (1,)), ((), ())), preferred_element_type=F32)


def dot_tn(a, b):
    return lax.dot_general(a, b, (((0,), (0,)), ((), ())), preferred_element_type=F32)


def soft(x):
    return jnp.maximum(x, 0.0) + jnp.log1p(jnp.exp(-jnp.abs(x)))


def slope_of(a, s):
    return s * (1.0 + a * (1.0 - s))


def call(body, outs, n_in, n_smem, scratch=(), flops=10**9):
    specs = [pl.BlockSpec(memory_space=pltpu.SMEM)] * n_smem + [
        pl.BlockSpec(memory_space=pltpu.VMEM)
    ] * (n_in - n_smem)
    return pl.pallas_call(
        body,
        out_shape=[jax.ShapeDtypeStruct(s, d) for s, d in outs],
        in_specs=specs,
        out_specs=[pl.BlockSpec(memory_space=pltpu.VMEM)] * len(outs),
        scratch_shapes=list(scratch),
        compiler_params=pltpu.CompilerParams(vmem_limit_bytes=VMEM_LIMIT),
        name=body.__name__,
    )


def rows_iota(r0, rows):
    return lax.broadcasted_iota(jnp.int32, (rows, LANES), 0) + r0


def tap_mask(sc_ref, docs, p, shift):
    ok = jnp.ones(p.shape, F32)
    for j in range(docs):
        off = sc_ref[1 + j]
        ok = jnp.where((off <= p) & (p < off + shift), 0.0, ok)
    return ok


def wide(mask, width):
    return jnp.concatenate([mask] * (width // LANES), axis=1)


def make_front(T, C, D, docs, XW, R):
    RB = 64

    def front(sc, hb, halo, dy, wa, wr, cw, cb, xu_o, z_o, u_o, v_o, pt_o, dg_o, wt_o, xh_o, xpad):
        w0 = wa[...]
        w1 = wr[:, 0:D]
        wo = wr[:, D + LANES : 2 * D + LANES]
        wt = wr[:, D : D + LANES].astype(F32).T.astype(BF)
        wt_o[...] = wt
        c0 = pl.multiple_of(sc[0], LANES)
        xh = dot_nt(halo[...], w0).astype(BF).astype(F32)
        xpad[0:8, :] = xh
        xh_o[...] = xh
        xu = dot_nt(hb[...], w0).astype(BF)
        xu_o[...] = xu
        xpad[8 : 8 + T, :] = xu.astype(F32)
        z_o[...] = dot_nt(hb[...], w1).astype(BF)
        dg_o[...] = dot_nt(dy[...], wo)
        taps = [cw[k : k + 1, pl.ds(c0, C)] for k in range(4)]
        bias = cb[0:1, pl.ds(c0, C)]

        def block(i, carry):
            r0 = i * RB
            p = rows_iota(r0, RB)
            v = bias + jnp.zeros((RB, C), F32)
            full = xpad[pl.ds(r0, RB + 8), :]
            for k in range(4):
                s = 3 - k
                x = full[8 - s : 8 - s + RB]
                if s:
                    x = x * wide(tap_mask(sc, docs, p, s), C)
                v = v + taps[k] * x
            v_o[pl.ds(r0, RB), :] = v
            u_o[pl.ds(r0, RB), :] = (v / (1.0 + jnp.exp(-v))).astype(BF)
            return carry

        lax.fori_loop(0, T // RB, block, 0)
        pt_o[...] = dot_nt(wt[0:XW], u_o[...])

    outs = [((T, C), BF), ((T, C), BF), ((T, C), BF), ((T, C), F32), ((XW, T), F32), ((T, C), F32), ((LANES, C), BF), ((8, C), F32)]
    return call(front, outs, 8, 1, [pltpu.VMEM((T + 8, C), F32)])


def lane_sums(ref):
    def join(a, b, w):
        m = (lax.broadcasted_iota(jnp.int32, a.shape, 2) & w) == 0
        if w == LANES // 2:
            return jnp.where(m, a, b) + pltpu.roll(jnp.where(m, b, a), w, 2)
        return jnp.where(m, a, b) + jnp.where(m, pltpu.roll(a, LANES - w, 2), pltpu.roll(b, w, 2))

    w = LANES // 2
    while w >= 8:

        def chunk(i, c, w=w):
            ref[pl.ds(i * 8, 8)] = join(ref[pl.ds(i * 8, 8)], ref[pl.ds(i * 8 + w, 8)], w)
            return c

        lax.fori_loop(0, w // 8, chunk, 0)
        w //= 2
    x = ref[0:8]
    while w:
        x = join(x[0:w], x[w : 2 * w], w)
        w //= 2
    return x[0]


def make_carry(T, C, docs, XW, R, N, CT):
    RB = 64
    LT = C // LANES

    def carry(sc, pa, pb, u, z, dg, wt, dtb, alog, pt_o, da_o, du_o, dyin_o, pre_o, ends_o):
        c0 = pl.multiple_of(sc[0], LANES)
        pt = pa[...] + pb[...]
        pt_o[...] = pt
        lin = dot_tn(pt[0:R].astype(BF), wt[XW : XW + R, :])
        pre_o[...] = lin + dtb[0:1, pl.ds(c0, C)]

        def block(i, tot):
            rs = pl.ds(i * RB, RB)
            p = rows_iota(i * RB, RB)
            keep = jnp.ones((RB, LANES), F32)
            for j in range(docs):
                keep = jnp.where(p == sc[1 + j], 0.0, keep)
            x = pre_o[rs, :]
            delta = soft(x)
            d = jnp.where(wide(keep, C) > 0.0, delta, RESET)
            r8 = pl.ds(i * (RB // 8), RB // 8)
            da_o[r8] = d.reshape(RB // 8, 8, C)
            du_o[r8] = (delta * u[rs, :].astype(F32)).reshape(RB // 8, 8, C)
            zf = z[rs, :].astype(F32)
            dyin_o[r8] = (dg[rs, :] * (zf / (1.0 + jnp.exp(-zf)))).reshape(RB // 8, 8, C)
            return tot + jnp.sum(d, axis=0, keepdims=True)

        tot = lax.fori_loop(0, T // RB, block, jnp.zeros((1, C), F32))
        am = [-jnp.exp(alog[:, pl.ds(c0 + l * LANES, LANES)]) for l in range(LT)]
        am2 = [a * LOG2E for a in am]

        def rows(ref, i, j):
            full = ref[i, pl.ds(j, N, stride=0), :]
            return [full[:, l * LANES : (l + 1) * LANES] for l in range(LT)]

        nb = T // LANES

        def outer(k, c):
            bt = pt_o[R_ : R_ + N, pl.ds(pl.multiple_of(k * LANES, LANES), LANES)]
            ct = pt_o[R_ + N : R_ + 2 * N, pl.ds(pl.multiple_of((nb - 1 - k) * LANES, LANES), LANES)]

            def inner(i, c):
                h, g, bt, ct = c
                h = list(h)
                g = list(g)
                fi = k * (LANES // 8) + i
                ri = T // 8 - 1 - fi
                for j in range(8):
                    bb = jnp.broadcast_to(bt[:, j : j + 1], (N, LANES))
                    cc = jnp.broadcast_to(ct[:, LANES - 1 - j : LANES - j], (N, LANES))
                    df, uf = rows(da_o, fi, j), rows(du_o, fi, j)
                    db, yb = rows(da_o, ri, 7 - j), rows(dyin_o, ri, 7 - j)
                    for l in range(LT):
                        h[l] = jnp.exp2(df[l] * am2[l]) * h[l] + uf[l] * bb
                        g[l] = jnp.exp2(db[l] * am2[l]) * (g[l] + yb[l] * cc)
                return tuple(h), tuple(g), pltpu.roll(bt, LANES - 8, 1), pltpu.roll(ct, 8, 1)

            h, g, _, _ = lax.fori_loop(0, LANES // 8, inner, (c[0], c[1], bt, ct))
            return h, g

        R_ = R
        zero = tuple(jnp.zeros((N, LANES), F32) for _ in range(LT))
        h, g = lax.fori_loop(0, nb, outer, (zero, zero))
        here = sc[1 + docs]
        for d in range(CT):
            for l in range(LT):
                ends_o[d, 0:N, l * LANES : (l + 1) * LANES] = jnp.where(d > here, h[l], g[l])
            ends_o[d, N : N + 8, :] = jnp.broadcast_to(tot, (8, C))

    outs = [((XW, T), F32)] + [((T // 8, 8, C), F32)] * 3 + [((T, C), F32)] + [((CT, N + 8, C), F32)]
    return call(carry, outs, 9, 1)


def make_scan(T, C, D, docs, XW, R, N, CT):
    RB = 64
    LT = C // LANES
    nb = T // LANES

    def scan(sc, pt, da, du, dyin, pre, u, z, dg, dy, hb, wr, wt, alog, skip, ends,
             g_o, dz_o, du1_o, dpre_o, dp_o, mix_o, pw_o, pdt_o, vec_o,
             a_s, h_s, y_s, lb_s, dd_s, sb_s, sc_s):
        c0 = pl.multiple_of(sc[0], LANES)
        am = [-jnp.exp(alog[:, pl.ds(c0 + l * LANES, LANES)]) for l in range(LT)]
        am2 = [a * LOG2E for a in am]
        sl = [slice(l * LANES, (l + 1) * LANES) for l in range(LT)]
        top4 = lax.broadcasted_iota(jnp.int32, (8, LANES), 0) < 4

        def rows(ref, i, j):
            full = ref[i, pl.ds(j, N, stride=0), :]
            return [full[:, sl[l]] for l in range(LT)]

        here = sc[1 + docs]
        hin, gin = [], []
        for l in range(LT):
            for way, got in ((-1, hin), (1, gin)):
                one = jnp.clip(here + way, 0, CT - 1)
                two = jnp.clip(here + 2 * way, 0, CT - 1)
                prod = jnp.exp2(jnp.broadcast_to(ends[one, N : N + 1, sl[l]], (N, LANES)) * am2[l])
                far = jnp.where(here + 2 * way == two, ends[two, 0:N, sl[l]], 0.0)
                got.append(jnp.where(here + way == one, ends[one, 0:N, sl[l]] + prod * far, 0.0))
            h_s[0, :, sl[l]] = hin[l]

        def fouter(k, h):
            blk = pl.ds(pl.multiple_of(k * LANES, LANES), LANES)
            bt = pt[R : R + N, blk]
            ct = pt[R + N : R + 2 * N, blk]

            def inner(i, c):
                h, bt, ct = c
                h = list(h)
                fi = k * (LANES // 8) + i
                for j in range(8):
                    t = fi * 8 + j
                    bb = jnp.broadcast_to(bt[:, j : j + 1], (N, LANES))
                    cc = jnp.broadcast_to(ct[:, j : j + 1], (N, LANES))
                    dr, ur = rows(da, fi, j), rows(du, fi, j)
                    for l in range(LT):
                        a = jnp.exp2(dr[l] * am2[l])
                        a_s[t, :, sl[l]] = a
                        h[l] = a * h[l] + ur[l] * bb
                        h_s[t + 1, :, sl[l]] = h[l]
                        y_s[fi, j : j + 1, sl[l]] = jnp.sum(h[l] * cc, axis=0, keepdims=True)
                return tuple(h), pltpu.roll(bt, LANES - 8, 1), pltpu.roll(ct, LANES - 8, 1)

            return lax.fori_loop(0, LANES // 8, inner, (h, bt, ct))[0]

        lax.fori_loop(0, nb, fouter, tuple(hin))

        def bouter(k, c):
            kb = nb - 1 - k
            blk = pl.ds(pl.multiple_of(kb * LANES, LANES), LANES)
            bt = pt[R : R + N, blk]
            ct = pt[R + N : R + 2 * N, blk]
            zero = jnp.zeros((N, LANES), F32)

            def inner(i, c):
                g, ga, bt, ct = c
                g = list(g)
                ga = list(ga)
                l0 = LANES - 1 - i * 8
                fi = kb * (LANES // 8) + LANES // 8 - 1 - i
                for j in range(8):
                    t = kb * LANES + l0 - j
                    jj = 7 - j
                    bb = jnp.broadcast_to(bt[:, LANES - 1 - j : LANES - j], (N, LANES))
                    cc = jnp.broadcast_to(ct[:, LANES - 1 - j : LANES - j], (N, LANES))
                    sb = zero
                    scc = zero
                    dr, ur, yr = rows(da, fi, jj), rows(du, fi, jj), rows(dyin, fi, jj)
                    for l in range(LT):
                        dyr = yr[l]
                        lam = cc * dyr + g[l]
                        g[l] = a_s[t, :, sl[l]] * lam
                        dal = g[l] * h_s[t, :, sl[l]]
                        pb = lam * bb
                        pd = dal * am[l]
                        pb = pb[0:8] + pb[8:16]
                        pd = pd[0:8] + pd[8:16]
                        both = jnp.where(top4, pb, pd) + pltpu.roll(jnp.where(top4, pd, pb), 4, 0)
                        both = both + pltpu.roll(both, 6, 0)
                        both = both + pltpu.roll(both, 7, 0)
                        lb_s[fi, jj : jj + 1, sl[l]] = both[0:1]
                        dd_s[fi, jj : jj + 1, sl[l]] = both[4:5]
                        ga[l] = ga[l] + dal * dr[l]
                        sb = sb + lam * ur[l]
                        scc = scc + dyr * h_s[t + 1, :, sl[l]]
                    sb_s[l0 - j] = sb
                    sc_s[l0 - j] = scc
                return tuple(g), tuple(ga), pltpu.roll(bt, 8, 1), pltpu.roll(ct, 8, 1)

            g, ga, _, _ = lax.fori_loop(0, LANES // 8, inner, (c[0], c[1], bt, ct))
            dp_o[R : R + N, blk] = lane_sums(sb_s)
            dp_o[R + N : R + 2 * N, blk] = lane_sums(sc_s)
            return g, ga

        zeros = tuple(jnp.zeros((N, LANES), F32) for _ in range(LT))
        _, ga = lax.fori_loop(0, nb, bouter, (tuple(gin), zeros))
        for l in range(LT):
            vec_o[8 : 8 + N, sl[l]] = am[l] * ga[l]
        skr = skip[0:1, pl.ds(c0, C)]

        def block(i, tot):
            gdt, gsk = tot
            rs = pl.ds(i * RB, RB)
            r8 = pl.ds(i * (RB // 8), RB // 8)
            uf = u[rs, :].astype(F32)
            zf = z[rs, :].astype(F32)
            s = 1.0 / (1.0 + jnp.exp(-zf))
            yin = y_s[r8].reshape(RB, C) + skr * uf
            g_o[rs, :] = (yin * (zf * s)).astype(BF)
            dz_o[rs, :] = (dg[rs, :] * yin * slope_of(zf, s)).astype(BF)
            lb = lb_s[r8].reshape(RB, C)
            dyr = dyin[r8].reshape(RB, C)
            x = pre[rs, :]
            dpre = (lb * uf + dd_s[r8].reshape(RB, C)) / (1.0 + jnp.exp(-x))
            dpre_o[rs, :] = dpre.astype(BF)
            du1_o[rs, :] = dyr * skr + lb * soft(x)
            return gdt + jnp.sum(dpre, axis=0, keepdims=True), gsk + jnp.sum(dyr * uf, axis=0, keepdims=True)

        z1 = jnp.zeros((1, C), F32)
        gdt, gsk = lax.fori_loop(0, T // RB, block, (z1, z1))
        vec_o[5:6, :] = gdt
        vec_o[6:7, :] = gsk
        vec_o[7:8, :] = z1
        vec_o[0:5, :] = jnp.zeros((5, C), F32)
        dp_o[0:R, :] = dot_nt(wt[XW : XW + R, :], dpre_o[...])
        pdt_o[...] = dot_nn(pt[0:R, :].astype(BF), dpre_o[...])
        mix_o[...] = dot_nn(g_o[...], wr[:, D + LANES : 2 * D + LANES]).astype(BF)
        pw_o[:, 0:D] = dot_tn(dz_o[...], hb[...]).astype(BF)
        pw_o[:, D : 2 * D] = dot_tn(g_o[...], dy[...]).astype(BF)

    outs = [((T, C), BF), ((T, C), BF), ((T, C), F32), ((T, C), BF), ((XW, T), F32), ((T, D), BF),
            ((C, 2 * D), BF), ((R, C), F32), ((8 + N, C), F32)]
    scratch = [pltpu.VMEM((T, N, C), F32), pltpu.VMEM((T + 1, N, C), F32)] + [pltpu.VMEM((T // 8, 8, C), F32)] * 3
    scratch += [pltpu.VMEM((LANES, N, LANES), F32)] * 2
    return call(scan, outs, 16, 1, scratch)


def make_back(T, C, D, docs, XW, R):
    RB = 64

    def back(sc, da_, db_, du1, v, u, xu, xhalo, wt, cw, vec, pdt, hb, halo, dxu_o, spill_o, pxt_o, vec_o, pad1, pad2, pad3, xpad):
        c0 = pl.multiple_of(sc[0], LANES)
        dpl = (da_[...] + db_[...]).astype(BF)
        pxt_o[:, D : D + LANES] = jnp.concatenate([dot_nn(dpl, u[...]), pdt[...]], axis=0).T.astype(BF)
        dxu_o[...] = du1[...] + dot_tn(dpl, wt[0:XW, :])
        pads = {1: pad1, 2: pad2, 3: pad3}
        xpad[0:8, :] = xhalo[...]
        xpad[8 : 8 + T, :] = xu[...].astype(F32)
        taps = [cw[k : k + 1, pl.ds(c0, C)] for k in range(4)]
        z8 = jnp.zeros((8, C), F32)
        for s in (1, 2, 3):
            pads[s][0:8, :] = z8
            pads[s][8 + T : 16 + T, :] = z8

        def block(i, tot):
            r0 = i * RB
            rs = pl.ds(r0, RB)
            p = rows_iota(r0, RB)
            vf = v[rs, :]
            sg = 1.0 / (1.0 + jnp.exp(-vf))
            dv = dxu_o[rs, :] * slope_of(vf, sg)
            new = [None] * 5
            full = xpad[pl.ds(r0, RB + 8), :]
            new[4] = tot[4] + jnp.sum(dv, axis=0, keepdims=True)
            for k in range(4):
                s = 3 - k
                x = full[8 - s : 8 - s + RB]
                m = dv
                if s:
                    m = dv * wide(tap_mask(sc, docs, p, s), C)
                    pads[s][pl.ds(8 + r0, RB), :] = taps[k] * m
                else:
                    dxu_o[rs, :] = taps[k] * m
                new[k] = tot[k] + jnp.sum(m * x, axis=0, keepdims=True)
            return tuple(new)

        z1 = jnp.zeros((1, C), F32)
        tot = lax.fori_loop(0, T // RB, block, (z1,) * 5)
        vec_o[...] = vec[...]
        for k in range(5):
            vec_o[k : k + 1, :] = tot[k]

        def gather(i, c):
            r0 = i * RB
            rs = pl.ds(r0, RB)
            acc = dxu_o[rs, :]
            for s in (1, 2, 3):
                acc = acc + pads[s][pl.ds(8 + r0, RB + 8), :][s : s + RB]
            dxu_o[rs, :] = acc
            return c

        lax.fori_loop(0, T // RB, gather, 0)
        acc = z8
        for s in (1, 2, 3):
            acc = acc + pads[s][s : s + 8, :]
        spill_o[...] = acc
        own = dot_tn(dxu_o[...].astype(BF), hb[...])
        pxt_o[:, 0:D] = (own + dot_tn(acc.astype(BF), halo[...])).astype(BF)

    outs = [((T, C), F32), ((8, C), F32), ((C, D + LANES), BF), (None, F32)]

    def build(vrows):
        o = outs[:3] + [((vrows, C), F32)]
        return call(back, o, 14, 1, [pltpu.VMEM((T + 16, C), F32)] * 3 + [pltpu.VMEM((T + 8, C), F32)])

    return build


def make_last(T, C, D, Q):
    def last(dxu, spill, dz, wa, wr, mix, x, rt, keep_o, send_o, gain_o):
        low = jnp.concatenate([jnp.zeros((T - 8, C), F32), spill[...]], axis=0)
        dx = (dxu[...] + low).astype(BF)
        dn = dot_nn(dx, wa[...]) + dot_nn(dz[...], wr[:, 0:D])
        xf = x[...].astype(F32)
        inv = lax.rsqrt(jnp.mean(xf * xf, axis=1, keepdims=True) + NORM_EPS)
        gain_o[...] = jnp.sum(dn * xf * inv, axis=0, keepdims=True)
        dnl = dn.astype(BF)
        for e in range(T // Q):
            r = rt[:, e * Q : (e + 1) * Q]
            o = send_o if e % 2 else keep_o
            at = slice((e // 2) * Q, (e // 2 + 1) * Q)
            o[at, 0:D] = dot_tn(r, mix[...]).astype(BF)
            o[at, D : 2 * D] = dot_tn(r, dnl).astype(BF)

    half = T // 2
    outs = [((half, 2 * D), BF), ((half, 2 * D), BF), ((1, D), F32)]
    return call(last, outs, 8, 0)


def flat_slots(k, shift, share, first):
    return (k >> shift) * share + first + (k & ((1 << shift) - 1))


def make_send(T, D, CT, TP):
    Q = T // TP
    share = T // CT
    SR = share // TP
    shift = SR.bit_length() - 1
    assert SR == 1 << shift and Q == CT * SR

    def send(rsc, perm, x, dy, buf_o, fin_o):
        c = rsc[0]
        tp = rsc[1]
        own = perm[0:1, pl.ds(pl.multiple_of(c * T, LANES), T)].astype(F32)
        r = lax.broadcasted_iota(jnp.int32, (T, T), 0)
        q = lax.broadcasted_iota(jnp.int32, (T, T), 1)
        row = jnp.broadcast_to(own, (T, T))
        col = jnp.broadcast_to(jnp.sum(jnp.where(r == q, row, 0.0), axis=1, keepdims=True), (T, T))
        pos_col = jnp.sum(jnp.where(row < col, 1.0, 0.0), axis=1, keepdims=True)
        pos_row = jnp.sum(jnp.where(col < row, 1.0, 0.0), axis=0, keepdims=True)
        k = lax.broadcasted_iota(jnp.int32, (Q, T), 0)
        pick = jnp.where(flat_slots(k, shift, share, SR * tp).astype(F32) == pos_row, 1.0, 0.0).astype(BF)
        buf_o[:, 0:D] = dot_nn(pick, x[...]).astype(BF)
        buf_o[:, D : 2 * D] = dot_nn(pick, dy[...]).astype(BF)
        f = lax.broadcasted_iota(jnp.int32, (T, Q), 1)
        for e in range(TP):
            slot = flat_slots(f, shift, share, SR * (tp ^ e)).astype(F32)
            fin_o[:, e * Q : (e + 1) * Q] = jnp.where(slot == pos_col, 1.0, 0.0).astype(BF)

    return call(send, [((Q, 2 * D), BF), ((T, T), BF)], 4, 1)


def make_recv(T, D, CT, TP):
    Q = T // TP
    share = T // CT
    SR = share // TP
    shift = SR.bit_length() - 1

    def recv(rsc, perm, gain, *rest):
        parts = rest[:TP]
        x_o, dy_o, hb_o, rt_o = rest[TP:]
        c = rsc[0]
        tp = rsc[1]
        place = (lax.broadcasted_iota(jnp.int32, (T, T), 0) + c * T)
        lane = lax.broadcasted_iota(jnp.int32, (T, LANES), 1)
        hot = jnp.zeros((T, LANES), F32)
        for s in range(CT):
            src = jnp.broadcast_to(perm[0:1, s * T : (s + 1) * T], (T, T))
            n = jnp.sum(jnp.where(src == place, 1.0, 0.0), axis=1, keepdims=True)
            hot = jnp.where(lane == s, n, hot)
        r = lax.broadcasted_iota(jnp.int32, (T, T), 0)
        q = lax.broadcasted_iota(jnp.int32, (T, T), 1)
        below = jnp.where(q < r, 1.0, 0.0).astype(BF)
        count = dot_nn(below, hot.astype(BF))
        rank = jnp.sum(hot * count, axis=1, keepdims=True)
        block = jnp.sum(hot * lane.astype(F32), axis=1, keepdims=True)
        want = block * share + rank
        f = lax.broadcasted_iota(jnp.int32, (T, Q), 1)
        xa = jnp.zeros((T, D), F32)
        ya = jnp.zeros((T, D), F32)
        for e in range(TP):
            slot = flat_slots(f, shift, share, SR * (tp ^ e)).astype(F32)
            m = jnp.where(slot == want, 1.0, 0.0).astype(BF)
            rt_o[:, e * Q : (e + 1) * Q] = m
            xa = xa + dot_nn(m, parts[e][:, 0:D])
            ya = ya + dot_nn(m, parts[e][:, D : 2 * D])
        x_o[...] = xa.astype(BF)
        dy_o[...] = ya.astype(BF)
        inv = lax.rsqrt(jnp.mean(xa * xa, axis=1, keepdims=True) + NORM_EPS)
        hb_o[...] = (xa * inv * gain[...]).astype(BF)

    return call(recv, [((T, D), BF)] * 3 + [((T, T), BF)], 3 + TP, 1)


def make_norm_back(Q, D):
    def norm_back(keep, got, far, own, gain, o):
        both = keep[0:Q].astype(F32) + got[0:Q].astype(F32) + far[...].astype(F32)
        xf = own[:, 0:D].astype(F32)
        inv = lax.rsqrt(jnp.mean(xf * xf, axis=1, keepdims=True) + NORM_EPS)
        dn = both[:, D : 2 * D]
        scaled = gain[...] * dn
        mean = jnp.mean(scaled * xf, axis=1, keepdims=True)
        o[:, 0:D] = (xf + both[:, 0:D]).astype(BF)
        o[:, D : 2 * D] = (
            own[:, D : 2 * D].astype(F32) + inv * scaled - xf * (inv * inv * inv) * mean
        ).astype(BF)

    return call(norm_back, [((Q, 2 * D), BF)], 5, 0)


def make_final(T, D, TP):
    Q = T // TP

    def final(fin, *rest):
        out_o, grad_o = rest[TP:]
        a = jnp.zeros((T, D), F32)
        b = jnp.zeros((T, D), F32)
        for e in range(TP):
            m = fin[:, e * Q : (e + 1) * Q]
            a = a + dot_nn(m, rest[e][:, 0:D])
            b = b + dot_nn(m, rest[e][:, D : 2 * D])
        out_o[...] = a.astype(BF)
        grad_o[...] = b.astype(BF)

    return call(final, [((T, D), BF)] * 2, 1 + TP, 0)


def halves(x):
    hi = x.astype(BF)
    return hi, (x - hi.astype(F32)).astype(BF)


def mul3(ah, al, bh, bl):
    return dot_nn(ah, bh) + (dot_nn(ah, bl) + dot_nn(al, bh))


def gram3(parts):
    def rows_of(i, b, n):
        at = slice(i * b, (i + 1) * b)
        tail = slice(i * b, n)
        tot = None
        for h, l in parts:
            one = dot_tn(h[:, at], h[:, tail]) + (dot_tn(h[:, at], l[:, tail]) + dot_tn(l[:, at], h[:, tail]))
            tot = one if tot is None else tot + one
        return tot

    return rows_of


def put_gram(o, parts, n):
    b = n // 3
    rows_of = gram3(parts)
    o[0:b, :] = rows_of(0, b, n)
    o[b : 2 * b, 0 : 2 * b] = rows_of(1, b, n)
    o[b : 2 * b, 2 * b : n] = rows_of(2, b, n)


def momentum_step(gradient, momentum_old):
    momentum_new = MOMENTUM * momentum_old + gradient
    return (momentum_new, gradient + MOMENTUM * momentum_new)


def add_parts(ref, cols):
    tot = ref[0, :, cols].astype(F32)
    for k in range(1, ref.shape[0]):
        tot = tot + ref[k, :, cols].astype(F32)
    return tot


def make_gram_out(G, rows, D):
    def gram_out(got, mom, g1_o, go_o, mo_o, uo_o, gram_o):
        g1_o[...] = add_parts(got, slice(0, D))
        g = add_parts(got, slice(D, 2 * D))
        m, u = momentum_step(g, mom[...])
        go_o[...] = g
        mo_o[...] = m
        uo_o[...] = u
        put_gram(gram_o, [halves(u)], D)

    outs = [((rows, D), F32)] * 4 + [((2 * D // 3, D), F32)]
    return call(gram_out, outs, 2, 0)


def make_gram_in(G, rows, D, XW, R, VR, pack, full):
    b = D // 3
    top = 2 * b

    def gram_in(place, got, g1, mom, xm, dm, vec, go, uo, gi_o, mi_o, gx_o, mx_o, gd_o, md_o, mine_o, away_o, um_o, ua_o, tmp):
        even = (place[1] & 1) == 0
        parts = []
        us = []
        for q in range(2):
            g = add_parts(got, slice(0, D)) if q == 0 else g1[...]
            m, u = momentum_step(g, mom[:, q, :])
            gi_o[:, q, :] = g
            mi_o[:, q, :] = m
            us.append(u)
            parts.append(halves(u))
        put_gram(tmp, parts, D)
        g = add_parts(got, slice(D, D + LANES))
        m, u = momentum_step(g, jnp.concatenate([xm[...], dm[...]], axis=1))
        gx_o[...] = g[:, 0:XW]
        gd_o[...] = g[:, XW : XW + R]
        mx_o[...] = m[:, 0:XW]
        md_o[...] = m[:, XW : XW + R]
        h, l = halves(u)
        small = dot_tn(h, h) + (dot_tn(h, l) + dot_tn(l, h))

        def put_in(buf, ub):
            buf[0:top, :] = tmp[...]
            buf[top : top + VR, :] = vec[...]
            if full > top + VR:
                buf[top + VR : full, :] = jnp.zeros((full - top - VR, D), F32)
            ub[0:rows, :] = us[0]
            ub[rows : 2 * rows, :] = us[1]

        def put_out(buf, ub):
            buf[0:top, :] = go[...]
            buf[top:full, :] = jnp.zeros((full - top, D), F32)
            for k in range(-(-LANES // pack)):
                lo = k * pack
                hi = min(lo + pack, LANES)
                buf[top : top + hi - lo, k * LANES : (k + 1) * LANES] = small[lo:hi]
            ub[0:rows, :] = uo[...]
            ub[rows : 2 * rows, :] = jnp.zeros((rows, D), F32)
            ub[rows : 2 * rows, 0:LANES] = u

        @pl.when(even)
        def _():
            put_in(mine_o, um_o)
            put_out(away_o, ua_o)

        @pl.when(jnp.logical_not(even))
        def _():
            put_out(mine_o, um_o)
            put_in(away_o, ua_o)

    outs = [((rows, 2, D), F32)] * 2
    outs += [((rows, XW), F32)] * 2 + [((rows, R), F32)] * 2 + [((full, D), F32)] * 2 + [((2 * rows, D), F32)] * 2
    return call(gram_in, outs, 9, 1, [pltpu.VMEM((top, D), F32)])


class Polar:
    def __init__(self, n, nbk, cuts, refs):
        self.n, self.nbk, self.cuts = n, nbk, list(cuts)
        self.blocks = n // nbk
        self.ah, self.al, self.qh, self.ql, self.th, self.tl, self.xs, self.acc = refs

    @staticmethod
    def scratch(n, rows):
        return [pltpu.VMEM((n, n), BF)] * 6 + [pltpu.VMEM((rows, n), F32), pltpu.VMEM((n, n), F32)]

    def at(self, b):
        return slice(b * self.nbk, (b + 1) * self.nbk)

    def put(self, i, value, hi_ref, lo_ref):
        h, l = halves(value)
        b = self.nbk
        hi_ref[self.at(i), i * b : self.n] = h
        lo_ref[self.at(i), i * b : self.n] = l
        for j in range(i + 1, self.blocks):
            h, l = halves(value[:, (j - i) * b : (j - i + 1) * b].T)
            hi_ref[self.at(j), self.at(i)] = h
            lo_ref[self.at(j), self.at(i)] = l

    def start(self, tails, upd):
        n, b = self.n, self.nbk
        col = lax.broadcasted_iota(jnp.int32, (1, n), 1)
        edges = [0] + self.cuts
        inv = jnp.zeros((1, n), F32)
        r = lax.broadcasted_iota(jnp.int32, (b, b), 0)
        c = lax.broadcasted_iota(jnp.int32, (b, b), 1)
        for lo, hi in zip(edges[:-1], edges[1:]):
            tot = jnp.zeros((1, 1), F32)
            for k in range(self.blocks):
                inside = (r == c) & (r + k * b >= lo) & (r + k * b < hi)
                d = jnp.sum(jnp.where(inside, tails[k][:, 0:b], 0.0), axis=1, keepdims=True)
                tot = tot + jnp.sum(d, axis=0, keepdims=True)
            inv = jnp.where((col >= lo) & (col < hi), 1.0 / (jnp.sqrt(tot) + 1e-07), inv)
        self.xs[...] = upd * inv
        for i in range(self.blocks):
            g = tails[i]
            if len(self.cuts) > 1:
                r = lax.broadcasted_iota(jnp.int32, g.shape, 0) + i * b
                c = lax.broadcasted_iota(jnp.int32, g.shape, 1) + i * b
                same = jnp.zeros(g.shape, F32)
                for lo, hi in zip(edges[:-1], edges[1:]):
                    same = jnp.where((r >= lo) & (r < hi) & (c >= lo) & (c < hi), 1.0, same)
                g = g * same
            one = inv[:, i * b : n]
            a = g * (one * one)
            self.acc[self.at(i), i * b : n] = a
            self.put(i, a, self.ah, self.al)

    def apply(self):
        for i in range(self.blocks):
            tail = slice(i * self.nbk, self.n)
            a2 = mul3(self.ah[self.at(i), :], self.al[self.at(i), :], self.ah[:, tail], self.al[:, tail])
            r = lax.broadcasted_iota(jnp.int32, a2.shape, 0)
            c = lax.broadcasted_iota(jnp.int32, a2.shape, 1)
            q = jnp.where(r == c, NS_A, 0.0) + (NS_B * self.acc[self.at(i), tail] + NS_C * a2)
            self.put(i, q, self.qh, self.ql)
        h, l = halves(self.xs[...])
        self.xs[...] = mul3(h, l, self.qh[...], self.ql[...])

    def advance(self):
        for src, dst in (((self.ah, self.al), (self.th, self.tl)), ((self.th, self.tl), (self.ah, self.al))):
            for i in range(self.blocks):
                tail = slice(i * self.nbk, self.n)
                a = mul3(src[0][self.at(i), :], src[1][self.at(i), :], self.qh[:, tail], self.ql[:, tail])
                if dst[0] is self.ah:
                    self.acc[self.at(i), tail] = a
                self.put(i, a, *dst)


def unpack_gram(buf, n):
    b = n // 3
    return [buf[0:b, :], buf[b : 2 * b, 0 : 2 * b], buf[b : 2 * b, 2 * b : n]]


def make_muon(D, rows, XW, R, pack, full):
    top = 2 * (D // 3)

    def muon(buf, um, ua, xm_o, xa_o, *refs):
        p = Polar(D, D // 3, (D,), refs[:8])
        s = Polar(LANES, LANES, (XW, XW + R), refs[8:16])
        small = jnp.concatenate(
            [
                buf[top : top + min(pack, LANES - k * pack), k * LANES : (k + 1) * LANES]
                for k in range(-(-LANES // pack))
            ],
            axis=0,
        )
        p.start(unpack_gram(buf, D), jnp.concatenate([um[...], ua[...]], axis=0))
        s.start([small], jnp.concatenate([um[rows:, 0:LANES], ua[rows:, 0:LANES]], axis=0))

        def step(k, c):
            p.apply()
            s.apply()
            p.advance()
            s.advance()
            return c

        lax.fori_loop(0, 4, step, 0)
        p.apply()
        s.apply()
        xm_o[...] = p.xs[0 : 2 * rows, :]
        xa_o[0:rows, :] = p.xs[2 * rows : 3 * rows, :]
        xa_o[rows : 2 * rows, :] = p.xs[3 * rows : 4 * rows, :]
        return s

    def body(place, buf, um, ua, xm_o, xa_o, *refs):
        s = muon(buf, um, ua, xm_o, xa_o, *refs)

        @pl.when((place[1] & 1) == 1)
        def _():
            xm_o[rows : 2 * rows, 0:LANES] = s.xs[0:rows, :]
            xa_o[rows : 2 * rows, 0:LANES] = s.xs[rows : 2 * rows, :]

    body.__name__ = "muon"
    scratch = Polar.scratch(D, 4 * rows) + Polar.scratch(LANES, 2 * rows)
    return call(body, [((2 * rows, D), F32)] * 2, 4, 1, scratch)


def make_finish(rows, D, XW, R, rates):
    def finish(place, xm, xr, wi, wx, wd, wo, oi, ox, od, oo):
        even = (place[1] & 1) == 0
        for q in range(2):
            at = slice(q * rows, (q + 1) * rows)
            oi[:, q, :] = wi[:, q, :] - rates[0] * jnp.where(even, xm[at], xr[at])
        oo[...] = wo[...] - rates[3] * jnp.where(even, xr[0:rows], xm[0:rows])
        s = jnp.where(even, xr[rows:, 0:LANES], xm[rows:, 0:LANES])
        ox[...] = wx[...] - rates[1] * s[:, 0:XW]
        od[...] = wd[...] - rates[2] * s[:, XW : XW + R]

    outs = [((rows, 2, D), F32), ((rows, XW), F32), ((rows, R), F32), ((rows, D), F32)]
    return call(finish, outs, 7, 1)


def make_pack(rows, D, XW, R):
    def pack(wi, wx, wd, wo, a_o, r_o):
        a_o[...] = wi[:, 0, :].astype(BF)
        r_o[:, 0:D] = wi[:, 1, :].astype(BF)
        r_o[:, D : D + LANES] = jnp.concatenate([wx[...], wd[...]], axis=1).astype(BF)
        r_o[:, D + LANES : 2 * D + LANES] = wo[...].astype(BF)

    return call(pack, [((rows, D), BF), ((rows, 2 * D + LANES), BF)], 4, 0)


def shifted(value, axis, by):
    devices = lax.axis_size(axis)
    pairs = [(i, i + by) for i in range(devices) if 0 <= i + by < devices]
    return lax.ppermute(value, axis, pairs)


def swap(value, axis, bit):
    devices = lax.axis_size(axis)
    return lax.ppermute(value, axis, [(i, i ^ bit) for i in range(devices)])


def side(axis, bit):
    return jnp.where((lax.axis_index(axis) & bit) != 0, 1, 0)


def in_order(mine, theirs, axis, bit):
    low = side(axis, bit) == 0
    return jnp.concatenate([jnp.where(low, mine, theirs), jnp.where(low, theirs, mine)], axis=0)


def half_sum(value, axis, bit):
    half = value.shape[0] // 2
    mine = side(axis, bit) * half
    away = lax.dynamic_slice_in_dim(value, half - mine, half)
    kept = lax.dynamic_slice_in_dim(value, mine, half)
    return kept + swap(away, axis, bit)


def half_join(value, axis, bit):
    return in_order(value, swap(value, axis, bit), axis, bit)


def bits_of(axis):
    count = lax.axis_size(axis)
    return [1 << k for k in range(count.bit_length() - 1)]


def sum_rest(value):
    cols = value.shape[1] // 2
    done = []
    for k in range(2):
        part = value[:, k * cols : (k + 1) * cols]
        cut = [("tp", 2), ("fsdp", 1), ("ctx", 1)] if k == 0 else [("fsdp", 1), ("tp", 2), ("ctx", 1)]
        rest = [(a, b) for a in ("tp", "fsdp", "ctx") for b in bits_of(a) if (a, b) not in cut + [("tp", 1)]]
        for axis, bit in cut:
            part = half_sum(part, axis, bit)
        for axis, bit in rest:
            part = part + swap(part, axis, bit)
        for axis, bit in cut[::-1]:
            part = half_join(part, axis, bit)
        done.append(part)
    return jnp.concatenate(done, axis=1)


def gather_fsdp(value):
    if lax.axis_size("fsdp") == 2:
        return in_order(value, swap(value, "fsdp", 1), "fsdp", 1)
    return lax.all_gather(value, "fsdp", axis=0, tiled=True)


def adam_update(parameters, gradient, moment_one, moment_two, adam_step):
    count = adam_step[0].astype(jnp.float32)
    first_new = BETA_ONE * moment_one + (1.0 - BETA_ONE) * gradient
    second_new = BETA_TWO * moment_two + (1.0 - BETA_TWO) * gradient * gradient
    first_hat = first_new / (1.0 - jnp.power(jnp.float32(BETA_ONE), count))
    second_hat = second_new / (1.0 - jnp.power(jnp.float32(BETA_TWO), count))
    updated = parameters - ADAM_RATE * (
        first_hat / (jnp.sqrt(second_hat) + ADAM_EPS) + DECAY_RATE * parameters
    )
    return (updated, first_new, second_new)


def on_device(
    block_input,
    cotangent,
    route_perm,
    doc_lengths,
    norm_gain,
    in_proj,
    conv_weight,
    conv_bias,
    x_proj,
    dt_proj,
    dt_bias,
    a_log,
    skip_gain,
    out_proj,
    in_momentum,
    x_momentum,
    dt_momentum,
    out_momentum,
    adam_first,
    adam_second,
    adam_step,
):
    ctx_count = lax.axis_size("ctx")
    fsdp_count = lax.axis_size("fsdp")
    tp_count = lax.axis_size("tp")
    owners = fsdp_count * ctx_count
    ctx_index = lax.axis_index("ctx")
    tp_index = lax.axis_index("tp")
    tokens, width = block_input.shape
    stream = tokens * ctx_count
    quarter = tokens // tp_count
    own_rows = in_proj.shape[0]
    channels = own_rows * owners
    inner = conv_bias.shape[0]
    states = a_log.shape[0]
    rank = dt_proj.shape[1]
    xw = x_proj.shape[1]
    lengths = doc_lengths[0]
    docs = lengths.shape[0]
    offsets = jnp.cumsum(lengths) - lengths
    scal = jnp.concatenate([(tp_index * channels)[None], offsets - ctx_index * tokens, ctx_index[None]]).astype(
        jnp.int32
    )
    place = jnp.stack([ctx_index, tp_index]).astype(jnp.int32)
    perm_row = (route_perm % stream).reshape(1, stream)
    gain_row = norm_gain.reshape(1, width)

    w_a, w_r = make_pack(own_rows, width, xw, rank)(in_proj, x_proj, dt_proj, out_proj)
    send, fin = make_send(tokens, width, ctx_count, tp_count)(place, perm_row, block_input, cotangent)
    sent = lax.all_to_all(
        send.reshape(ctx_count, quarter // ctx_count, 2 * width), "ctx", split_axis=0, concat_axis=0, tiled=True
    )
    w_rest = gather_fsdp(lax.all_gather(w_r, "ctx", axis=0, tiled=True))
    w_in = gather_fsdp(lax.all_gather(w_a, "ctx", axis=0, tiled=True))
    own = sent.reshape(quarter, 2 * width)
    far = swap(own, "tp", 2)
    stream_x, stream_dy, normed, route = make_recv(tokens, width, ctx_count, tp_count)(
        place, perm_row, gain_row, own, swap(own, "tp", 1), far, swap(far, "tp", 1)
    )

    halo = shifted(normed[tokens - 8 :], "ctx", 1)
    conv_in, gate_in, conv_act, conv_out, pt_part, d_gated, w_turn, x_halo = make_front(
        tokens, channels, width, docs, xw, rank
    )(scal, normed, halo, stream_dy, w_in, w_rest, conv_weight, conv_bias.reshape(1, inner))
    pt_pair = pt_part + swap(pt_part, "tp", 1)
    pt, dec, drv, d_inner, pre, ends = make_carry(
        tokens, channels, docs, xw, rank, states, ctx_count
    )(scal, pt_pair, swap(pt_pair, "tp", 2), conv_act, gate_in, d_gated, w_turn, dt_bias.reshape(1, inner), a_log)
    ends = lax.all_to_all(ends, "ctx", split_axis=0, concat_axis=0, tiled=True)
    gate_low, d_gate, du_one, d_pre_low, dp_part, mix_part, grads_one, part_dt, vec_part = make_scan(
        tokens, channels, width, docs, xw, rank, states, ctx_count
    )(
        scal, pt, dec, drv, d_inner, pre, conv_act, gate_in, d_gated, stream_dy, normed, w_rest, w_turn, a_log,
        skip_gain.reshape(1, inner), ends,
    )

    def to_owners(grads):
        return lax.all_to_all(
            grads.reshape(owners, own_rows, grads.shape[1]), ("fsdp", "ctx"), split_axis=0, concat_axis=0, tiled=True
        )

    got_one = to_owners(grads_one)
    dp_pair = dp_part + swap(dp_part, "tp", 1)
    d_conv_in, spill, grads_two, vec_chan = make_back(tokens, channels, width, docs, xw, rank)(8 + states)(
        scal, dp_pair, swap(dp_pair, "tp", 2), du_one, conv_out, conv_act, conv_in, x_halo, w_turn, conv_weight,
        vec_part, part_dt, normed, halo,
    )
    got_two = to_owners(grads_two)
    keep, away, g_gain = make_last(tokens, channels, width, quarter)(
        d_conv_in, shifted(spill, "ctx", -1), d_gate, w_in, w_rest, mix_part, stream_x, route
    )

    near = swap(away, "tp", 1)
    cross = (keep[quarter:].astype(F32) + near[quarter:].astype(F32)).astype(BF)
    back = make_norm_back(quarter, width)(keep, near, swap(cross, "tp", 2), own, gain_row)[0]
    home = lax.all_to_all(
        back.reshape(ctx_count, quarter // ctx_count, 2 * width), "ctx", split_axis=0, concat_axis=0, tiled=True
    ).reshape(quarter, 2 * width)
    home_far = swap(home, "tp", 2)
    block_out, input_grad = make_final(tokens, width, tp_count)(
        fin, home, swap(home, "tp", 1), home_far, swap(home_far, "tp", 1)
    )

    kinds = 8 + states
    pack = 24
    vec_wide = lax.dynamic_update_slice(jnp.zeros((kinds, inner), F32), vec_chan, (0, tp_index * channels))
    vec_wide = vec_wide + jnp.pad(g_gain, ((7, kinds - 8), (0, inner - width)))
    vec_rows = kinds * inner // width
    g_one, g_out, mom_out, upd_out, gram_out = make_gram_out(owners, own_rows, width)(got_one, out_momentum)
    top = 2 * (width // 3)
    full = -(-(top + max(vec_rows, pack)) // 64) * 64
    g_in, mom_in, g_x, mom_x, g_dt, mom_dt, gram_mine, gram_away, upd_mine, upd_away = make_gram_in(
        owners, own_rows, width, xw, rank, vec_rows, pack, full
    )(place, got_two, g_one, in_momentum, x_momentum, dt_momentum, vec_wide.reshape(vec_rows, width), gram_out, upd_out)
    gram = sum_rest(gram_mine + swap(gram_away, "tp", 1))
    x_mine, x_away = make_muon(width, own_rows, xw, rank, pack, full)(place, gram, upd_mine, swap(upd_away, "tp", 1))
    rates = [MUON_RATE * 0.2 * math.sqrt(max(a, b)) for a, b in ((2 * inner, width), (inner, xw), (inner, rank), (inner, width))]
    new_in, new_x, new_dt, new_out = make_finish(own_rows, width, xw, rank, rates)(
        place, x_mine, swap(x_away, "tp", 1), in_proj, x_proj, dt_proj, out_proj
    )
    vec_own = gram[top : top + vec_rows]
    vec_sum = jnp.where((tp_index & 1) == 0, vec_own, swap(vec_own, "tp", 1)).reshape(kinds, inner)
    g_alog = vec_sum[8:]
    vec_grads = jnp.concatenate(
        [vec_sum[7, :width], vec_sum[0:4].reshape(-1), vec_sum[4], vec_sum[5], g_alog.reshape(-1), vec_sum[6]]
    )
    vec_params = jnp.concatenate(
        [norm_gain, conv_weight.reshape(-1), conv_bias, dt_bias, a_log.reshape(-1), skip_gain]
    )
    new_vec, first_new, second_new = adam_update(vec_params, vec_grads, adam_first, adam_second, adam_step)
    cut_b = width + 4 * inner
    cut_c = cut_b + inner
    cut_d = cut_c + inner
    cut_e = cut_d + states * inner
    return (
        block_out,
        input_grad,
        vec_sum[7, :width],
        g_in,
        vec_sum[0:4],
        vec_sum[4],
        g_x,
        g_dt,
        vec_sum[5],
        g_alog,
        vec_sum[6],
        g_out,
        new_vec[:width],
        new_in,
        new_vec[width:cut_b].reshape(4, inner),
        new_vec[cut_b:cut_c],
        new_x,
        new_dt,
        new_vec[cut_c:cut_d],
        new_vec[cut_d:cut_e].reshape(states, inner),
        new_vec[cut_e:],
        new_out,
        mom_in,
        mom_x,
        mom_dt,
        mom_out,
        first_new,
        second_new,
    )


def solution(mesh):
    return jax.shard_map(
        on_device,
        mesh=mesh,
        in_specs=(
            P(("fsdp", "ctx"), None),
            P(("fsdp", "ctx"), None),
            P("fsdp"),
            P("fsdp", None),
            P(),
            P(("tp", "fsdp", "ctx"), None, None),
            P(),
            P(),
            P(("tp", "fsdp", "ctx"), None),
            P(("tp", "fsdp", "ctx"), None),
            P(),
            P(),
            P(),
            P(("tp", "fsdp", "ctx"), None),
            P(("tp", "fsdp", "ctx"), None, None),
            P(("tp", "fsdp", "ctx"), None),
            P(("tp", "fsdp", "ctx"), None),
            P(("tp", "fsdp", "ctx"), None),
            P(),
            P(),
            P(),
        ),
        out_specs=(
            P(("fsdp", "ctx"), None),
            P(("fsdp", "ctx"), None),
            P(),
            P(("tp", "fsdp", "ctx"), None, None),
            P(),
            P(),
            P(("tp", "fsdp", "ctx"), None),
            P(("tp", "fsdp", "ctx"), None),
            P(),
            P(),
            P(),
            P(("tp", "fsdp", "ctx"), None),
            P(),
            P(("tp", "fsdp", "ctx"), None, None),
            P(),
            P(),
            P(("tp", "fsdp", "ctx"), None),
            P(("tp", "fsdp", "ctx"), None),
            P(),
            P(),
            P(),
            P(("tp", "fsdp", "ctx"), None),
            P(("tp", "fsdp", "ctx"), None, None),
            P(("tp", "fsdp", "ctx"), None),
            P(("tp", "fsdp", "ctx"), None),
            P(("tp", "fsdp", "ctx"), None),
            P(),
            P(),
        ),
        check_vma=False,
    )
```

profile of v0, /device:TPU:0, one launch (start us, length us, event | category | flops | bytes accessed | tf_op | source)
XLA Modules:
  0.0 344.8 jit_solution(17724262047974831890)
XLA Ops:
  2.6 2.8 send.1
  5.4 6.3 %all-to-all-start = ((bf16[4,32,1536]{2,1,0:T(8,128)(2,1)}), bf16[4,32,1536]{2,1,0:T(8,128)(2,1)S(1)}, u32[]{:S(2)}, u32[]{:S(2)}) async-start(bf16[4,32,1536]{2,1,0:T(8,128)(2,1)} %bitcast.29), calls=%async_computation | async-start | bytes 786432 | tf_op jit(solution)/shard_map/all_to_all | solution.py:948
  11.8 2.2 pack.1
  14.0 17.4 %all_gather.6 = bf16[192,768]{1,0:T(8,128)(2,1)S(1)} all-gather(bf16[48,768]{1,0:T(8,128)(2,1)} %get-tuple-element.91), channel_id=1, replica_groups=mesh['fsdp'=2,'ctx'=4,'tp'=4] {'ctx'}, dimensions={0}, use_global_device_ids=true | all-gather | bytes 368640 | tf_op jit(solution)/shard_map/all_gather | solution.py:952
  31.4 1.5 collective-permute-start.4
  32.9 16.8 %all_gather.7 = bf16[192,1664]{1,0:T(8,128)(2,1)S(1)} all-gather(bf16[48,1664]{1,0:T(8,128)(2,1)} %get-tuple-element.92), channel_id=1, replica_groups=mesh['fsdp'=2,'ctx'=4,'tp'=4] {'ctx'}, dimensions={0}, use_global_device_ids=true | all-gather | bytes 798720 | tf_op jit(solution)/shard_map/all_gather | solution.py:951
  50.5 1.6 collective-permute-start.1
  54.7 3.6 %collective-permute-done.1.rest_2_ = bf16[128,1536]{1,0:T(8,128)(2,1)S(1)} collective-permute-done((bf16[128,1536]{1,0:T(8,128)(2,1)S(1)}, bf16[128,1536]{1,0:T(8,128)(2,1)S(1)}, u32[]{:S(2)}, u32[]{:S(2)}) %collective-permute-start.1) | collective-permute-done | bytes 393248 | tf_op jit(solution)/shard_map/ppermute | solution.py:834
  58.3 1.9 collective-permute-done.5
  61.1 5.5 %recv.1 = (bf16[512,768]{1,0:T(8,128)(2,1)}, bf16[512,768]{1,0:T(8,128)(2,1)}, bf16[512,768]{1,0:T(8,128)(2,1)}, bf16[512,512]{1,0:T(8,128)(2,1)}) custom-call(s32[2]{0:T(128)} %pad_add_fusion.rsc.place, s32[1,2048]{1,0:T(1,128)} %bitcast.31, f32[1,768]{1,0:T(1,128)} %reshape.162.gain, bf16[128,1536]{1,0:T(8,128)(2,1)} %bitcast.21, ...), custom_call_target="tpu_custom_call" | custom-call | tf_op jit(solution)/shard_map/recv/pallas_call | solution.py:955
  70.6 6.5 %front.1 = (bf16[512,384]{1,0:T(8,128)(2,1)}, bf16[512,384]{1,0:T(8,128)(2,1)}, bf16[512,384]{1,0:T(8,128)(2,1)}, f32[512,384]{1,0:T(8,128)}, f32[80,512]{1,0:T(...) custom-call(s32[6]{0:T(128)} %pad_add_fusion.1.sc, ...), custom_call_target="tpu_custom_call" | custom-call | tf_op jit(solution)/shard_map/front/pallas_call | solution.py:960
  77.2 1.6 collective-permute-done.6
  79.7 1.6 collective-permute-start.7
  81.9 4.2 %collective-permute-done.7.pb = f32[80,512]{1,0:T(8,128)S(1)} collective-permute-done((f32[80,512]{1,0:T(8,128)S(1)}, f32[80,512]{1,0:T(8,128)S(1)}, u32[]{:S(2)}, u32[]{:S(2)}) %collective-permute-start.7) | collective-permute-done | bytes 163872 | tf_op jit(solution)/shard_map/ppermute | solution.py:834
  86.7 12.6 %carry.1 = (f32[80,512]{1,0:T(8,128)}, f32[64,8,384]{2,1,0:T(8,128)}, f32[64,8,384]{2,1,0:T(8,128)}, f32[64,8,384]{2,1,0:T(8,128)}, f32[512,384]{1,0:T(8,128)}, /*index=5*/f32[4,24,384]{2,1,0:T(8,128)}) custom-call(s32[6]{0:T(128)} %pad_add_fusion.1.sc, f32[80,512]{1,0:T(8,128)} %copy-done.9, f32[80,512]{1,0:T(8,128)} %copy-done.19, ...), custom_call_target="tpu_custom_call" | custom-call | tf_op jit(solution)/shard_map/carry/pallas_call | solution.py:964
  99.3 5.6 %all-to-all-start.1 = ((f32[4,24,384]{2,1,0:T(8,128)}), f32[4,24,384]{2,1,0:T(8,128)S(1)}, u32[]{:S(2)}, u32[]{:S(2)}) async-start(f32[4,24,384]{2,1,0:T(8,128)} %get-tuple-element.103), calls=%async_computation.1 | async-start | bytes 294912 | tf_op jit(solution)/shard_map/all_to_all | solution.py:967
  105.5 5.4 %all-to-all-done.1.ends = f32[4,24,384]{2,1,0:T(8,128)S(1)} async-done(((f32[4,24,384]{2,1,0:T(8,128)}), f32[4,24,384]{2,1,0:T(8,128)S(1)}, u32[]{:S(2)}, u32[]{:S(2)}) %all-to-all-start.1) | async-done | bytes 147488 | tf_op jit(solution)/shard_map/all_to_all | solution.py:967
  111.6 39.7 %scan.1 = (bf16[512,384]{1,0:T(8,128)(2,1)}, bf16[512,384]{1,0:T(8,128)(2,1)}, f32[512,384]{1,0:T(8,128)}, bf16[512,384]{1,0:T(8,128)(2,1)}, f32[80,512]{1,0:T(8...) custom-call(s32[6]{0:T(128)} %pad_add_fusion.1.sc, ...), custom_call_target="tpu_custom_call" | custom-call | tf_op jit(solution)/shard_map/scan/pallas_call | solution.py:968
  151.3 3.7 %all-to-all-start.4 = ((bf16[8,48,1536]{2,1,0:T(8,128)(2,1)}), bf16[8,48,1536]{2,1,0:T(8,128)(2,1)S(1)}, u32[]{:S(2)}, u32[]{:S(2)}) async-start(bf16[8,48,1536]{2,1,0:T(8,128)(2,1)} %bitcast.27), calls=%async_computation.4 | async-start | bytes 2359296 | tf_op jit(solution)/shard_map/all_to_all | solution.py:976
  155.1 1.4 collective-permute-done.8
  156.5 1.6 collective-permute-start.9
  158.1 4.8 %collective-permute-done.9.db_ = f32[80,512]{1,0:T(8,128)S(1)} collective-permute-done((f32[80,512]{1,0:T(8,128)S(1)}, f32[80,512]{1,0:T(8,128)S(1)}, u32[]{:S(2)}, u32[]{:S(2)}) %collective-permute-start.9) | collective-permute-done | bytes 163872 | tf_op jit(solution)/shard_map/ppermute | solution.py:834
  163.5 5.8 %back.1 = (f32[512,384]{1,0:T(8,128)}, f32[8,384]{1,0:T(8,128)}, bf16[384,896]{1,0:T(8,128)(2,1)}, f32[24,384]{1,0:T(8,128)}) custom-call(s32[6]{0:T(128)} %pad_add_fusion.1.sc, f32[80,512]{1,0:T(8,128)} %copy-done.8, f32[80,512]{1,0:T(8,128)} %copy-done.17, f32[512,384]{1,0:T(8,128)} %get-tuple-element.105.du1, f32[512,384]{1,0:T(8,128)} %get-tuple-element.106.v, ...), custom_call_target="tpu_custom_call" | custom-call | tf_op jit(solution)/shard_map/back/pallas_call | solution.py:982
  169.3 13.4 %all-to-all-done.4.got = bf16[8,48,1536]{2,1,0:T(8,128)(2,1)S(1)} async-done(((bf16[8,48,1536]{2,1,0:T(8,128)(2,1)}), bf16[8,48,1536]{2,1,0:T(8,128)(2,1)S(1)}, u32[]{:S(2)}, u32[]{:S(2)}) %all-to-all-start.4) | async-done | bytes 1179680 | tf_op jit(solution)/shard_map/all_to_all | solution.py:976
  182.7 3.5 %all-to-all-start.3 = ((bf16[8,48,896]{2,1,0:T(8,128)(2,1)}), bf16[8,48,896]{2,1,0:T(8,128)(2,1)S(1)}, u32[]{:S(2)}, u32[]{:S(2)}) async-start(bf16[8,48,896]{2,1,0:T(8,128)(2,1)} %bitcast.28), calls=%async_computation.3 | async-start | bytes 1376256 | tf_op jit(solution)/shard_map/all_to_all | solution.py:976
  186.2 1.5 collective-permute-start.10
  187.7 5.4 %collective-permute-done.10.spill = f32[8,384]{1,0:T(8,128)S(1)} collective-permute-done((f32[8,384]{1,0:T(8,128)}, f32[8,384]{1,0:T(8,128)S(1)}, u32[]{:S(2)}, u32[]{:S(2)}) %collective-permute-start.10) | collective-permute-done | bytes 12320 | tf_op jit(solution)/shard_map/ppermute | solution.py:829
  193.7 5.5 %last.1 = (bf16[256,1536]{1,0:T(8,128)(2,1)}, bf16[256,1536]{1,0:T(8,128)(2,1)}, f32[1,768]{1,0:T(1,128)}) custom-call(f32[512,384]{1,0:T(8,128)} %get-tuple-element.111.dxu, f32[8,384]{1,0:T(8,128)} %copy-done.35, bf16[512,384]{1,0:T(8,128)(2,1)} %get-tuple-element.113.dz, bf16[384,768]{1,0:T(8,128)(2,1)} %pad_maximum_fusion.1.wa, ...), custom_call_target="tpu_custom_call" | custom-call | tf_op jit(solution)/shard_map/last/pallas_call | solution.py:987
  201.4 3.4 gram_out.1
  205.6 6.0 %gram_in.1 = (f32[48,2,768]{2,1,0:T(2,128)}, f32[48,2,768]{2,1,0:T(2,128)}, f32[48,80]{1,0:T(8,128)}, f32[48,80]{1,0:T(8,128)}, f32[48,48]{1,0:T(8,128)}, /*inde...) custom-call(s32[2]{0:T(128)} %pad_add_fusion.rsc.place, ...), custom_call_target="tpu_custom_call" | custom-call | tf_op jit(solution)/shard_map/gram_in/pallas_call | solution.py:1010
  212.1 3.4 collective-permute-done.16
  215.5 1.7 add.109
  218.1 1.5 collective-permute-start.24
  224.8 8.1 %collective-permute-done.12.far = bf16[128,1536]{1,0:T(8,128)(2,1)} collective-permute-done((bf16[128,1536]{1,0:T(8,128)(2,1)}, bf16[128,1536]{1,0:T(8,128)(2,1)}, u32[]{:S(2)}, u32[]{:S(2)}) %collective-permute-start.12) | collective-permute-done | bytes 393248 | tf_op jit(solution)/shard_map/ppermute | solution.py:834
  232.9 2.7 norm_back.1
  235.6 11.7 %all-to-all-start.2 = ((bf16[4,32,1536]{2,1,0:T(8,128)(2,1)}), bf16[4,32,1536]{2,1,0:T(8,128)(2,1)S(1)}, u32[]{:S(2)}, u32[]{:S(2)}) async-start(bf16[4,32,1536]{2,1,0:T(8,128)(2,1)} %bitcast.26), calls=%async_computation.2 | async-start | bytes 786432 | tf_op jit(solution)/shard_map/all_to_all | solution.py:994
  250.1 3.4 collective-permute-done.25
  253.5 3.0 collective-permute-start.26
  256.6 3.5 %collective-permute-start.19 = (f32[72,384]{1,0:T(8,128)S(1)}, f32[72,384]{1,0:T(8,128)S(1)}, u32[]{:S(2)}, u32[]{:S(2)}) collective-permute-start(f32[72,384]{1,0:T(8,128)S(1)} %constant_dynamic-slice_fusion.3), channel_id=1, source_target_pairs={{0,4},{4,0},{8,12},{12,8},{1,5},{5,1},{9,13},{13,9},{2,6},{6,2},{1... | collective-permute-start | bytes 331784 | tf_op jit(solution)/shard_map/ppermute | solution.py:834
  261.3 2.2 collective-permute-done.19
  264.1 4.6 %collective-permute-done.27 = f32[72,384]{1,0:T(8,128)S(1)} collective-permute-done((f32[72,384]{1,0:T(8,128)S(1)}, f32[72,384]{1,0:T(8,128)S(1)}, u32[]{:S(2)}, u32[]{:S(2)}) %collective-permute-start.27) | collective-permute-done | bytes 110624 | tf_op jit(solution)/shard_map/ppermute | solution.py:834
  271.2 2.0 collective-permute-start.21
  274.6 1.4 collective-permute-done.21
  276.7 6.6 %collective-permute-done.29 = f32[144,384]{1,0:T(8,128)S(1)} collective-permute-done((f32[144,384]{1,0:T(8,128)S(1)}, f32[144,384]{1,0:T(8,128)S(1)}, u32[]{:S(2)}, u32[]{:S(2)}) %collective-permute-start.29) | collective-permute-done | bytes 221216 | tf_op jit(solution)/shard_map/ppermute | solution.py:834
  288.9 2.8 collective-permute-done.30
  297.3 4.3 %final.1 = (bf16[512,768]{1,0:T(8,128)(2,1)}, bf16[512,768]{1,0:T(8,128)(2,1)}) custom-call(bf16[512,512]{1,0:T(8,128)(2,1)} %get-tuple-element.87.fin, bf16[128,1536]{1,0:T(8,128)(2,1)} %bitcast.25, bf16[128,1536]{1,0:T(8,128)(2,1)} %copy-done.12, bf16[128,1536]{1,0:T(8,128)(2,1)} %copy-done.11, bf16[128,1536]{1,0:T(8,128)(2,1)} %collective-permute-done.15.rest_3_), custom_call_target="tpu_custom_call" | custom-call | tf_op jit(solution)/shard_map/final/pallas_call | solution.py:998
  301.7 33.7 %muon.1 = (f32[96,768]{1,0:T(8,128)}, f32[96,768]{1,0:T(8,128)}) custom-call(s32[2]{0:T(128)} %pad_add_fusion.rsc.place, f32[576,768]{1,0:T(8,128)} %copy-done, f32[96,768]{1,0:T(8,128)} %get-tuple-element.134.um, f32[96,768]{1,0:T(8,128)} %collective-permute-done.32.ua), custom_call_target="tpu_custom_call" | custom-call | tf_op jit(solution)/shard_map/muon/pallas_call | solution.py:1014
  342.5 2.2 finish.1
  (204 shorter events, 51.1 us)
Async XLA Ops:
  2.6 47.7 %copy-start.36 = (s32[1,4]{1,0:T(1,128)S(1)}, s32[1,4]{1,0:T(1,128)}, u32[]{:S(2)}) copy-start(s32[1,4]{1,0:T(1,128)} %param.24) | copy-start | bytes 52
  2.6 50.1 %copy-start.33 = (f32[768]{0:T(1024)S(1)}, f32[768]{0:T(1024)}, u32[]{:S(2)}) copy-start(f32[768]{0:T(1024)} %param.25) | copy-start | bytes 9220
  2.6 50.6 %copy-start.27 = (f32[1536]{0:T(1024)S(1)}, f32[1536]{0:T(1024)}, u32[]{:S(2)}) copy-start(f32[1536]{0:T(1024)} %param.28) | copy-start | bytes 18436
  5.4 45.1 %all-to-all-start = ((bf16[4,32,1536]{2,1,0:T(8,128)(2,1)}), bf16[4,32,1536]{2,1,0:T(8,128)(2,1)S(1)}, u32[]{:S(2)}, u32[]{:S(2)}) async-start(bf16[4,32,1536]{2,1,0:T(8,128)(2,1)} %bitcast.29), calls=%async_computation | async-start | bytes 786432 | tf_op jit(solution)/shard_map/all_to_all | solution.py:948
  31.4 22.4 %collective-permute-start.4 = (bf16[192,768]{1,0:T(8,128)(2,1)S(1)}, bf16[192,768]{1,0:T(8,128)(2,1)S(1)}, u32[]{:S(2)}, u32[]{:S(2)}) collective-permute-start(bf16[192,768]{1,0:T(8,128)(2,1)S(1)} %all_gather.6), channel_id=1, source_target_pairs={{0,16},{16,0},{1,17},{17,1},{2,18},{18,2},{3,19},{19,3},{4,20},{20... | collective-permute-start | bytes 884744 | tf_op jit(solution)/shard_map/ppermute | solution.py:834
  49.8 10.4 %collective-permute-start.5 = (bf16[192,1664]{1,0:T(8,128)(2,1)S(1)}, bf16[192,1664]{1,0:T(8,128)(2,1)S(1)}, u32[]{:S(2)}, u32[]{:S(2)}) collective-permute-start(bf16[192,1664]{1,0:T(8,128)(2,1)S(1)} %all_gather.7), channel_id=1, source_target_pairs={{0,16},{16,0},{1,17},{17,1},{2,18},{18,2},{3,19},{19,3},{4,20},{20... | collective-permute-start | bytes 1916936 | tf_op jit(solution)/shard_map/ppermute | solution.py:834
  50.5 7.8 %collective-permute-start.1 = (bf16[128,1536]{1,0:T(8,128)(2,1)S(1)}, bf16[128,1536]{1,0:T(8,128)(2,1)S(1)}, u32[]{:S(2)}, u32[]{:S(2)}) collective-permute-start(bf16[128,1536]{1,0:T(8,128)(2,1)S(1)} %bitcast.19), channel_id=1, source_target_pairs={{0,2},{1,3},{2,0},{3,1},{4,6},{5,7},{6,4},{7,5},{8,10},{9,11},{10,... | collective-permute-start | bytes 1179656 | tf_op jit(solution)/shard_map/ppermute | solution.py:834
  54.7 5.6 %collective-permute-start = (bf16[128,1536]{1,0:T(8,128)(2,1)S(1)}, bf16[128,1536]{1,0:T(8,128)(2,1)S(1)}, u32[]{:S(2)}, u32[]{:S(2)}) collective-permute-start(bf16[128,1536]{1,0:T(8,128)(2,1)S(1)} %bitcast.20), channel_id=1, source_target_pairs={{0,1},{1,0},{2,3},{3,2},{4,5},{5,4},{6,7},{7,6},{8,9},{9,8},{10,11... | collective-permute-start | bytes 1179656 | tf_op jit(solution)/shard_map/ppermute | solution.py:834
  58.3 2.0 collective-permute-start.2
  67.3 2.7 collective-permute-start.3
  77.1 27.8 %copy-start.29 = (f32[1536]{0:T(1024)S(1)}, f32[1536]{0:T(1024)}, u32[]{:S(2)}) copy-start(f32[1536]{0:T(1024)} %param.33) | copy-start | bytes 18436
  77.1 1.7 collective-permute-start.6
  79.7 6.3 %collective-permute-start.7 = (f32[80,512]{1,0:T(8,128)S(1)}, f32[80,512]{1,0:T(8,128)S(1)}, u32[]{:S(2)}, u32[]{:S(2)}) collective-permute-start(f32[80,512]{1,0:T(8,128)S(1)} %add.104.pa), channel_id=1, source_target_pairs={{0,2},{1,3},{2,0},{3,1},{4,6},{5,7},{6,4},{7,5},{8,10},{9,11},{10,... | collective-permute-start | bytes 491528 | tf_op jit(solution)/shard_map/ppermute | solution.py:834
  99.3 11.5 %all-to-all-start.1 = ((f32[4,24,384]{2,1,0:T(8,128)}), f32[4,24,384]{2,1,0:T(8,128)S(1)}, u32[]{:S(2)}, u32[]{:S(2)}) async-start(f32[4,24,384]{2,1,0:T(8,128)} %get-tuple-element.103), calls=%async_computation.1 | async-start | bytes 294912 | tf_op jit(solution)/shard_map/all_to_all | solution.py:967
  151.3 31.4 %all-to-all-start.4 = ((bf16[8,48,1536]{2,1,0:T(8,128)(2,1)}), bf16[8,48,1536]{2,1,0:T(8,128)(2,1)S(1)}, u32[]{:S(2)}, u32[]{:S(2)}) async-start(bf16[8,48,1536]{2,1,0:T(8,128)(2,1)} %bitcast.27), calls=%async_computation.4 | async-start | bytes 2359296 | tf_op jit(solution)/shard_map/all_to_all | solution.py:976
  155.0 1.5 collective-permute-start.8
  156.5 6.3 %collective-permute-start.9 = (f32[80,512]{1,0:T(8,128)S(1)}, f32[80,512]{1,0:T(8,128)S(1)}, u32[]{:S(2)}, u32[]{:S(2)}) collective-permute-start(f32[80,512]{1,0:T(8,128)S(1)} %add.105.da_), channel_id=1, source_target_pairs={{0,2},{1,3},{2,0},{3,1},{4,6},{5,7},{6,4},{7,5},{8,10},{9,11},{10,... | collective-permute-start | bytes 491528 | tf_op jit(solution)/shard_map/ppermute | solution.py:834
  182.7 16.5 %copy-start.1 = (bf16[8,48,1536]{2,1,0:T(8,128)(2,1)}, bf16[8,48,1536]{2,1,0:T(8,128)(2,1)S(1)}, u32[]{:S(2)}) copy-start(bf16[8,48,1536]{2,1,0:T(8,128)(2,1)S(1)} %all-to-all-done.4.got) | copy-start | bytes 3538948
  182.7 22.1 %all-to-all-start.3 = ((bf16[8,48,896]{2,1,0:T(8,128)(2,1)}), bf16[8,48,896]{2,1,0:T(8,128)(2,1)S(1)}, u32[]{:S(2)}, u32[]{:S(2)}) async-start(bf16[8,48,896]{2,1,0:T(8,128)(2,1)} %bitcast.28), calls=%async_computation.3 | async-start | bytes 1376256 | tf_op jit(solution)/shard_map/all_to_all | solution.py:976
  186.2 6.9 %collective-permute-start.10 = (f32[8,384]{1,0:T(8,128)}, f32[8,384]{1,0:T(8,128)S(1)}, u32[]{:S(2)}, u32[]{:S(2)}) collective-permute-start(f32[8,384]{1,0:T(8,128)} %get-tuple-element.112), channel_id=1, source_target_pairs={{4,0},{8,4},{12,8},{5,1},{9,5},{13,9},{6,2},{10,6},{14,10},{7,3},{... | collective-permute-start | bytes 36872 | tf_op jit(solution)/shard_map/ppermute | solution.py:829
  211.6 3.9 %collective-permute-start.16 = (f32[576,768]{1,0:T(8,128)}, f32[576,768]{1,0:T(8,128)S(1)}, u32[]{:S(2)}, u32[]{:S(2)}) collective-permute-start(f32[576,768]{1,0:T(8,128)} %get-tuple-element.129), channel_id=1, source_target_pairs={{0,1},{1,0},{2,3},{3,2},{4,5},{5,4},{6,7},{7,6},{8,9},{9,8},{10,11... | collective-permute-start | bytes 5308424 | tf_op jit(solution)/shard_map/ppermute | solution.py:834
  211.6 8.0 %collective-permute-start.11 = (bf16[256,1536]{1,0:T(8,128)(2,1)}, bf16[256,1536]{1,0:T(8,128)(2,1)S(1)}, u32[]{:S(2)}, u32[]{:S(2)}) collective-permute-start(bf16[256,1536]{1,0:T(8,128)(2,1)} %get-tuple-element.118), channel_id=1, source_target_pairs={{0,1},{1,0},{2,3},{3,2},{4,5},{5,4},{6,7},{7,6},{8,9},{9,8},{10,11... | collective-permute-start | bytes 2359304 | tf_op jit(solution)/shard_map/ppermute | solution.py:834
  218.1 29.2 %collective-permute-start.24 = (f32[288,384]{1,0:T(8,128)}, f32[288,384]{1,0:T(8,128)S(1)}, u32[]{:S(2)}, u32[]{:S(2)}) collective-permute-start(f32[288,384]{1,0:T(8,128)} %constant_dynamic-slice_fusion.2), channel_id=1, source_target_pairs={{0,16},{16,0},{1,17},{17,1},{2,18},{18,2},{3,19},{19,3},{4,20},{20... | collective-permute-start | bytes 1327112 | tf_op jit(solution)/shard_map/ppermute | solution.py:834
  220.6 12.3 %collective-permute-start.12 = (bf16[128,1536]{1,0:T(8,128)(2,1)}, bf16[128,1536]{1,0:T(8,128)(2,1)}, u32[]{:S(2)}, u32[]{:S(2)}) collective-permute-start(bf16[128,1536]{1,0:T(8,128)(2,1)} %add_convert_fusion), channel_id=1, source_target_pairs={{0,2},{1,3},{2,0},{3,1},{4,6},{5,7},{6,4},{7,5},{8,10},{9,11},{10,... | collective-permute-start | bytes 1179656 | tf_op jit(solution)/shard_map/ppermute | solution.py:834
  222.3 26.1 %collective-permute-start.17 = (f32[288,384]{1,0:T(8,128)}, f32[288,384]{1,0:T(8,128)}, u32[]{:S(2)}, u32[]{:S(2)}) collective-permute-start(f32[288,384]{1,0:T(8,128)} %constant_dynamic-slice_fusion.5), channel_id=1, source_target_pairs={{0,2},{1,3},{2,0},{3,1},{4,6},{5,7},{6,4},{7,5},{8,10},{9,11},{10,... | collective-permute-start | bytes 1327112 | tf_op jit(solution)/shard_map/ppermute | solution.py:834
  235.6 34.6 %all-to-all-start.2 = ((bf16[4,32,1536]{2,1,0:T(8,128)(2,1)}), bf16[4,32,1536]{2,1,0:T(8,128)(2,1)S(1)}, u32[]{:S(2)}, u32[]{:S(2)}) async-start(bf16[4,32,1536]{2,1,0:T(8,128)(2,1)} %bitcast.26), calls=%async_computation.2 | async-start | bytes 786432 | tf_op jit(solution)/shard_map/all_to_all | solution.py:994
  247.5 6.0 %collective-permute-start.25 = (f32[144,384]{1,0:T(8,128)S(1)}, f32[144,384]{1,0:T(8,128)S(1)}, u32[]{:S(2)}, u32[]{:S(2)}) collective-permute-start(f32[144,384]{1,0:T(8,128)S(1)} %constant_dynamic-slice_fusion.1), channel_id=1, source_target_pairs={{0,2},{1,3},{2,0},{3,1},{4,6},{5,7},{6,4},{7,5},{8,10},{9,11},{10,... | collective-permute-start | bytes 663560 | tf_op jit(solution)/shard_map/ppermute | solution.py:834
  249.4 7.1 %collective-permute-start.18 = (f32[144,384]{1,0:T(8,128)S(1)}, f32[144,384]{1,0:T(8,128)S(1)}, u32[]{:S(2)}, u32[]{:S(2)}) collective-permute-start(f32[144,384]{1,0:T(8,128)S(1)} %constant_dynamic-slice_fusion.4), channel_id=1, source_target_pairs={{0,16},{16,0},{1,17},{17,1},{2,18},{18,2},{3,19},{19,3},{4,20},{20... | collective-permute-start | bytes 663560 | tf_op jit(solution)/shard_map/ppermute | solution.py:834
  253.5 6.8 %collective-permute-start.26 = (f32[72,384]{1,0:T(8,128)S(1)}, f32[72,384]{1,0:T(8,128)S(1)}, u32[]{:S(2)}, u32[]{:S(2)}) collective-permute-start(f32[72,384]{1,0:T(8,128)S(1)} %constant_dynamic-slice_fusion), channel_id=1, source_target_pairs={{0,4},{4,0},{8,12},{12,8},{1,5},{5,1},{9,13},{13,9},{2,6},{6,2},{1... | collective-permute-start | bytes 331784 | tf_op jit(solution)/shard_map/ppermute | solution.py:834
  256.6 6.9 %collective-permute-start.19 = (f32[72,384]{1,0:T(8,128)S(1)}, f32[72,384]{1,0:T(8,128)S(1)}, u32[]{:S(2)}, u32[]{:S(2)}) collective-permute-start(f32[72,384]{1,0:T(8,128)S(1)} %constant_dynamic-slice_fusion.3), channel_id=1, source_target_pairs={{0,4},{4,0},{8,12},{12,8},{1,5},{5,1},{9,13},{13,9},{2,6},{6,2},{1... | collective-permute-start | bytes 331784 | tf_op jit(solution)/shard_map/ppermute | solution.py:834
  260.4 8.3 %collective-permute-start.27 = (f32[72,384]{1,0:T(8,128)S(1)}, f32[72,384]{1,0:T(8,128)S(1)}, u32[]{:S(2)}, u32[]{:S(2)}) collective-permute-start(f32[72,384]{1,0:T(8,128)S(1)} %dynamic-slice_add_fusion.4), channel_id=1, source_target_pairs={{0,8},{4,12},{8,0},{12,4},{1,9},{5,13},{9,1},{13,5},{2,10},{6,14},... | collective-permute-start | bytes 331784 | tf_op jit(solution)/shard_map/ppermute | solution.py:834
  263.5 7.6 %collective-permute-start.20 = (f32[72,384]{1,0:T(8,128)S(1)}, f32[72,384]{1,0:T(8,128)S(1)}, u32[]{:S(2)}, u32[]{:S(2)}) collective-permute-start(f32[72,384]{1,0:T(8,128)S(1)} %dynamic-slice_add_fusion.5), channel_id=1, source_target_pairs={{0,8},{4,12},{8,0},{12,4},{1,9},{5,13},{9,1},{13,5},{2,10},{6,14},... | collective-permute-start | bytes 331784 | tf_op jit(solution)/shard_map/ppermute | solution.py:834
  268.7 4.8 %collective-permute-start.28 = (f32[72,384]{1,0:T(8,128)S(1)}, f32[72,384]{1,0:T(8,128)S(1)}, u32[]{:S(2)}, u32[]{:S(2)}) collective-permute-start(f32[72,384]{1,0:T(8,128)S(1)} %add.127), channel_id=1, source_target_pairs={{0,4},{4,0},{8,12},{12,8},{1,5},{5,1},{9,13},{13,9},{2,6},{6,2},{1... | collective-permute-start | bytes 331784 | tf_op jit(solution)/shard_map/ppermute | solution.py:834
  270.2 18.0 %copy-start.6 = (bf16[4,32,1536]{2,1,0:T(8,128)(2,1)}, bf16[4,32,1536]{2,1,0:T(8,128)(2,1)S(1)}, u32[]{:S(2)}) copy-start(bf16[4,32,1536]{2,1,0:T(8,128)(2,1)S(1)} %all-to-all-done.2) | copy-start | bytes 1179652
  270.2 18.6 %collective-permute-start.14 = (bf16[128,1536]{1,0:T(8,128)(2,1)S(1)}, bf16[128,1536]{1,0:T(8,128)(2,1)S(1)}, u32[]{:S(2)}, u32[]{:S(2)}) collective-permute-start(bf16[128,1536]{1,0:T(8,128)(2,1)S(1)} %bitcast.23), channel_id=1, source_target_pairs={{0,2},{1,3},{2,0},{3,1},{4,6},{5,7},{6,4},{7,5},{8,10},{9,11},{10,... | collective-permute-start | bytes 1179656 | tf_op jit(solution)/shard_map/ppermute | solution.py:834
  271.2 4.8 %collective-permute-start.21 = (f32[72,384]{1,0:T(8,128)S(1)}, f32[72,384]{1,0:T(8,128)S(1)}, u32[]{:S(2)}, u32[]{:S(2)}) collective-permute-start(f32[72,384]{1,0:T(8,128)S(1)} %add.119), channel_id=1, source_target_pairs={{0,4},{4,0},{8,12},{12,8},{1,5},{5,1},{9,13},{13,9},{2,6},{6,2},{1... | collective-permute-start | bytes 331784 | tf_op jit(solution)/shard_map/ppermute | solution.py:834
  273.6 9.7 %collective-permute-start.29 = (f32[144,384]{1,0:T(8,128)S(1)}, f32[144,384]{1,0:T(8,128)S(1)}, u32[]{:S(2)}, u32[]{:S(2)}) collective-permute-start(f32[144,384]{1,0:T(8,128)S(1)} %pad_maximum_fusion.5), channel_id=1, source_target_pairs={{0,2},{1,3},{2,0},{3,1},{4,6},{5,7},{6,4},{7,5},{8,10},{9,11},{10,... | collective-permute-start | bytes 663560 | tf_op jit(solution)/shard_map/ppermute | solution.py:834
  276.0 8.4 %collective-permute-start.22 = (f32[144,384]{1,0:T(8,128)S(1)}, f32[144,384]{1,0:T(8,128)S(1)}, u32[]{:S(2)}, u32[]{:S(2)}) collective-permute-start(f32[144,384]{1,0:T(8,128)S(1)} %pad_maximum_fusion.4), channel_id=1, source_target_pairs={{0,16},{16,0},{1,17},{17,1},{2,18},{18,2},{3,19},{19,3},{4,20},{20... | collective-permute-start | bytes 663560 | tf_op jit(solution)/shard_map/ppermute | solution.py:834
  283.3 8.4 %collective-permute-start.30 = (f32[288,384]{1,0:T(8,128)S(1)}, f32[288,384]{1,0:T(8,128)S(1)}, u32[]{:S(2)}, u32[]{:S(2)}) collective-permute-start(f32[288,384]{1,0:T(8,128)S(1)} %pad_maximum_fusion.3), channel_id=1, source_target_pairs={{0,16},{16,0},{1,17},{17,1},{2,18},{18,2},{3,19},{19,3},{4,20},{20... | collective-permute-start | bytes 1327112 | tf_op jit(solution)/shard_map/ppermute | solution.py:834
  284.5 8.4 %collective-permute-start.23 = (f32[288,384]{1,0:T(8,128)S(1)}, f32[288,384]{1,0:T(8,128)S(1)}, u32[]{:S(2)}, u32[]{:S(2)}) collective-permute-start(f32[288,384]{1,0:T(8,128)S(1)} %pad_maximum_fusion.2), channel_id=1, source_target_pairs={{0,2},{1,3},{2,0},{3,1},{4,6},{5,7},{6,4},{7,5},{8,10},{9,11},{10,... | collective-permute-start | bytes 1327112 | tf_op jit(solution)/shard_map/ppermute | solution.py:834
  288.3 13.4 %collective-permute-start.32 = (f32[96,768]{1,0:T(8,128)}, f32[96,768]{1,0:T(8,128)}, u32[]{:S(2)}, u32[]{:S(2)}) collective-permute-start(f32[96,768]{1,0:T(8,128)} %get-tuple-element.135), channel_id=1, source_target_pairs={{0,1},{1,0},{2,3},{3,2},{4,5},{5,4},{6,7},{7,6},{8,9},{9,8},{10,11... | collective-permute-start | bytes 884744 | tf_op jit(solution)/shard_map/ppermute | solution.py:834
  288.3 8.3 %collective-permute-start.13 = (bf16[128,1536]{1,0:T(8,128)(2,1)S(1)}, bf16[128,1536]{1,0:T(8,128)(2,1)S(1)}, u32[]{:S(2)}, u32[]{:S(2)}) collective-permute-start(bf16[128,1536]{1,0:T(8,128)(2,1)S(1)} %bitcast.24), channel_id=1, source_target_pairs={{0,1},{1,0},{2,3},{3,2},{4,5},{5,4},{6,7},{7,6},{8,9},{9,8},{10,11... | collective-permute-start | bytes 1179656 | tf_op jit(solution)/shard_map/ppermute | solution.py:834
  288.8 7.8 %collective-permute-start.15 = (bf16[128,1536]{1,0:T(8,128)(2,1)S(1)}, bf16[128,1536]{1,0:T(8,128)(2,1)}, u32[]{:S(2)}, u32[]{:S(2)}) collective-permute-start(bf16[128,1536]{1,0:T(8,128)(2,1)S(1)} %collective-permute-done.14.rest_2_), channel_id=1, source_target_pairs={{0,1},{1,0},{2,3},{3,2},{4,5},{5,4},{6,7},{7,6},{8,9},{9,8},{10,11... | collective-permute-start | bytes 1179656 | tf_op jit(solution)/shard_map/ppermute | solution.py:834
  293.8 42.0 %collective-permute-start.31 = (f32[48,768]{1,0:T(8,128)}, f32[48,768]{1,0:T(8,128)}, u32[]{:S(2)}, u32[]{:S(2)}) collective-permute-start(f32[48,768]{1,0:T(8,128)} %slice.91), channel_id=1, source_target_pairs={{0,1},{1,0},{2,3},{3,2},{4,5},{5,4},{6,7},{7,6},{8,9},{9,8},{10,11... | collective-permute-start | bytes 442376 | tf_op jit(solution)/shard_map/ppermute | solution.py:834
  301.6 35.5 %copy-start.20 = (f32[36096]{0:T(1024)S(1)}, f32[36096]{0:T(1024)}, u32[]{:S(2)}) copy-start(f32[36096]{0:T(1024)} %param.40) | copy-start | bytes 433156
  301.6 35.5 %copy-start.21 = (f32[36096]{0:T(1024)S(1)}, f32[36096]{0:T(1024)}, u32[]{:S(2)}) copy-start(f32[36096]{0:T(1024)} %param.39) | copy-start | bytes 433156
  301.6 35.5 %copy-start.24 = (f32[36096]{0:T(1024)S(1)}, f32[36096]{0:T(1024)}, u32[]{:S(2)}) copy-start(f32[36096]{0:T(1024)} %constant_dynamic-update-slice_fusion) | copy-start | bytes 433156
  335.3 6.4 %collective-permute-start.33 = (f32[96,768]{1,0:T(8,128)}, f32[96,768]{1,0:T(8,128)S(1)}, u32[]{:S(2)}, u32[]{:S(2)}) collective-permute-start(f32[96,768]{1,0:T(8,128)} %get-tuple-element.137), channel_id=1, source_target_pairs={{0,1},{1,0},{2,3},{3,2},{4,5},{5,4},{6,7},{7,6},{8,9},{9,8},{10,11... | collective-permute-start | bytes 884744 | tf_op jit(solution)/shard_map/ppermute | solution.py:834
  (28 other events, 120.4 us)
where the time goes:
time: 346 us; the launch traced here: 345 us
  Pallas kernels  133 us (38%)
  waiting for transfers between devices  76.8 us (22%)
  starting transfers between devices  61.3 us (18%)
  blocking collectives  34.3 us (10%)
  local copies, waits for them, and re-layouts  24.6 us (7%)
  other arithmetic  12.7 us (4%)
    ppermute x32, waiting for transfers between devices, swap(): return lax.ppermute(value, axis, [(i, i ^ bit) for i in range(devices)])  52.4 us
    pallas_call x1, Pallas kernels, on_device(): make_scan(tokens, channels, width, docs, xw, rank, states, ctx_count)  39.7 us
    pallas_call x1, Pallas kernels, on_device(): make_muon(width, own_rows, xw, rank, pack, full)  33.7 us
    ppermute x32, starting transfers between devices, swap(): return lax.ppermute(value, axis, [(i, i ^ bit) for i in range(devices)])  27.6 us
    all_gather x1, blocking collectives, on_device(): w_in = gather_fsdp(lax.all_gather(w_a, 'ctx', axis=0, tiled=True))  17.4 us
    all_gather x1, blocking collectives, on_device(): w_rest = gather_fsdp(lax.all_gather(w_r, 'ctx', axis=0, tiled=True))  16.8 us
    all_to_all x2, waiting for transfers between devices, to_owners(): lax.all_to_all(grads.reshape(owners, own_rows, grads.shape[1]), ('fsdp',...  13.4 us
    pallas_call x1, Pallas kernels, on_device(): make_carry(tokens, channels, docs, xw, rank, states, ctx_count)  12.6 us
  transfers between devices with their start and end apart: 39, of which 22 were waited for; matrix products, arithmetic and copies ran while one was open for 8% of the time, Pallas kernels for 17%

commit v1 on v0

--- a/solution.py
+++ b/solution.py
@@ -77,10 +77,26 @@
     return jnp.concatenate([mask] * (width // LANES), axis=1)
 
 
-def make_front(T, C, D, docs, XW, R):
+def make_front(T, C, D, docs, XW, R, CT, FS, swapped):
     RB = 64
 
-    def front(sc, hb, halo, dy, wa, wr, cw, cb, xu_o, z_o, u_o, v_o, pt_o, dg_o, wt_o, xh_o, xpad):
+    def front(sc, hb, halo, dy, a0, a1, r0, r1, cw, cb, wa, wr, xu_o, z_o, u_o, v_o, pt_o, dg_o, wt_o, xh_o, xpad):
+        own = C // (CT * FS)
+        if swapped:
+            z, f = sc[1 + docs], sc[2 + docs]
+            for pieces, out in (((a0, a1), wa), ((r0, r1), wr)):
+                for e in range(CT * FS):
+                    fe, ze = (e % FS, e // FS) if out is wa else (e // CT, e % CT)
+                    at = pl.multiple_of(((f ^ fe) * CT + (z ^ ze)) * own, own)
+                    k = e * own
+                    half = C // 2
+                    piece = pieces[k // half]
+                    out[pl.ds(at, own), :] = piece[k % half : k % half + own, :]
+        else:
+            wa[0 : C // 2, :] = a0[...]
+            wa[C // 2 : C, :] = a1[...]
+            wr[0 : C // 2, :] = r0[...]
+            wr[C // 2 : C, :] = r1[...]
         w0 = wa[...]
         w1 = wr[:, 0:D]
         wo = wr[:, D + LANES : 2 * D + LANES]
@@ -116,8 +132,9 @@
         lax.fori_loop(0, T // RB, block, 0)
         pt_o[...] = dot_nt(wt[0:XW], u_o[...])
 
-    outs = [((T, C), BF), ((T, C), BF), ((T, C), BF), ((T, C), F32), ((XW, T), F32), ((T, C), F32), ((LANES, C), BF), ((8, C), F32)]
-    return call(front, outs, 8, 1, [pltpu.VMEM((T + 8, C), F32)])
+    outs = [((C, D), BF), ((C, 2 * D + LANES), BF)]
+    outs += [((T, C), BF)] * 3 + [((T, C), F32), ((XW, T), F32), ((T, C), F32), ((LANES, C), BF), ((8, C), F32)]
+    return call(front, outs, 10, 1, [pltpu.VMEM((T + 8, C), F32)])
 
 
 def lane_sums(ref):
@@ -209,7 +226,7 @@
         here = sc[1 + docs]
         for d in range(CT):
             for l in range(LT):
-                ends_o[d, 0:N, l * LANES : (l + 1) * LANES] = jnp.where(d > here, h[l], g[l])
+                ends_o[d, 0:N, l * LANES : (l + 1) * LANES] = jnp.where((here ^ d) > here, h[l], g[l])
             ends_o[d, N : N + 8, :] = jnp.broadcast_to(tot, (8, C))
 
     outs = [((XW, T), F32)] + [((T // 8, 8, C), F32)] * 3 + [((T, C), F32)] + [((CT, N + 8, C), F32)]
@@ -221,9 +238,12 @@
     LT = C // LANES
     nb = T // LANES
 
-    def scan(sc, pt, da, du, dyin, pre, u, z, dg, dy, hb, wr, wt, alog, skip, ends,
-             g_o, dz_o, du1_o, dpre_o, dp_o, mix_o, pw_o, pdt_o, vec_o,
-             a_s, h_s, y_s, lb_s, dd_s, sb_s, sc_s):
+    def scan(sc, pt, da, du, dyin, pre, u, z, dg, dy, hb, wr, wt, alog, skip, *rest):
+        ends = rest[: CT - 1]
+        (
+            g_o, dz_o, du1_o, dpre_o, dp_o, mix_o, pw_o, pdt_o, vec_o,
+            a_s, h_s, y_s, lb_s, dd_s, sb_s, sc_s,
+        ) = rest[CT - 1 :]
         c0 = pl.multiple_of(sc[0], LANES)
         am = [-jnp.exp(alog[:, pl.ds(c0 + l * LANES, LANES)]) for l in range(LT)]
         am2 = [a * LOG2E for a in am]
@@ -238,11 +258,15 @@
         hin, gin = [], []
         for l in range(LT):
             for way, got in ((-1, hin), (1, gin)):
-                one = jnp.clip(here + way, 0, CT - 1)
-                two = jnp.clip(here + 2 * way, 0, CT - 1)
-                prod = jnp.exp2(jnp.broadcast_to(ends[one, N : N + 1, sl[l]], (N, LANES)) * am2[l])
-                far = jnp.where(here + 2 * way == two, ends[two, 0:N, sl[l]], 0.0)
-                got.append(jnp.where(here + way == one, ends[one, 0:N, sl[l]] + prod * far, 0.0))
+                near = jnp.zeros((N, LANES), F32)
+                tot = jnp.zeros((1, LANES), F32)
+                far = near
+                for d in range(1, CT):
+                    e = ends[d - 1]
+                    near = jnp.where((here ^ d) == here + way, e[0:N, sl[l]], near)
+                    tot = jnp.where((here ^ d) == here + way, e[N : N + 1, sl[l]], tot)
+                    far = jnp.where((here ^ d) == here + 2 * way, e[0:N, sl[l]], far)
+                got.append(near + jnp.exp2(jnp.broadcast_to(tot, (N, LANES)) * am2[l]) * far)
             h_s[0, :, sl[l]] = hin[l]
 
         def fouter(k, h):
@@ -358,7 +382,7 @@
             ((C, 2 * D), BF), ((R, C), F32), ((8 + N, C), F32)]
     scratch = [pltpu.VMEM((T, N, C), F32), pltpu.VMEM((T + 1, N, C), F32)] + [pltpu.VMEM((T // 8, 8, C), F32)] * 3
     scratch += [pltpu.VMEM((LANES, N, LANES), F32)] * 2
-    return call(scan, outs, 16, 1, scratch)
+    return call(scan, outs, 14 + CT, 1, scratch)
 
 
 def make_back(T, C, D, docs, XW, R):
@@ -453,18 +477,22 @@
     return call(last, outs, 8, 0)
 
 
-def flat_slots(k, shift, share, first):
-    return (k >> shift) * share + first + (k & ((1 << shift) - 1))
-
-
-def make_send(T, D, CT, TP):
-    Q = T // TP
+def flat_slots(k, shift, share, first, here):
+    return ((k >> shift) ^ here) * share + first + (k & ((1 << shift) - 1))
+
+
+def chunk_shape(T, CT, TP):
     share = T // CT
     SR = share // TP
     shift = SR.bit_length() - 1
-    assert SR == 1 << shift and Q == CT * SR
-
-    def send(rsc, perm, x, dy, buf_o, fin_o):
+    assert SR == 1 << shift and T // TP == CT * SR
+    return T // TP, share, SR, shift
+
+
+def make_send(T, D, CT, TP):
+    Q, share, SR, shift = chunk_shape(T, CT, TP)
+
+    def send(rsc, perm, x, dy, buf_o, pos_o):
         c = rsc[0]
         tp = rsc[1]
         own = perm[0:1, pl.ds(pl.multiple_of(c * T, LANES), T)].astype(F32)
@@ -472,52 +500,57 @@
         q = lax.broadcasted_iota(jnp.int32, (T, T), 1)
         row = jnp.broadcast_to(own, (T, T))
         col = jnp.broadcast_to(jnp.sum(jnp.where(r == q, row, 0.0), axis=1, keepdims=True), (T, T))
-        pos_col = jnp.sum(jnp.where(row < col, 1.0, 0.0), axis=1, keepdims=True)
         pos_row = jnp.sum(jnp.where(col < row, 1.0, 0.0), axis=0, keepdims=True)
         k = lax.broadcasted_iota(jnp.int32, (Q, T), 0)
-        pick = jnp.where(flat_slots(k, shift, share, SR * tp).astype(F32) == pos_row, 1.0, 0.0).astype(BF)
+        slot = flat_slots(k, shift, share, SR * tp, c).astype(F32)
+        pick = jnp.where(slot == pos_row, 1.0, 0.0).astype(BF)
         buf_o[:, 0:D] = dot_nn(pick, x[...]).astype(BF)
         buf_o[:, D : 2 * D] = dot_nn(pick, dy[...]).astype(BF)
-        f = lax.broadcasted_iota(jnp.int32, (T, Q), 1)
-        for e in range(TP):
-            slot = flat_slots(f, shift, share, SR * (tp ^ e)).astype(F32)
-            fin_o[:, e * Q : (e + 1) * Q] = jnp.where(slot == pos_col, 1.0, 0.0).astype(BF)
-
-    return call(send, [((Q, 2 * D), BF), ((T, T), BF)], 4, 1)
-
-
-def make_recv(T, D, CT, TP):
-    Q = T // TP
-    share = T // CT
-    SR = share // TP
-    shift = SR.bit_length() - 1
-
-    def recv(rsc, perm, gain, *rest):
-        parts = rest[:TP]
-        x_o, dy_o, hb_o, rt_o = rest[TP:]
+        pos_o[...] = pos_row
+
+    return call(send, [((Q, 2 * D), BF), ((1, T), F32)], 4, 1)
+
+
+def make_plan(T, CT, TP):
+    Q, share, SR, shift = chunk_shape(T, CT, TP)
+
+    def plan(rsc, perm, pos, rt_o, fin_o):
         c = rsc[0]
         tp = rsc[1]
-        place = (lax.broadcasted_iota(jnp.int32, (T, T), 0) + c * T)
+        r = lax.broadcasted_iota(jnp.int32, (T, T), 0)
+        q = lax.broadcasted_iota(jnp.int32, (T, T), 1)
+        place = r + c * T
         lane = lax.broadcasted_iota(jnp.int32, (T, LANES), 1)
         hot = jnp.zeros((T, LANES), F32)
         for s in range(CT):
             src = jnp.broadcast_to(perm[0:1, s * T : (s + 1) * T], (T, T))
             n = jnp.sum(jnp.where(src == place, 1.0, 0.0), axis=1, keepdims=True)
             hot = jnp.where(lane == s, n, hot)
-        r = lax.broadcasted_iota(jnp.int32, (T, T), 0)
-        q = lax.broadcasted_iota(jnp.int32, (T, T), 1)
         below = jnp.where(q < r, 1.0, 0.0).astype(BF)
         count = dot_nn(below, hot.astype(BF))
         rank = jnp.sum(hot * count, axis=1, keepdims=True)
         block = jnp.sum(hot * lane.astype(F32), axis=1, keepdims=True)
         want = block * share + rank
+        back = jnp.sum(jnp.where(r == q, jnp.broadcast_to(pos[...], (T, T)), 0.0), axis=1, keepdims=True)
         f = lax.broadcasted_iota(jnp.int32, (T, Q), 1)
+        for e in range(TP):
+            slot = flat_slots(f, shift, share, SR * (tp ^ e), c).astype(F32)
+            rt_o[:, e * Q : (e + 1) * Q] = jnp.where(slot == want, 1.0, 0.0).astype(BF)
+            fin_o[:, e * Q : (e + 1) * Q] = jnp.where(slot == back, 1.0, 0.0).astype(BF)
+
+    return call(plan, [((T, T), BF)] * 2, 3, 1)
+
+
+def make_recv(T, D, TP):
+    Q = T // TP
+
+    def recv(rt, gain, *rest):
+        parts = rest[:TP]
+        x_o, dy_o, hb_o = rest[TP:]
         xa = jnp.zeros((T, D), F32)
         ya = jnp.zeros((T, D), F32)
         for e in range(TP):
-            slot = flat_slots(f, shift, share, SR * (tp ^ e)).astype(F32)
-            m = jnp.where(slot == want, 1.0, 0.0).astype(BF)
-            rt_o[:, e * Q : (e + 1) * Q] = m
+            m = rt[:, e * Q : (e + 1) * Q]
             xa = xa + dot_nn(m, parts[e][:, 0:D])
             ya = ya + dot_nn(m, parts[e][:, D : 2 * D])
         x_o[...] = xa.astype(BF)
@@ -525,7 +558,7 @@
         inv = lax.rsqrt(jnp.mean(xa * xa, axis=1, keepdims=True) + NORM_EPS)
         hb_o[...] = (xa * inv * gain[...]).astype(BF)
 
-    return call(recv, [((T, D), BF)] * 3 + [((T, T), BF)], 3 + TP, 1)
+    return call(recv, [((T, D), BF)] * 3, 2 + TP, 0)
 
 
 def make_norm_back(Q, D):
@@ -596,17 +629,10 @@
     return (momentum_new, gradient + MOMENTUM * momentum_new)
 
 
-def add_parts(ref, cols):
-    tot = ref[0, :, cols].astype(F32)
-    for k in range(1, ref.shape[0]):
-        tot = tot + ref[k, :, cols].astype(F32)
-    return tot
-
-
-def make_gram_out(G, rows, D):
+def make_gram_out(rows, D):
     def gram_out(got, mom, g1_o, go_o, mo_o, uo_o, gram_o):
-        g1_o[...] = add_parts(got, slice(0, D))
-        g = add_parts(got, slice(D, 2 * D))
+        g1_o[...] = got[:, 0:D]
+        g = got[:, D : 2 * D]
         m, u = momentum_step(g, mom[...])
         go_o[...] = g
         mo_o[...] = m
@@ -617,7 +643,7 @@
     return call(gram_out, outs, 2, 0)
 
 
-def make_gram_in(G, rows, D, XW, R, VR, pack, full):
+def make_gram_in(rows, D, XW, R, VR, pack, full):
     b = D // 3
     top = 2 * b
 
@@ -626,14 +652,14 @@
         parts = []
         us = []
         for q in range(2):
-            g = add_parts(got, slice(0, D)) if q == 0 else g1[...]
+            g = got[:, 0:D] if q == 0 else g1[...]
             m, u = momentum_step(g, mom[:, q, :])
             gi_o[:, q, :] = g
             mi_o[:, q, :] = m
             us.append(u)
             parts.append(halves(u))
         put_gram(tmp, parts, D)
-        g = add_parts(got, slice(D, D + LANES))
+        g = got[:, D : D + LANES]
         m, u = momentum_step(g, jnp.concatenate([xm[...], dm[...]], axis=1))
         gx_o[...] = g[:, 0:XW]
         gd_o[...] = g[:, XW : XW + R]
@@ -877,10 +903,34 @@
     return jnp.concatenate(done, axis=1)
 
 
-def gather_fsdp(value):
-    if lax.axis_size("fsdp") == 2:
-        return in_order(value, swap(value, "fsdp", 1), "fsdp", 1)
-    return lax.all_gather(value, "fsdp", axis=0, tiled=True)
+def to_owners(grads, rows):
+    steps = [("fsdp", b) for b in bits_of("fsdp")[::-1]] + [("ctx", b) for b in bits_of("ctx")]
+    value = grads
+    for axis, bit in steps:
+        if axis == "fsdp":
+            value = value.reshape(1, 2, value.shape[0] // 2, value.shape[1])
+        else:
+            value = value.reshape(value.shape[0] // (2 * rows), 2, rows, value.shape[1])
+        mine = side(axis, bit)
+        away = lax.dynamic_slice_in_dim(value, 1 - mine, 1, 1).astype(BF)
+        kept = lax.dynamic_slice_in_dim(value, mine, 1, 1)
+        value = kept.astype(F32) + swap(away, axis, bit).astype(F32)
+        value = value.reshape(-1, value.shape[3])
+    return value
+
+
+def over_ctx(value):
+    count = lax.axis_size("ctx")
+    rows = value.shape[0] // count
+    parts = [value[d * rows : (d + 1) * rows] for d in range(count)]
+    return jnp.concatenate([parts[0]] + [swap(parts[d], "ctx", d) for d in range(1, count)], axis=0)
+
+
+def doubled(value, axes):
+    steps = [(a, b) for a in axes for b in bits_of(a)]
+    for axis, bit in steps[:-1]:
+        value = jnp.concatenate([value, swap(value, axis, bit)], axis=0)
+    return value, swap(value, *steps[-1])
 
 
 def adam_update(parameters, gradient, moment_one, moment_two, adam_step):
@@ -936,54 +986,54 @@
     lengths = doc_lengths[0]
     docs = lengths.shape[0]
     offsets = jnp.cumsum(lengths) - lengths
-    scal = jnp.concatenate([(tp_index * channels)[None], offsets - ctx_index * tokens, ctx_index[None]]).astype(
-        jnp.int32
-    )
+    scal = jnp.concatenate(
+        [(tp_index * channels)[None], offsets - ctx_index * tokens, ctx_index[None], lax.axis_index("fsdp")[None]]
+    ).astype(jnp.int32)
     place = jnp.stack([ctx_index, tp_index]).astype(jnp.int32)
     perm_row = (route_perm % stream).reshape(1, stream)
     gain_row = norm_gain.reshape(1, width)
 
     w_a, w_r = make_pack(own_rows, width, xw, rank)(in_proj, x_proj, dt_proj, out_proj)
-    send, fin = make_send(tokens, width, ctx_count, tp_count)(place, perm_row, block_input, cotangent)
-    sent = lax.all_to_all(
-        send.reshape(ctx_count, quarter // ctx_count, 2 * width), "ctx", split_axis=0, concat_axis=0, tiled=True
+    send, send_pos = make_send(tokens, width, ctx_count, tp_count)(place, perm_row, block_input, cotangent)
+    own = over_ctx(send)
+    swapped = own_rows % 16 == 0
+    if swapped:
+        parts_in = doubled(w_a, ("fsdp", "ctx"))
+        parts_rest = doubled(w_r, ("ctx", "fsdp"))
+    else:
+        half = channels // 2
+        full_in, full_rest = [lax.all_gather(w, ("fsdp", "ctx"), axis=0, tiled=True) for w in (w_a, w_r)]
+        parts_in = (full_in[:half], full_in[half:])
+        parts_rest = (full_rest[:half], full_rest[half:])
+    route, fin = make_plan(tokens, ctx_count, tp_count)(place, perm_row, send_pos)
+    far = swap(own, "tp", 2)
+    stream_x, stream_dy, normed = make_recv(tokens, width, tp_count)(
+        route, gain_row, own, swap(own, "tp", 1), far, swap(far, "tp", 1)
     )
-    w_rest = gather_fsdp(lax.all_gather(w_r, "ctx", axis=0, tiled=True))
-    w_in = gather_fsdp(lax.all_gather(w_a, "ctx", axis=0, tiled=True))
-    own = sent.reshape(quarter, 2 * width)
-    far = swap(own, "tp", 2)
-    stream_x, stream_dy, normed, route = make_recv(tokens, width, ctx_count, tp_count)(
-        place, perm_row, gain_row, own, swap(own, "tp", 1), far, swap(far, "tp", 1)
-    )
 
     halo = shifted(normed[tokens - 8 :], "ctx", 1)
-    conv_in, gate_in, conv_act, conv_out, pt_part, d_gated, w_turn, x_halo = make_front(
-        tokens, channels, width, docs, xw, rank
-    )(scal, normed, halo, stream_dy, w_in, w_rest, conv_weight, conv_bias.reshape(1, inner))
+    w_in, w_rest, conv_in, gate_in, conv_act, conv_out, pt_part, d_gated, w_turn, x_halo = make_front(
+        tokens, channels, width, docs, xw, rank, ctx_count, fsdp_count, swapped
+    )(scal, normed, halo, stream_dy, *parts_in, *parts_rest, conv_weight, conv_bias.reshape(1, inner))
     pt_pair = pt_part + swap(pt_part, "tp", 1)
     pt, dec, drv, d_inner, pre, ends = make_carry(
         tokens, channels, docs, xw, rank, states, ctx_count
     )(scal, pt_pair, swap(pt_pair, "tp", 2), conv_act, gate_in, d_gated, w_turn, dt_bias.reshape(1, inner), a_log)
-    ends = lax.all_to_all(ends, "ctx", split_axis=0, concat_axis=0, tiled=True)
+    ends = [swap(ends[d], "ctx", d) for d in range(1, ctx_count)]
     gate_low, d_gate, du_one, d_pre_low, dp_part, mix_part, grads_one, part_dt, vec_part = make_scan(
         tokens, channels, width, docs, xw, rank, states, ctx_count
     )(
         scal, pt, dec, drv, d_inner, pre, conv_act, gate_in, d_gated, stream_dy, normed, w_rest, w_turn, a_log,
-        skip_gain.reshape(1, inner), ends,
+        skip_gain.reshape(1, inner), *ends,
     )
 
-    def to_owners(grads):
-        return lax.all_to_all(
-            grads.reshape(owners, own_rows, grads.shape[1]), ("fsdp", "ctx"), split_axis=0, concat_axis=0, tiled=True
-        )
-
-    got_one = to_owners(grads_one)
+    got_one = to_owners(grads_one, own_rows)
     dp_pair = dp_part + swap(dp_part, "tp", 1)
     d_conv_in, spill, grads_two, vec_chan = make_back(tokens, channels, width, docs, xw, rank)(8 + states)(
         scal, dp_pair, swap(dp_pair, "tp", 2), du_one, conv_out, conv_act, conv_in, x_halo, w_turn, conv_weight,
         vec_part, part_dt, normed, halo,
     )
-    got_two = to_owners(grads_two)
+    got_two = to_owners(grads_two, own_rows)
     keep, away, g_gain = make_last(tokens, channels, width, quarter)(
         d_conv_in, shifted(spill, "ctx", -1), d_gate, w_in, w_rest, mix_part, stream_x, route
     )
@@ -991,9 +1041,7 @@
     near = swap(away, "tp", 1)
     cross = (keep[quarter:].astype(F32) + near[quarter:].astype(F32)).astype(BF)
     back = make_norm_back(quarter, width)(keep, near, swap(cross, "tp", 2), own, gain_row)[0]
-    home = lax.all_to_all(
-        back.reshape(ctx_count, quarter // ctx_count, 2 * width), "ctx", split_axis=0, concat_axis=0, tiled=True
-    ).reshape(quarter, 2 * width)
+    home = over_ctx(back)
     home_far = swap(home, "tp", 2)
     block_out, input_grad = make_final(tokens, width, tp_count)(
         fin, home, swap(home, "tp", 1), home_far, swap(home_far, "tp", 1)
@@ -1004,11 +1052,11 @@
     vec_wide = lax.dynamic_update_slice(jnp.zeros((kinds, inner), F32), vec_chan, (0, tp_index * channels))
     vec_wide = vec_wide + jnp.pad(g_gain, ((7, kinds - 8), (0, inner - width)))
     vec_rows = kinds * inner // width
-    g_one, g_out, mom_out, upd_out, gram_out = make_gram_out(owners, own_rows, width)(got_one, out_momentum)
+    g_one, g_out, mom_out, upd_out, gram_out = make_gram_out(own_rows, width)(got_one, out_momentum)
     top = 2 * (width // 3)
     full = -(-(top + max(vec_rows, pack)) // 64) * 64
     g_in, mom_in, g_x, mom_x, g_dt, mom_dt, gram_mine, gram_away, upd_mine, upd_away = make_gram_in(
-        owners, own_rows, width, xw, rank, vec_rows, pack, full
+        own_rows, width, xw, rank, vec_rows, pack, full
     )(place, got_two, g_one, in_momentum, x_momentum, dt_momentum, vec_wide.reshape(vec_rows, width), gram_out, upd_out)
     gram = sum_rest(gram_mine + swap(gram_away, "tp", 1))
     x_mine, x_away = make_muon(width, own_rows, xw, rank, pack, full)(place, gram, upd_mine, swap(upd_away, "tp", 1))

time: 346 us -> 333 us (0.962)
  blocking collectives: 34.3 us -> 0 us
  waiting for transfers between devices: 76.8 us -> 97.2 us
  starting transfers between devices: 61.3 us -> 51.8 us
  local copies, waits for them, and re-layouts: 24.6 us -> 30.3 us
    ppermute x32 -> x51, waiting for transfers between devices: 52.4 us -> 95 us  [swap(): return lax.ppermute(value, axis, [(i, i ^ bit) for i in range(devices)])]
    all_gather x2 -> x0, blocking collectives: 34.3 us -> none  [the longest x1 17.4 us: on_device(): w_in = gather_fsdp(lax.all_gather(w_a, 'ctx', axis=0, tiled=True))]
    all_to_all x5 -> x0, starting transfers between devices: 30.9 us -> none  [the longest x1 11.7 us: on_device(): lax.all_to_all(back.reshape(ctx_count, quarter // ctx_count, 2 * width),...]
    ppermute x32 -> x51, starting transfers between devices: 27.6 us -> 46.4 us  [swap(): return lax.ppermute(value, axis, [(i, i ^ bit) for i in range(devices)])]
    all_to_all x5 -> x0, waiting for transfers between devices: 18.8 us -> none  [the longest x2 13.4 us: to_owners(): lax.all_to_all(grads.reshape(owners, own_rows, grads.shape[1]), ('fsdp',...]
    unnamed x84 -> x108, local copies, waits for them, and re-layouts: 12.4 us -> 14.6 us
    pallas_call x4 -> x5, Pallas kernels: 21.4 us -> 23.2 us  [the longest x1 7.1 us: on_device(): make_front(tokens, channels, width, docs, xw, rank, ctx_count, fsdp_count...]
  transfers between devices with their start and end apart: 39 -> 53, of which waited for: 22 -> 30; matrix products, arithmetic and copies ran while one was open for 8% -> 9% of each run, Pallas kernels for 17% -> 17%
where the time goes in v1:
time: 333 us; the launch traced here: 331 us
  Pallas kernels  135 us (41%)
  waiting for transfers between devices  97.2 us (29%)
  starting transfers between devices  51.8 us (16%)
  local copies, waits for them, and re-layouts  30.3 us (9%)
  other arithmetic  14.9 us (4%)
    ppermute x51, waiting for transfers between devices, swap(): return lax.ppermute(value, axis, [(i, i ^ bit) for i in range(devices)])  95 us
    ppermute x51, starting transfers between devices, swap(): return lax.ppermute(value, axis, [(i, i ^ bit) for i in range(devices)])  46.4 us
    pallas_call x1, Pallas kernels, on_device(): make_scan(tokens, channels, width, docs, xw, rank, states, ctx_count)  39.8 us
    pallas_call x1, Pallas kernels, on_device(): make_muon(width, own_rows, xw, rank, pack, full)  33.7 us
    unnamed x108, local copies, waits for them, and re-layouts  14.6 us
    pallas_call x1, Pallas kernels, on_device(): make_carry(tokens, channels, docs, xw, rank, states, ctx_count)  12.6 us
    pallas_call x1, Pallas kernels, on_device(): make_front(tokens, channels, width, docs, xw, rank, ctx_count, fsdp_count...  7.1 us
  transfers between devices with their start and end apart: 53, of which 30 were waited for; matrix products, arithmetic and copies ran while one was open for 9% of the time, Pallas kernels for 17%

profile of v1, /device:TPU:0, one launch (start us, length us, event | category | flops | bytes accessed | tf_op | source)
XLA Modules:
  0.0 331.3 jit_solution(4837123012154081613)
XLA Ops:
  2.6 2.7 send.1
  6.3 5.1 %collective-permute-start.2 = (bf16[32,1536]{1,0:T(8,128)(2,1)S(1)}, bf16[32,1536]{1,0:T(8,128)(2,1)S(1)}, u32[]{:S(2)}, u32[]{:S(2)}) collective-permute-start(bf16[32,1536]{1,0:T(8,128)(2,1)S(1)} %get-tuple-element.170), channel_id=1, source_target_pairs={{0,12},{4,8},{8,4},{12,0},{1,13},{5,9},{9,5},{13,1},{2,14},{6,10},... | collective-permute-start | bytes 294920 | tf_op jit(solution)/shard_map/ppermute | solution.py:860
  12.1 2.2 pack.1
  14.3 1.7 collective-permute-start.7
  21.2 2.0 collective-permute-done.10
  24.2 1.8 collective-permute-start.11
  27.6 12.8 %collective-permute-done.11 = bf16[96,1664]{1,0:T(8,128)(2,1)S(1)} collective-permute-done((bf16[96,1664]{1,0:T(8,128)(2,1)S(1)}, bf16[96,1664]{1,0:T(8,128)(2,1)S(1)}, u32[]{:S(2)}, u32[]{:S(2)}) %collective-permute-start.11) | collective-permute-done | bytes 319520 | tf_op jit(solution)/shard_map/ppermute | solution.py:860
  40.9 2.7 plan.1
  47.4 4.6 %recv.1 = (bf16[512,768]{1,0:T(8,128)(2,1)}, bf16[512,768]{1,0:T(8,128)(2,1)}, bf16[512,768]{1,0:T(8,128)(2,1)}) custom-call(bf16[512,512]{1,0:T(8,128)(2,1)} %get-tuple-element.92.rt, f32[1,768]{1,0:T(1,128)} %reshape.164.gain, bf16[128,1536]{1,0:T(8,128)(2,1)} %copy-done.1, bf16[128,1536]{1,0:T(8,128)(2,1)} %copy-done.19, bf16[128,1536]{1,0:T(8,128)(2,1)} %copy-done.17, ...), custom_call_target="tpu_custom_call" | custom-call | tf_op jit(solution)/shard_map/recv/pallas_call | solution.py:1010
  52.7 3.9 %collective-permute-start.6 = (bf16[8,768]{1,0:T(8,128)(2,1)S(1)}, bf16[8,768]{1,0:T(8,128)(2,1)S(1)}, u32[]{:S(2)}, u32[]{:S(2)}) collective-permute-start(bf16[8,768]{1,0:T(8,128)(2,1)S(1)} %slice.105), channel_id=1, source_target_pairs={{0,4},{4,8},{8,12},{1,5},{5,9},{9,13},{2,6},{6,10},{10,14},{3,7},{... | collective-permute-start | bytes 36872 | tf_op jit(solution)/shard_map/ppermute | solution.py:855
  57.8 3.3 %collective-permute-done.9.a1 = bf16[192,768]{1,0:T(8,128)(2,1)S(1)} collective-permute-done((bf16[192,768]{1,0:T(8,128)(2,1)S(1)}, bf16[192,768]{1,0:T(8,128)(2,1)S(1)}, u32[]{:S(2)}, u32[]{:S(2)}) %collective-permute-start.9) | collective-permute-done | bytes 294944 | tf_op jit(solution)/shard_map/ppermute | solution.py:860
  62.1 7.1 %front.1 = (bf16[384,768]{1,0:T(8,128)(2,1)}, bf16[384,1664]{1,0:T(8,128)(2,1)}, bf16[512,384]{1,0:T(8,128)(2,1)}, bf16[512,384]{1,0:T(8,128)(2,1)}, bf16[512,38...) custom-call(s32[7]{0:T(128)} %pad_add_fusion.1.sc, ...), custom_call_target="tpu_custom_call" | custom-call | tf_op jit(solution)/shard_map/front/pallas_call | solution.py:1015
  73.9 4.2 %collective-permute-done.14.pb = f32[80,512]{1,0:T(8,128)S(1)} collective-permute-done((f32[80,512]{1,0:T(8,128)S(1)}, f32[80,512]{1,0:T(8,128)S(1)}, u32[]{:S(2)}, u32[]{:S(2)}) %collective-permute-start.14) | collective-permute-done | bytes 163872 | tf_op jit(solution)/shard_map/ppermute | solution.py:860
  78.8 12.6 %carry.1 = (f32[80,512]{1,0:T(8,128)}, f32[64,8,384]{2,1,0:T(8,128)}, f32[64,8,384]{2,1,0:T(8,128)}, f32[64,8,384]{2,1,0:T(8,128)}, f32[512,384]{1,0:T(8,128)}, /*index=5*/f32[4,24,384]{2,1,0:T(8,128)}) custom-call(s32[7]{0:T(128)} %pad_add_fusion.1.sc, f32[80,512]{1,0:T(8,128)} %copy-done.12, f32[80,512]{1,0:T(8,128)} %copy-done.27, ...), custom_call_target="tpu_custom_call" | custom-call | tf_op jit(solution)/shard_map/carry/pallas_call | solution.py:1019
  92.3 1.9 collective-permute-start.16
  94.2 2.5 collective-permute-start.17
  97.3 2.7 collective-permute-done.17.rest_2_
  100.6 39.8 %scan.1 = (bf16[512,384]{1,0:T(8,128)(2,1)}, bf16[512,384]{1,0:T(8,128)(2,1)}, f32[512,384]{1,0:T(8,128)}, bf16[512,384]{1,0:T(8,128)(2,1)}, f32[80,512]{1,0:T(8...) custom-call(s32[7]{0:T(128)} %pad_add_fusion.1.sc, ...), custom_call_target="tpu_custom_call" | custom-call | tf_op jit(solution)/shard_map/scan/pallas_call | solution.py:1023
  141.6 1.7 collective-permute-start.32
  145.8 4.8 %collective-permute-done.19.db_ = f32[80,512]{1,0:T(8,128)S(1)} collective-permute-done((f32[80,512]{1,0:T(8,128)S(1)}, f32[80,512]{1,0:T(8,128)S(1)}, u32[]{:S(2)}, u32[]{:S(2)}) %collective-permute-start.19) | collective-permute-done | bytes 163872 | tf_op jit(solution)/shard_map/ppermute | solution.py:860
  151.3 5.8 %back.1 = (f32[512,384]{1,0:T(8,128)}, f32[8,384]{1,0:T(8,128)}, bf16[384,896]{1,0:T(8,128)(2,1)}, f32[24,384]{1,0:T(8,128)}) custom-call(s32[7]{0:T(128)} %pad_add_fusion.1.sc, f32[80,512]{1,0:T(8,128)} %copy-done.11, f32[80,512]{1,0:T(8,128)} %copy-done.26, f32[512,384]{1,0:T(8,128)} %get-tuple-element.111.du1, f32[512,384]{1,0:T(8,128)} %get-tuple-element.112.v, ...), custom_call_target="tpu_custom_call" | custom-call | tf_op jit(solution)/shard_map/back/pallas_call | solution.py:1032
  158.6 1.7 constant_dynamic-slice_fusion.7
  160.7 2.2 collective-permute-done.20.spill
  163.5 5.7 %last.1 = (bf16[256,1536]{1,0:T(8,128)(2,1)}, bf16[256,1536]{1,0:T(8,128)(2,1)}, f32[1,768]{1,0:T(1,128)}) custom-call(f32[512,384]{1,0:T(8,128)} %get-tuple-element.117.dxu, f32[8,384]{1,0:T(8,128)} %copy-done.44, bf16[512,384]{1,0:T(8,128)(2,1)} %get-tuple-element.119.dz, bf16[384,768]{1,0:T(8,128)(2,1)} %get-tuple-element.120.wa, ...), custom_call_target="tpu_custom_call" | custom-call | tf_op jit(solution)/shard_map/last/pallas_call | solution.py:1037
  173.9 6.0 %collective-permute-done.30 = bf16[2,1,48,896]{3,2,1,0:T(8,128)(2,1)S(1)} collective-permute-done((bf16[2,1,48,896]{3,2,1,0:T(8,128)(2,1)S(1)}, bf16[2,1,48,896]{3,2,1,0:T(8,128)(2,1)S(1)}, u32[]{:S(2)}, u32[]{:S(2)}) %collective-permute-start.30) | collective-permute-done | bytes 172064 | tf_op jit(solution)/shard_map/ppermute | solution.py:860
  180.1 3.4 %collective-permute-done.33 = bf16[2,1,48,1536]{3,2,1,0:T(8,128)(2,1)S(1)} collective-permute-done((bf16[2,1,48,1536]{3,2,1,0:T(8,128)(2,1)S(1)}, bf16[2,1,48,1536]{3,2,1,0:T(8,128)(2,1)S(1)}, u32[]{:S(2)}, u32[]{:S(2)}) %collective-permute-start.33) | collective-permute-done | bytes 294944 | tf_op jit(solution)/shard_map/ppermute | solution.py:860
  183.7 4.3 %collective-permute-done.31 = bf16[1,1,48,896]{3,2,1,0:T(8,128)(2,1)S(1)} collective-permute-done((bf16[1,1,48,896]{3,2,1,0:T(8,128)(2,1)S(1)}, bf16[1,1,48,896]{3,2,1,0:T(8,128)(2,1)S(1)}, u32[]{:S(2)}, u32[]{:S(2)}) %collective-permute-start.31) | collective-permute-done | bytes 86048 | tf_op jit(solution)/shard_map/ppermute | solution.py:860
  188.7 3.1 collective-permute-done.34
  192.6 3.0 gram_out.1
  195.5 5.8 %gram_in.1 = (f32[48,2,768]{2,1,0:T(2,128)}, f32[48,2,768]{2,1,0:T(2,128)}, f32[48,80]{1,0:T(8,128)}, f32[48,80]{1,0:T(8,128)}, f32[48,48]{1,0:T(8,128)}, /*inde...) custom-call(s32[2]{0:T(128)} %pad_add_fusion.rsc.place, ...), custom_call_target="tpu_custom_call" | custom-call | tf_op jit(solution)/shard_map/gram_in/pallas_call | solution.py:1058
  201.8 4.5 %collective-permute-done.21.got = bf16[256,1536]{1,0:T(8,128)(2,1)S(1)} collective-permute-done((bf16[256,1536]{1,0:T(8,128)(2,1)S(1)}, bf16[256,1536]{1,0:T(8,128)(2,1)S(1)}, u32[]{:S(2)}, u32[]{:S(2)}) %collective-permute-start.21) | collective-permute-done | bytes 786464 | tf_op jit(solution)/shard_map/ppermute | solution.py:860
  211.5 7.2 %collective-permute-done.22.far = bf16[128,1536]{1,0:T(8,128)(2,1)S(1)} collective-permute-done((bf16[128,1536]{1,0:T(8,128)(2,1)}, bf16[128,1536]{1,0:T(8,128)(2,1)S(1)}, u32[]{:S(2)}, u32[]{:S(2)}) %collective-permute-start.22) | collective-permute-done | bytes 393248 | tf_op jit(solution)/shard_map/ppermute | solution.py:860
  219.4 2.7 norm_back.1
  222.1 1.7 add.157
  226.2 1.7 collective-permute-start.25
  227.9 2.7 collective-permute-start.23
  230.7 4.7 %collective-permute-done.43 = f32[288,384]{1,0:T(8,128)S(1)} collective-permute-done((f32[288,384]{1,0:T(8,128)S(1)}, f32[288,384]{1,0:T(8,128)S(1)}, u32[]{:S(2)}, u32[]{:S(2)}) %collective-permute-start.43) | collective-permute-done | bytes 442400 | tf_op jit(solution)/shard_map/ppermute | solution.py:860
  237.7 3.7 %collective-permute-done.44 = f32[144,384]{1,0:T(8,128)S(1)} collective-permute-done((f32[144,384]{1,0:T(8,128)S(1)}, f32[144,384]{1,0:T(8,128)S(1)}, u32[]{:S(2)}, u32[]{:S(2)}) %collective-permute-start.44) | collective-permute-done | bytes 221216 | tf_op jit(solution)/shard_map/ppermute | solution.py:860
  243.7 2.6 collective-permute-done.45
  246.5 2.5 collective-permute-done.38
  249.8 4.7 %collective-permute-done.46 = f32[72,384]{1,0:T(8,128)S(1)} collective-permute-done((f32[72,384]{1,0:T(8,128)S(1)}, f32[72,384]{1,0:T(8,128)S(1)}, u32[]{:S(2)}, u32[]{:S(2)}) %collective-permute-start.46) | collective-permute-done | bytes 110624 | tf_op jit(solution)/shard_map/ppermute | solution.py:860
  257.3 2.0 collective-permute-done.47
  261.9 5.1 %collective-permute-done.48 = f32[144,384]{1,0:T(8,128)S(1)} collective-permute-done((f32[144,384]{1,0:T(8,128)S(1)}, f32[144,384]{1,0:T(8,128)S(1)}, u32[]{:S(2)}, u32[]{:S(2)}) %collective-permute-start.48) | collective-permute-done | bytes 221216 | tf_op jit(solution)/shard_map/ppermute | solution.py:860
  275.5 2.0 collective-permute-done.42
  282.9 4.3 %final.1 = (bf16[512,768]{1,0:T(8,128)(2,1)}, bf16[512,768]{1,0:T(8,128)(2,1)}) custom-call(bf16[512,512]{1,0:T(8,128)(2,1)} %get-tuple-element.91.fin, bf16[128,1536]{1,0:T(8,128)(2,1)} %copy-done.5, bf16[128,1536]{1,0:T(8,128)(2,1)} %copy-done.16, bf16[128,1536]{1,0:T(8,128)(2,1)} %copy-done.15, bf16[128,1536]{1,0:T(8,128)(2,1)} %copy-done.18), custom_call_target="tpu_custom_call" | custom-call | tf_op jit(solution)/shard_map/final/pallas_call | solution.py:1046
  287.2 33.7 %muon.1 = (f32[96,768]{1,0:T(8,128)}, f32[96,768]{1,0:T(8,128)}) custom-call(s32[2]{0:T(128)} %pad_add_fusion.rsc.place, f32[576,768]{1,0:T(8,128)} %copy-done, f32[96,768]{1,0:T(8,128)} %get-tuple-element.140.um, f32[96,768]{1,0:T(8,128)} %collective-permute-done.51.ua), custom_call_target="tpu_custom_call" | custom-call | tf_op jit(solution)/shard_map/muon/pallas_call | solution.py:1062
  322.7 1.7 multiply_subtract_fusion
  329.0 2.2 finish.1
  (272 shorter events, 78.1 us)
Async XLA Ops:
  6.3 19.7 %collective-permute-start.2 = (bf16[32,1536]{1,0:T(8,128)(2,1)S(1)}, bf16[32,1536]{1,0:T(8,128)(2,1)S(1)}, u32[]{:S(2)}, u32[]{:S(2)}) collective-permute-start(bf16[32,1536]{1,0:T(8,128)(2,1)S(1)} %get-tuple-element.170), channel_id=1, source_target_pairs={{0,12},{4,8},{8,4},{12,0},{1,13},{5,9},{9,5},{13,1},{2,14},{6,10},... | collective-permute-start | bytes 294920 | tf_op jit(solution)/shard_map/ppermute | solution.py:860
  11.5 14.5 %collective-permute-start.1 = (bf16[32,1536]{1,0:T(8,128)(2,1)S(1)}, bf16[32,1536]{1,0:T(8,128)(2,1)S(1)}, u32[]{:S(2)}, u32[]{:S(2)}) collective-permute-start(bf16[32,1536]{1,0:T(8,128)(2,1)S(1)} %get-tuple-element.171), channel_id=1, source_target_pairs={{0,8},{4,12},{8,0},{12,4},{1,9},{5,13},{9,1},{13,5},{2,10},{6,14},... | collective-permute-start | bytes 294920 | tf_op jit(solution)/shard_map/ppermute | solution.py:860
  11.5 14.5 %collective-permute-start = (bf16[32,1536]{1,0:T(8,128)(2,1)S(1)}, bf16[32,1536]{1,0:T(8,128)(2,1)S(1)}, u32[]{:S(2)}, u32[]{:S(2)}) collective-permute-start(bf16[32,1536]{1,0:T(8,128)(2,1)S(1)} %get-tuple-element.172), channel_id=1, source_target_pairs={{0,4},{4,0},{8,12},{12,8},{1,5},{5,1},{9,13},{13,9},{2,6},{6,2},{1... | collective-permute-start | bytes 294920 | tf_op jit(solution)/shard_map/ppermute | solution.py:860
  16.0 7.3 %collective-permute-start.10 = (bf16[48,1664]{1,0:T(8,128)(2,1)}, bf16[48,1664]{1,0:T(8,128)(2,1)S(1)}, u32[]{:S(2)}, u32[]{:S(2)}) collective-permute-start(bf16[48,1664]{1,0:T(8,128)(2,1)} %get-tuple-element.97), channel_id=1, source_target_pairs={{0,4},{4,0},{8,12},{12,8},{1,5},{5,1},{9,13},{13,9},{2,6},{6,2},{1... | collective-permute-start | bytes 479240 | tf_op jit(solution)/shard_map/ppermute | solution.py:860
  19.8 25.1 %collective-permute-start.8 = (bf16[96,768]{1,0:T(8,128)(2,1)S(1)}, bf16[96,768]{1,0:T(8,128)(2,1)S(1)}, u32[]{:S(2)}, u32[]{:S(2)}) collective-permute-start(bf16[96,768]{1,0:T(8,128)(2,1)S(1)} %pad_maximum_fusion.7), channel_id=1, source_target_pairs={{0,4},{4,0},{8,12},{12,8},{1,5},{5,1},{9,13},{13,9},{2,6},{6,2},{1... | collective-permute-start | bytes 442376 | tf_op jit(solution)/shard_map/ppermute | solution.py:860
  24.2 16.2 %collective-permute-start.11 = (bf16[96,1664]{1,0:T(8,128)(2,1)S(1)}, bf16[96,1664]{1,0:T(8,128)(2,1)S(1)}, u32[]{:S(2)}, u32[]{:S(2)}) collective-permute-start(bf16[96,1664]{1,0:T(8,128)(2,1)S(1)} %pad_maximum_fusion.4), channel_id=1, source_target_pairs={{0,8},{4,12},{8,0},{12,4},{1,9},{5,13},{9,1},{13,5},{2,10},{6,14},... | collective-permute-start | bytes 958472 | tf_op jit(solution)/shard_map/ppermute | solution.py:860
  26.0 18.3 %collective-permute-start.4 = (bf16[128,1536]{1,0:T(8,128)(2,1)S(1)}, bf16[128,1536]{1,0:T(8,128)(2,1)S(1)}, u32[]{:S(2)}, u32[]{:S(2)}) collective-permute-start(bf16[128,1536]{1,0:T(8,128)(2,1)S(1)} %pad_maximum_fusion.2.rest_0_.own), channel_id=1, source_target_pairs={{0,2},{1,3},{2,0},{3,1},{4,6},{5,7},{6,4},{7,5},{8,10},{9,11},{10,... | collective-permute-start | bytes 1179656 | tf_op jit(solution)/shard_map/ppermute | solution.py:860
  40.4 20.7 %collective-permute-start.12 = (bf16[192,1664]{1,0:T(8,128)(2,1)S(1)}, bf16[192,1664]{1,0:T(8,128)(2,1)S(1)}, u32[]{:S(2)}, u32[]{:S(2)}) collective-permute-start(bf16[192,1664]{1,0:T(8,128)(2,1)S(1)} %constant_dynamic-update-slice_fusion.3.r0), channel_id=1, source_target_pairs={{0,16},{16,0},{1,17},{17,1},{2,18},{18,2},{3,19},{19,3},{4,20},{20... | collective-permute-start | bytes 1916936 | tf_op jit(solution)/shard_map/ppermute | solution.py:860
  44.9 16.3 %collective-permute-start.9 = (bf16[192,768]{1,0:T(8,128)(2,1)S(1)}, bf16[192,768]{1,0:T(8,128)(2,1)S(1)}, u32[]{:S(2)}, u32[]{:S(2)}) collective-permute-start(bf16[192,768]{1,0:T(8,128)(2,1)S(1)} %constant_dynamic-update-slice_fusion.a0), channel_id=1, source_target_pairs={{0,8},{4,12},{8,0},{12,4},{1,9},{5,13},{9,1},{13,5},{2,10},{6,14},... | collective-permute-start | bytes 884744 | tf_op jit(solution)/shard_map/ppermute | solution.py:860
  52.7 8.4 %collective-permute-start.6 = (bf16[8,768]{1,0:T(8,128)(2,1)S(1)}, bf16[8,768]{1,0:T(8,128)(2,1)S(1)}, u32[]{:S(2)}, u32[]{:S(2)}) collective-permute-start(bf16[8,768]{1,0:T(8,128)(2,1)S(1)} %slice.105), channel_id=1, source_target_pairs={{0,4},{4,8},{8,12},{1,5},{5,9},{9,13},{2,6},{6,10},{10,14},{3,7},{... | collective-permute-start | bytes 36872 | tf_op jit(solution)/shard_map/ppermute | solution.py:855
  71.8 6.3 %collective-permute-start.14 = (f32[80,512]{1,0:T(8,128)S(1)}, f32[80,512]{1,0:T(8,128)S(1)}, u32[]{:S(2)}, u32[]{:S(2)}) collective-permute-start(f32[80,512]{1,0:T(8,128)S(1)} %add.143.pa), channel_id=1, source_target_pairs={{0,2},{1,3},{2,0},{3,1},{4,6},{5,7},{6,4},{7,5},{8,10},{9,11},{10,... | collective-permute-start | bytes 491528 | tf_op jit(solution)/shard_map/ppermute | solution.py:860
  92.2 5.1 %collective-permute-start.15 = (f32[24,384]{1,0:T(8,128)S(1)}, f32[24,384]{1,0:T(8,128)S(1)}, u32[]{:S(2)}, u32[]{:S(2)}) collective-permute-start(f32[24,384]{1,0:T(8,128)S(1)} %get-tuple-element.185), channel_id=1, source_target_pairs={{0,4},{4,0},{8,12},{12,8},{1,5},{5,1},{9,13},{13,9},{2,6},{6,2},{1... | collective-permute-start | bytes 110600 | tf_op jit(solution)/shard_map/ppermute | solution.py:860
  92.3 5.0 %collective-permute-start.16 = (f32[24,384]{1,0:T(8,128)S(1)}, f32[24,384]{1,0:T(8,128)S(1)}, u32[]{:S(2)}, u32[]{:S(2)}) collective-permute-start(f32[24,384]{1,0:T(8,128)S(1)} %get-tuple-element.184), channel_id=1, source_target_pairs={{0,8},{4,12},{8,0},{12,4},{1,9},{5,13},{9,1},{13,5},{2,10},{6,14},... | collective-permute-start | bytes 110600 | tf_op jit(solution)/shard_map/ppermute | solution.py:860
  94.2 5.8 %collective-permute-start.17 = (f32[24,384]{1,0:T(8,128)S(1)}, f32[24,384]{1,0:T(8,128)S(1)}, u32[]{:S(2)}, u32[]{:S(2)}) collective-permute-start(f32[24,384]{1,0:T(8,128)S(1)} %get-tuple-element.183), channel_id=1, source_target_pairs={{0,12},{4,8},{8,4},{12,0},{1,13},{5,9},{9,5},{13,1},{2,14},{6,10},... | collective-permute-start | bytes 110600 | tf_op jit(solution)/shard_map/ppermute | solution.py:860
  141.6 29.8 %collective-permute-start.32 = (bf16[1,1,192,1536]{3,2,1,0:T(8,128)(2,1)S(1)}, bf16[1,1,192,1536]{3,2,1,0:T(8,128)(2,1)S(1)}, u32[]{:S(2)}, u32[]{:S(2)}) collective-permute-start(bf16[1,1,192,1536]{3,2,1,0:T(8,128)(2,1)S(1)} %constant_dynamic-slice_fusion.6), channel_id=1, source_target_pairs={{0,16},{16,0},{1,17},{17,1},{2,18},{18,2},{3,19},{19,3},{4,20},{20... | collective-permute-start | bytes 1769480 | tf_op jit(solution)/shard_map/ppermute | solution.py:860
  144.2 6.4 %collective-permute-start.19 = (f32[80,512]{1,0:T(8,128)S(1)}, f32[80,512]{1,0:T(8,128)S(1)}, u32[]{:S(2)}, u32[]{:S(2)}) collective-permute-start(f32[80,512]{1,0:T(8,128)S(1)} %add.144.da_), channel_id=1, source_target_pairs={{0,2},{1,3},{2,0},{3,1},{4,6},{5,7},{6,4},{7,5},{8,10},{9,11},{10,... | collective-permute-start | bytes 491528 | tf_op jit(solution)/shard_map/ppermute | solution.py:860
  157.1 5.8 %collective-permute-start.20 = (f32[8,384]{1,0:T(8,128)}, f32[8,384]{1,0:T(8,128)S(1)}, u32[]{:S(2)}, u32[]{:S(2)}) collective-permute-start(f32[8,384]{1,0:T(8,128)} %get-tuple-element.118), channel_id=1, source_target_pairs={{4,0},{8,4},{12,8},{5,1},{9,5},{13,9},{6,2},{10,6},{14,10},{7,3},{... | collective-permute-start | bytes 36872 | tf_op jit(solution)/shard_map/ppermute | solution.py:855
  160.3 11.3 %collective-permute-start.29 = (bf16[1,1,192,896]{3,2,1,0:T(8,128)(2,1)}, bf16[1,1,192,896]{3,2,1,0:T(8,128)(2,1)S(1)}, u32[]{:S(2)}, u32[]{:S(2)}) collective-permute-start(bf16[1,1,192,896]{3,2,1,0:T(8,128)(2,1)} %constant_dynamic-slice_fusion.7), channel_id=1, source_target_pairs={{0,16},{16,0},{1,17},{17,1},{2,18},{18,2},{3,19},{19,3},{4,20},{20... | collective-permute-start | bytes 1032200 | tf_op jit(solution)/shard_map/ppermute | solution.py:860
  171.7 8.2 %collective-permute-start.30 = (bf16[2,1,48,896]{3,2,1,0:T(8,128)(2,1)S(1)}, bf16[2,1,48,896]{3,2,1,0:T(8,128)(2,1)S(1)}, u32[]{:S(2)}, u32[]{:S(2)}) collective-permute-start(bf16[2,1,48,896]{3,2,1,0:T(8,128)(2,1)S(1)} %dynamic-slice_convert_fusion.1), channel_id=1, source_target_pairs={{0,4},{4,0},{8,12},{12,8},{1,5},{5,1},{9,13},{13,9},{2,6},{6,2},{1... | collective-permute-start | bytes 516104 | tf_op jit(solution)/shard_map/ppermute | solution.py:860
  172.4 11.1 %collective-permute-start.33 = (bf16[2,1,48,1536]{3,2,1,0:T(8,128)(2,1)S(1)}, bf16[2,1,48,1536]{3,2,1,0:T(8,128)(2,1)S(1)}, u32[]{:S(2)}, u32[]{:S(2)}) collective-permute-start(bf16[2,1,48,1536]{3,2,1,0:T(8,128)(2,1)S(1)} %dynamic-slice_convert_fusion), channel_id=1, source_target_pairs={{0,4},{4,0},{8,12},{12,8},{1,5},{5,1},{9,13},{13,9},{2,6},{6,2},{1... | collective-permute-start | bytes 884744 | tf_op jit(solution)/shard_map/ppermute | solution.py:860
  180.0 8.0 %collective-permute-start.31 = (bf16[1,1,48,896]{3,2,1,0:T(8,128)(2,1)S(1)}, bf16[1,1,48,896]{3,2,1,0:T(8,128)(2,1)S(1)}, u32[]{:S(2)}, u32[]{:S(2)}) collective-permute-start(bf16[1,1,48,896]{3,2,1,0:T(8,128)(2,1)S(1)} %dynamic-slice_convert_fusion.3), channel_id=1, source_target_pairs={{0,8},{4,12},{8,0},{12,4},{1,9},{5,13},{9,1},{13,5},{2,10},{6,14},... | collective-permute-start | bytes 258056 | tf_op jit(solution)/shard_map/ppermute | solution.py:860
  183.6 8.2 %collective-permute-start.34 = (bf16[1,1,48,1536]{3,2,1,0:T(8,128)(2,1)S(1)}, bf16[1,1,48,1536]{3,2,1,0:T(8,128)(2,1)S(1)}, u32[]{:S(2)}, u32[]{:S(2)}) collective-permute-start(bf16[1,1,48,1536]{3,2,1,0:T(8,128)(2,1)S(1)} %dynamic-slice_convert_fusion.2), channel_id=1, source_target_pairs={{0,8},{4,12},{8,0},{12,4},{1,9},{5,13},{9,1},{13,5},{2,10},{6,14},... | collective-permute-start | bytes 442376 | tf_op jit(solution)/shard_map/ppermute | solution.py:860
  201.3 20.8 %collective-permute-start.35 = (f32[576,768]{1,0:T(8,128)}, f32[576,768]{1,0:T(8,128)}, u32[]{:S(2)}, u32[]{:S(2)}) collective-permute-start(f32[576,768]{1,0:T(8,128)} %get-tuple-element.135), channel_id=1, source_target_pairs={{0,1},{1,0},{2,3},{3,2},{4,5},{5,4},{6,7},{7,6},{8,9},{9,8},{10,11... | collective-permute-start | bytes 5308424 | tf_op jit(solution)/shard_map/ppermute | solution.py:860
  201.3 5.0 %collective-permute-start.21 = (bf16[256,1536]{1,0:T(8,128)(2,1)S(1)}, bf16[256,1536]{1,0:T(8,128)(2,1)S(1)}, u32[]{:S(2)}, u32[]{:S(2)}) collective-permute-start(bf16[256,1536]{1,0:T(8,128)(2,1)S(1)} %copy-done.46), channel_id=1, source_target_pairs={{0,1},{1,0},{2,3},{3,2},{4,5},{5,4},{6,7},{7,6},{8,9},{9,8},{10,11... | collective-permute-start | bytes 2359304 | tf_op jit(solution)/shard_map/ppermute | solution.py:860
  207.3 11.4 %collective-permute-start.22 = (bf16[128,1536]{1,0:T(8,128)(2,1)}, bf16[128,1536]{1,0:T(8,128)(2,1)S(1)}, u32[]{:S(2)}, u32[]{:S(2)}) collective-permute-start(bf16[128,1536]{1,0:T(8,128)(2,1)} %add_convert_fusion), channel_id=1, source_target_pairs={{0,2},{1,3},{2,0},{3,1},{4,6},{5,7},{6,4},{7,5},{8,10},{9,11},{10,... | collective-permute-start | bytes 1179656 | tf_op jit(solution)/shard_map/ppermute | solution.py:860
  224.0 11.4 %collective-permute-start.43 = (f32[288,384]{1,0:T(8,128)S(1)}, f32[288,384]{1,0:T(8,128)S(1)}, u32[]{:S(2)}, u32[]{:S(2)}) collective-permute-start(f32[288,384]{1,0:T(8,128)S(1)} %constant_dynamic-slice_fusion.2), channel_id=1, source_target_pairs={{0,16},{16,0},{1,17},{17,1},{2,18},{18,2},{3,19},{19,3},{4,20},{20... | collective-permute-start | bytes 1327112 | tf_op jit(solution)/shard_map/ppermute | solution.py:860
  225.3 11.7 %collective-permute-start.36 = (f32[288,384]{1,0:T(8,128)S(1)}, f32[288,384]{1,0:T(8,128)S(1)}, u32[]{:S(2)}, u32[]{:S(2)}) collective-permute-start(f32[288,384]{1,0:T(8,128)S(1)} %constant_dynamic-slice_fusion.5), channel_id=1, source_target_pairs={{0,2},{1,3},{2,0},{3,1},{4,6},{5,7},{6,4},{7,5},{8,10},{9,11},{10,... | collective-permute-start | bytes 1327112 | tf_op jit(solution)/shard_map/ppermute | solution.py:860
  226.2 28.4 %collective-permute-start.25 = (bf16[32,1536]{1,0:T(8,128)(2,1)S(1)}, bf16[32,1536]{1,0:T(8,128)(2,1)S(1)}, u32[]{:S(2)}, u32[]{:S(2)}) collective-permute-start(bf16[32,1536]{1,0:T(8,128)(2,1)S(1)} %get-tuple-element.166), channel_id=1, source_target_pairs={{0,12},{4,8},{8,4},{12,0},{1,13},{5,9},{9,5},{13,1},{2,14},{6,10},... | collective-permute-start | bytes 294920 | tf_op jit(solution)/shard_map/ppermute | solution.py:860
  227.9 26.7 %collective-permute-start.24 = (bf16[32,1536]{1,0:T(8,128)(2,1)S(1)}, bf16[32,1536]{1,0:T(8,128)(2,1)S(1)}, u32[]{:S(2)}, u32[]{:S(2)}) collective-permute-start(bf16[32,1536]{1,0:T(8,128)(2,1)S(1)} %get-tuple-element.167), channel_id=1, source_target_pairs={{0,8},{4,12},{8,0},{12,4},{1,9},{5,13},{9,1},{13,5},{2,10},{6,14},... | collective-permute-start | bytes 294920 | tf_op jit(solution)/shard_map/ppermute | solution.py:860
  227.9 26.7 %collective-permute-start.23 = (bf16[32,1536]{1,0:T(8,128)(2,1)S(1)}, bf16[32,1536]{1,0:T(8,128)(2,1)S(1)}, u32[]{:S(2)}, u32[]{:S(2)}) collective-permute-start(bf16[32,1536]{1,0:T(8,128)(2,1)S(1)} %get-tuple-element.168), channel_id=1, source_target_pairs={{0,4},{4,0},{8,12},{12,8},{1,5},{5,1},{9,13},{13,9},{2,6},{6,2},{1... | collective-permute-start | bytes 294920 | tf_op jit(solution)/shard_map/ppermute | solution.py:860
  235.5 6.0 %collective-permute-start.44 = (f32[144,384]{1,0:T(8,128)S(1)}, f32[144,384]{1,0:T(8,128)S(1)}, u32[]{:S(2)}, u32[]{:S(2)}) collective-permute-start(f32[144,384]{1,0:T(8,128)S(1)} %constant_dynamic-slice_fusion.1), channel_id=1, source_target_pairs={{0,2},{1,3},{2,0},{3,1},{4,6},{5,7},{6,4},{7,5},{8,10},{9,11},{10,... | collective-permute-start | bytes 663560 | tf_op jit(solution)/shard_map/ppermute | solution.py:860
  237.1 6.0 %collective-permute-start.37 = (f32[144,384]{1,0:T(8,128)S(1)}, f32[144,384]{1,0:T(8,128)S(1)}, u32[]{:S(2)}, u32[]{:S(2)}) collective-permute-start(f32[144,384]{1,0:T(8,128)S(1)} %constant_dynamic-slice_fusion.4), channel_id=1, source_target_pairs={{0,16},{16,0},{1,17},{17,1},{2,18},{18,2},{3,19},{19,3},{4,20},{20... | collective-permute-start | bytes 663560 | tf_op jit(solution)/shard_map/ppermute | solution.py:860
  241.5 4.8 %collective-permute-start.45 = (f32[72,384]{1,0:T(8,128)S(1)}, f32[72,384]{1,0:T(8,128)S(1)}, u32[]{:S(2)}, u32[]{:S(2)}) collective-permute-start(f32[72,384]{1,0:T(8,128)S(1)} %constant_dynamic-slice_fusion), channel_id=1, source_target_pairs={{0,4},{4,0},{8,12},{12,8},{1,5},{5,1},{9,13},{13,9},{2,6},{6,2},{1... | collective-permute-start | bytes 331784 | tf_op jit(solution)/shard_map/ppermute | solution.py:860
  243.2 5.9 %collective-permute-start.38 = (f32[72,384]{1,0:T(8,128)S(1)}, f32[72,384]{1,0:T(8,128)S(1)}, u32[]{:S(2)}, u32[]{:S(2)}) collective-permute-start(f32[72,384]{1,0:T(8,128)S(1)} %constant_dynamic-slice_fusion.3), channel_id=1, source_target_pairs={{0,4},{4,0},{8,12},{12,8},{1,5},{5,1},{9,13},{13,9},{2,6},{6,2},{1... | collective-permute-start | bytes 331784 | tf_op jit(solution)/shard_map/ppermute | solution.py:860
  246.4 8.1 %collective-permute-start.46 = (f32[72,384]{1,0:T(8,128)S(1)}, f32[72,384]{1,0:T(8,128)S(1)}, u32[]{:S(2)}, u32[]{:S(2)}) collective-permute-start(f32[72,384]{1,0:T(8,128)S(1)} %dynamic-slice_add_fusion.4), channel_id=1, source_target_pairs={{0,8},{4,12},{8,0},{12,4},{1,9},{5,13},{9,1},{13,5},{2,10},{6,14},... | collective-permute-start | bytes 331784 | tf_op jit(solution)/shard_map/ppermute | solution.py:860
  249.1 6.7 %collective-permute-start.39 = (f32[72,384]{1,0:T(8,128)S(1)}, f32[72,384]{1,0:T(8,128)S(1)}, u32[]{:S(2)}, u32[]{:S(2)}) collective-permute-start(f32[72,384]{1,0:T(8,128)S(1)} %dynamic-slice_add_fusion.5), channel_id=1, source_target_pairs={{0,8},{4,12},{8,0},{12,4},{1,9},{5,13},{9,1},{13,5},{2,10},{6,14},... | collective-permute-start | bytes 331784 | tf_op jit(solution)/shard_map/ppermute | solution.py:860
  254.5 4.8 %collective-permute-start.47 = (f32[72,384]{1,0:T(8,128)S(1)}, f32[72,384]{1,0:T(8,128)S(1)}, u32[]{:S(2)}, u32[]{:S(2)}) collective-permute-start(f32[72,384]{1,0:T(8,128)S(1)} %add.175), channel_id=1, source_target_pairs={{0,4},{4,0},{8,12},{12,8},{1,5},{5,1},{9,13},{13,9},{2,6},{6,2},{1... | collective-permute-start | bytes 331784 | tf_op jit(solution)/shard_map/ppermute | solution.py:860
  254.6 19.1 %collective-permute-start.27 = (bf16[128,1536]{1,0:T(8,128)(2,1)S(1)}, bf16[128,1536]{1,0:T(8,128)(2,1)S(1)}, u32[]{:S(2)}, u32[]{:S(2)}) collective-permute-start(bf16[128,1536]{1,0:T(8,128)(2,1)S(1)} %pad_maximum_fusion.3.rest_0_), channel_id=1, source_target_pairs={{0,2},{1,3},{2,0},{3,1},{4,6},{5,7},{6,4},{7,5},{8,10},{9,11},{10,... | collective-permute-start | bytes 1179656 | tf_op jit(solution)/shard_map/ppermute | solution.py:860
  255.8 4.8 %collective-permute-start.40 = (f32[72,384]{1,0:T(8,128)S(1)}, f32[72,384]{1,0:T(8,128)S(1)}, u32[]{:S(2)}, u32[]{:S(2)}) collective-permute-start(f32[72,384]{1,0:T(8,128)S(1)} %add.167), channel_id=1, source_target_pairs={{0,4},{4,0},{8,12},{12,8},{1,5},{5,1},{9,13},{13,9},{2,6},{6,2},{1... | collective-permute-start | bytes 331784 | tf_op jit(solution)/shard_map/ppermute | solution.py:860
  259.4 7.6 %collective-permute-start.48 = (f32[144,384]{1,0:T(8,128)S(1)}, f32[144,384]{1,0:T(8,128)S(1)}, u32[]{:S(2)}, u32[]{:S(2)}) collective-permute-start(f32[144,384]{1,0:T(8,128)S(1)} %pad_maximum_fusion.6), channel_id=1, source_target_pairs={{0,2},{1,3},{2,0},{3,1},{4,6},{5,7},{6,4},{7,5},{8,10},{9,11},{10,... | collective-permute-start | bytes 663560 | tf_op jit(solution)/shard_map/ppermute | solution.py:860
  260.6 8.4 %collective-permute-start.41 = (f32[144,384]{1,0:T(8,128)S(1)}, f32[144,384]{1,0:T(8,128)S(1)}, u32[]{:S(2)}, u32[]{:S(2)}) collective-permute-start(f32[144,384]{1,0:T(8,128)S(1)} %pad_maximum_fusion.5), channel_id=1, source_target_pairs={{0,16},{16,0},{1,17},{17,1},{2,18},{18,2},{3,19},{19,3},{4,20},{20... | collective-permute-start | bytes 663560 | tf_op jit(solution)/shard_map/ppermute | solution.py:860
  267.0 8.4 %collective-permute-start.49 = (f32[288,384]{1,0:T(8,128)S(1)}, f32[288,384]{1,0:T(8,128)S(1)}, u32[]{:S(2)}, u32[]{:S(2)}) collective-permute-start(f32[288,384]{1,0:T(8,128)S(1)} %pad_maximum_fusion.1), channel_id=1, source_target_pairs={{0,16},{16,0},{1,17},{17,1},{2,18},{18,2},{3,19},{19,3},{4,20},{20... | collective-permute-start | bytes 1327112 | tf_op jit(solution)/shard_map/ppermute | solution.py:860
  269.1 8.4 %collective-permute-start.42 = (f32[288,384]{1,0:T(8,128)S(1)}, f32[288,384]{1,0:T(8,128)S(1)}, u32[]{:S(2)}, u32[]{:S(2)}) collective-permute-start(f32[288,384]{1,0:T(8,128)S(1)} %pad_maximum_fusion), channel_id=1, source_target_pairs={{0,2},{1,3},{2,0},{3,1},{4,6},{5,7},{6,4},{7,5},{8,10},{9,11},{10,... | collective-permute-start | bytes 1327112 | tf_op jit(solution)/shard_map/ppermute | solution.py:860
  273.2 14.0 %collective-permute-start.51 = (f32[96,768]{1,0:T(8,128)}, f32[96,768]{1,0:T(8,128)}, u32[]{:S(2)}, u32[]{:S(2)}) collective-permute-start(f32[96,768]{1,0:T(8,128)} %get-tuple-element.141), channel_id=1, source_target_pairs={{0,1},{1,0},{2,3},{3,2},{4,5},{5,4},{6,7},{7,6},{8,9},{9,8},{10,11... | collective-permute-start | bytes 884744 | tf_op jit(solution)/shard_map/ppermute | solution.py:860
  273.2 8.8 %collective-permute-start.26 = (bf16[128,1536]{1,0:T(8,128)(2,1)S(1)}, bf16[128,1536]{1,0:T(8,128)(2,1)S(1)}, u32[]{:S(2)}, u32[]{:S(2)}) collective-permute-start(bf16[128,1536]{1,0:T(8,128)(2,1)S(1)} %pad_maximum_fusion.3.rest_0_), channel_id=1, source_target_pairs={{0,1},{1,0},{2,3},{3,2},{4,5},{5,4},{6,7},{7,6},{8,9},{9,8},{10,11... | collective-permute-start | bytes 1179656 | tf_op jit(solution)/shard_map/ppermute | solution.py:860
  273.7 8.3 %collective-permute-start.28 = (bf16[128,1536]{1,0:T(8,128)(2,1)S(1)}, bf16[128,1536]{1,0:T(8,128)(2,1)S(1)}, u32[]{:S(2)}, u32[]{:S(2)}) collective-permute-start(bf16[128,1536]{1,0:T(8,128)(2,1)S(1)} %collective-permute-done.27.rest_2_), channel_id=1, source_target_pairs={{0,1},{1,0},{2,3},{3,2},{4,5},{5,4},{6,7},{7,6},{8,9},{9,8},{10,11... | collective-permute-start | bytes 1179656 | tf_op jit(solution)/shard_map/ppermute | solution.py:860
  278.4 43.0 %collective-permute-start.50 = (f32[48,768]{1,0:T(8,128)}, f32[48,768]{1,0:T(8,128)}, u32[]{:S(2)}, u32[]{:S(2)}) collective-permute-start(f32[48,768]{1,0:T(8,128)} %slice.139), channel_id=1, source_target_pairs={{0,1},{1,0},{2,3},{3,2},{4,5},{5,4},{6,7},{7,6},{8,9},{9,8},{10,11... | collective-permute-start | bytes 442376 | tf_op jit(solution)/shard_map/ppermute | solution.py:860
  320.9 7.3 %collective-permute-start.52 = (f32[96,768]{1,0:T(8,128)}, f32[96,768]{1,0:T(8,128)S(1)}, u32[]{:S(2)}, u32[]{:S(2)}) collective-permute-start(f32[96,768]{1,0:T(8,128)} %get-tuple-element.143), channel_id=1, source_target_pairs={{0,1},{1,0},{2,3},{3,2},{4,5},{5,4},{6,7},{7,6},{8,9},{9,8},{10,11... | collective-permute-start | bytes 884744 | tf_op jit(solution)/shard_map/ppermute | solution.py:860
  (52 other events, 503.8 us)

commit v2 on v1

--- a/solution.py
+++ b/solution.py
@@ -137,34 +137,49 @@
     return call(front, outs, 10, 1, [pltpu.VMEM((T + 8, C), F32)])
 
 
+CHUNK = 128
+
+
+def at_lane(i, n):
+    shape = (CHUNK, n, LANES)
+    return lax.broadcasted_iota(jnp.int32, shape, 2) == lax.broadcasted_iota(jnp.int32, shape, 0) + i * CHUNK
+
+
+def row_totals(hi, lo):
+    rows = hi.shape[0] * hi.shape[1]
+    both = jnp.concatenate([hi.reshape(rows, LANES).astype(BF), lo.reshape(rows, LANES).astype(BF)], axis=1)
+    return dot_nn(both, jnp.ones((2 * LANES, LANES), BF)).reshape(hi.shape)
+
+
 def lane_sums(ref):
-    def join(a, b, w):
-        m = (lax.broadcasted_iota(jnp.int32, a.shape, 2) & w) == 0
-        if w == LANES // 2:
-            return jnp.where(m, a, b) + pltpu.roll(jnp.where(m, b, a), w, 2)
-        return jnp.where(m, a, b) + jnp.where(m, pltpu.roll(a, LANES - w, 2), pltpu.roll(b, w, 2))
-
-    w = LANES // 2
-    while w >= 8:
-
-        def chunk(i, c, w=w):
-            ref[pl.ds(i * 8, 8)] = join(ref[pl.ds(i * 8, 8)], ref[pl.ds(i * 8 + w, 8)], w)
-            return c
-
-        lax.fori_loop(0, w // 8, chunk, 0)
-        w //= 2
-    x = ref[0:8]
-    while w:
-        x = join(x[0:w], x[w : 2 * w], w)
-        w //= 2
-    return x[0]
+    n = ref.shape[1]
+
+    def chunk(i, tot):
+        x = ref[pl.ds(i * CHUNK, CHUNK)]
+        hi = x.astype(BF).astype(F32)
+        return tot + jnp.sum(jnp.where(at_lane(i, n), row_totals(hi, x - hi), 0.0), axis=0)
+
+    return lax.fori_loop(0, LANES // CHUNK, chunk, jnp.zeros((n, LANES), F32))
+
+
+def spread(x, out, base):
+    n = x.shape[0]
+    hi = x.astype(BF).astype(F32)
+    lo = x - hi
+
+    def chunk(i, c):
+        m = at_lane(i, n)
+        out[pl.ds(base + i * CHUNK, CHUNK)] = row_totals(jnp.where(m, hi[None], 0.0), jnp.where(m, lo[None], 0.0))
+        return c
+
+    lax.fori_loop(0, LANES // CHUNK, chunk, 0)
 
 
 def make_carry(T, C, docs, XW, R, N, CT):
     RB = 64
     LT = C // LANES
 
-    def carry(sc, pa, pb, u, z, dg, wt, dtb, alog, pt_o, da_o, du_o, dyin_o, pre_o, ends_o):
+    def carry(sc, pa, pb, u, z, dg, wt, dtb, alog, pt_o, da_o, du_o, dyin_o, pre_o, ends_o, bs, cs):
         c0 = pl.multiple_of(sc[0], LANES)
         pt = pa[...] + pb[...]
         pt_o[...] = pt
@@ -201,24 +216,26 @@
             bt = pt_o[R_ : R_ + N, pl.ds(pl.multiple_of(k * LANES, LANES), LANES)]
             ct = pt_o[R_ + N : R_ + 2 * N, pl.ds(pl.multiple_of((nb - 1 - k) * LANES, LANES), LANES)]
 
+            spread(bt, bs, 0)
+            spread(ct, cs, 0)
+
             def inner(i, c):
-                h, g, bt, ct = c
+                h, g = c
                 h = list(h)
                 g = list(g)
                 fi = k * (LANES // 8) + i
                 ri = T // 8 - 1 - fi
                 for j in range(8):
-                    bb = jnp.broadcast_to(bt[:, j : j + 1], (N, LANES))
-                    cc = jnp.broadcast_to(ct[:, LANES - 1 - j : LANES - j], (N, LANES))
+                    bb = bs[i * 8 + j]
+                    cc = cs[LANES - 1 - i * 8 - j]
                     df, uf = rows(da_o, fi, j), rows(du_o, fi, j)
                     db, yb = rows(da_o, ri, 7 - j), rows(dyin_o, ri, 7 - j)
                     for l in range(LT):
                         h[l] = jnp.exp2(df[l] * am2[l]) * h[l] + uf[l] * bb
                         g[l] = jnp.exp2(db[l] * am2[l]) * (g[l] + yb[l] * cc)
-                return tuple(h), tuple(g), pltpu.roll(bt, LANES - 8, 1), pltpu.roll(ct, 8, 1)
-
-            h, g, _, _ = lax.fori_loop(0, LANES // 8, inner, (c[0], c[1], bt, ct))
-            return h, g
+                return tuple(h), tuple(g)
+
+            return lax.fori_loop(0, LANES // 8, inner, (c[0], c[1]))
 
         R_ = R
         zero = tuple(jnp.zeros((N, LANES), F32) for _ in range(LT))
@@ -230,7 +247,7 @@
             ends_o[d, N : N + 8, :] = jnp.broadcast_to(tot, (8, C))
 
     outs = [((XW, T), F32)] + [((T // 8, 8, C), F32)] * 3 + [((T, C), F32)] + [((CT, N + 8, C), F32)]
-    return call(carry, outs, 9, 1)
+    return call(carry, outs, 9, 1, [pltpu.VMEM((LANES, N, LANES), F32)] * 2)
 
 
 def make_scan(T, C, D, docs, XW, R, N, CT):
@@ -242,7 +259,7 @@
         ends = rest[: CT - 1]
         (
             g_o, dz_o, du1_o, dpre_o, dp_o, mix_o, pw_o, pdt_o, vec_o,
-            a_s, h_s, y_s, lb_s, dd_s, sb_s, sc_s,
+            a_s, h_s, y_s, lb_s, dd_s, sb_s, sc_s, bs, cs,
         ) = rest[CT - 1 :]
         c0 = pl.multiple_of(sc[0], LANES)
         am = [-jnp.exp(alog[:, pl.ds(c0 + l * LANES, LANES)]) for l in range(LT)]
@@ -271,17 +288,16 @@
 
         def fouter(k, h):
             blk = pl.ds(pl.multiple_of(k * LANES, LANES), LANES)
-            bt = pt[R : R + N, blk]
-            ct = pt[R + N : R + 2 * N, blk]
-
-            def inner(i, c):
-                h, bt, ct = c
+            spread(pt[R : R + N, blk], bs, k * LANES)
+            spread(pt[R + N : R + 2 * N, blk], cs, k * LANES)
+
+            def inner(i, h):
                 h = list(h)
                 fi = k * (LANES // 8) + i
                 for j in range(8):
                     t = fi * 8 + j
-                    bb = jnp.broadcast_to(bt[:, j : j + 1], (N, LANES))
-                    cc = jnp.broadcast_to(ct[:, j : j + 1], (N, LANES))
+                    bb = bs[t]
+                    cc = cs[t]
                     dr, ur = rows(da, fi, j), rows(du, fi, j)
                     for l in range(LT):
                         a = jnp.exp2(dr[l] * am2[l])
@@ -289,21 +305,19 @@
                         h[l] = a * h[l] + ur[l] * bb
                         h_s[t + 1, :, sl[l]] = h[l]
                         y_s[fi, j : j + 1, sl[l]] = jnp.sum(h[l] * cc, axis=0, keepdims=True)
-                return tuple(h), pltpu.roll(bt, LANES - 8, 1), pltpu.roll(ct, LANES - 8, 1)
-
-            return lax.fori_loop(0, LANES // 8, inner, (h, bt, ct))[0]
+                return tuple(h)
+
+            return lax.fori_loop(0, LANES // 8, inner, h)
 
         lax.fori_loop(0, nb, fouter, tuple(hin))
 
         def bouter(k, c):
             kb = nb - 1 - k
             blk = pl.ds(pl.multiple_of(kb * LANES, LANES), LANES)
-            bt = pt[R : R + N, blk]
-            ct = pt[R + N : R + 2 * N, blk]
             zero = jnp.zeros((N, LANES), F32)
 
             def inner(i, c):
-                g, ga, bt, ct = c
+                g, ga = c
                 g = list(g)
                 ga = list(ga)
                 l0 = LANES - 1 - i * 8
@@ -311,8 +325,8 @@
                 for j in range(8):
                     t = kb * LANES + l0 - j
                     jj = 7 - j
-                    bb = jnp.broadcast_to(bt[:, LANES - 1 - j : LANES - j], (N, LANES))
-                    cc = jnp.broadcast_to(ct[:, LANES - 1 - j : LANES - j], (N, LANES))
+                    bb = bs[t]
+                    cc = cs[t]
                     sb = zero
                     scc = zero
                     dr, ur, yr = rows(da, fi, jj), rows(du, fi, jj), rows(dyin, fi, jj)
@@ -335,9 +349,9 @@
                         scc = scc + dyr * h_s[t + 1, :, sl[l]]
                     sb_s[l0 - j] = sb
                     sc_s[l0 - j] = scc
-                return tuple(g), tuple(ga), pltpu.roll(bt, 8, 1), pltpu.roll(ct, 8, 1)
-
-            g, ga, _, _ = lax.fori_loop(0, LANES // 8, inner, (c[0], c[1], bt, ct))
+                return tuple(g), tuple(ga)
+
+            g, ga = lax.fori_loop(0, LANES // 8, inner, (c[0], c[1]))
             dp_o[R : R + N, blk] = lane_sums(sb_s)
             dp_o[R + N : R + 2 * N, blk] = lane_sums(sc_s)
             return g, ga
@@ -381,7 +395,7 @@
     outs = [((T, C), BF), ((T, C), BF), ((T, C), F32), ((T, C), BF), ((XW, T), F32), ((T, D), BF),
             ((C, 2 * D), BF), ((R, C), F32), ((8 + N, C), F32)]
     scratch = [pltpu.VMEM((T, N, C), F32), pltpu.VMEM((T + 1, N, C), F32)] + [pltpu.VMEM((T // 8, 8, C), F32)] * 3
-    scratch += [pltpu.VMEM((LANES, N, LANES), F32)] * 2
+    scratch += [pltpu.VMEM((LANES, N, LANES), F32)] * 2 + [pltpu.VMEM((T, N, LANES), F32)] * 2
     return call(scan, outs, 14 + CT, 1, scratch)
 
 

time: 333 us -> 319 us (0.958)
  Pallas kernels: 135 us -> 121 us
    pallas_call x1, Pallas kernels: 39.8 us -> 26.7 us  [on_device(): make_scan(tokens, channels, width, docs, xw, rank, states, ctx_count)]
  transfers between devices with their start and end apart: 53 -> 53, of which waited for: 30 -> 30; matrix products, arithmetic and copies ran while one was open for 9% -> 10% of each run, Pallas kernels for 17% -> 18%
where the time goes in v2:
time: 319 us; the launch traced here: 318 us
  Pallas kernels  121 us (38%)
  waiting for transfers between devices  97.5 us (31%)
  starting transfers between devices  51.5 us (16%)
  local copies, waits for them, and re-layouts  30.3 us (9%)
  other arithmetic  14.9 us (5%)
    ppermute x51, waiting for transfers between devices, swap(): return lax.ppermute(value, axis, [(i, i ^ bit) for i in range(devices)])  95.3 us
    ppermute x51, starting transfers between devices, swap(): return lax.ppermute(value, axis, [(i, i ^ bit) for i in range(devices)])  46 us
    pallas_call x1, Pallas kernels, on_device(): make_muon(width, own_rows, xw, rank, pack, full)  33.7 us
    pallas_call x1, Pallas kernels, on_device(): make_scan(tokens, channels, width, docs, xw, rank, states, ctx_count)  26.7 us
    unnamed x108, local copies, waits for them, and re-layouts  14.6 us
    pallas_call x1, Pallas kernels, on_device(): make_carry(tokens, channels, docs, xw, rank, states, ctx_count)  11.9 us
    pallas_call x1, Pallas kernels, on_device(): make_front(tokens, channels, width, docs, xw, rank, ctx_count, fsdp_count...  7.1 us
  transfers between devices with their start and end apart: 53, of which 30 were waited for; matrix products, arithmetic and copies ran while one was open for 10% of the time, Pallas kernels for 18%

profile of v2, /device:TPU:0, one launch (start us, length us, event | category | flops | bytes accessed | tf_op | source)
XLA Modules:
  0.0 317.6 jit_solution(3875109115071226166)
XLA Ops:
  2.6 2.7 send.1
  6.3 5.1 %collective-permute-start.2 = (bf16[32,1536]{1,0:T(8,128)(2,1)S(1)}, bf16[32,1536]{1,0:T(8,128)(2,1)S(1)}, u32[]{:S(2)}, u32[]{:S(2)}) collective-permute-start(bf16[32,1536]{1,0:T(8,128)(2,1)S(1)} %get-tuple-element.170), channel_id=1, source_target_pairs={{0,12},{4,8},{8,4},{12,0},{1,13},{5,9},{9,5},{13,1},{2,14},{6,10},... | collective-permute-start | bytes 294920 | tf_op jit(solution)/shard_map/ppermute | solution.py:874
  12.1 2.2 pack.1
  14.3 1.7 collective-permute-start.7
  21.2 2.0 collective-permute-done.10
  24.2 1.8 collective-permute-start.11
  27.6 12.8 %collective-permute-done.11 = bf16[96,1664]{1,0:T(8,128)(2,1)S(1)} collective-permute-done((bf16[96,1664]{1,0:T(8,128)(2,1)S(1)}, bf16[96,1664]{1,0:T(8,128)(2,1)S(1)}, u32[]{:S(2)}, u32[]{:S(2)}) %collective-permute-start.11) | collective-permute-done | bytes 319520 | tf_op jit(solution)/shard_map/ppermute | solution.py:874
  40.9 2.7 plan.1
  47.4 4.6 %recv.1 = (bf16[512,768]{1,0:T(8,128)(2,1)}, bf16[512,768]{1,0:T(8,128)(2,1)}, bf16[512,768]{1,0:T(8,128)(2,1)}) custom-call(bf16[512,512]{1,0:T(8,128)(2,1)} %get-tuple-element.92.rt, f32[1,768]{1,0:T(1,128)} %reshape.164.gain, bf16[128,1536]{1,0:T(8,128)(2,1)} %copy-done.1, bf16[128,1536]{1,0:T(8,128)(2,1)} %copy-done.19, bf16[128,1536]{1,0:T(8,128)(2,1)} %copy-done.17, ...), custom_call_target="tpu_custom_call" | custom-call | tf_op jit(solution)/shard_map/recv/pallas_call | solution.py:1024
  52.7 4.0 %collective-permute-start.6 = (bf16[8,768]{1,0:T(8,128)(2,1)S(1)}, bf16[8,768]{1,0:T(8,128)(2,1)S(1)}, u32[]{:S(2)}, u32[]{:S(2)}) collective-permute-start(bf16[8,768]{1,0:T(8,128)(2,1)S(1)} %slice.105), channel_id=1, source_target_pairs={{0,4},{4,8},{8,12},{1,5},{5,9},{9,13},{2,6},{6,10},{10,14},{3,7},{... | collective-permute-start | bytes 36872 | tf_op jit(solution)/shard_map/ppermute | solution.py:869
  58.0 3.2 collective-permute-done.9.a1
  62.1 7.1 %front.1 = (bf16[384,768]{1,0:T(8,128)(2,1)}, bf16[384,1664]{1,0:T(8,128)(2,1)}, bf16[512,384]{1,0:T(8,128)(2,1)}, bf16[512,384]{1,0:T(8,128)(2,1)}, bf16[512,38...) custom-call(s32[7]{0:T(128)} %pad_add_fusion.1.sc, ...), custom_call_target="tpu_custom_call" | custom-call | tf_op jit(solution)/shard_map/front/pallas_call | solution.py:1029
  73.9 4.2 %collective-permute-done.14.pb = f32[80,512]{1,0:T(8,128)S(1)} collective-permute-done((f32[80,512]{1,0:T(8,128)S(1)}, f32[80,512]{1,0:T(8,128)S(1)}, u32[]{:S(2)}, u32[]{:S(2)}) %collective-permute-start.14) | collective-permute-done | bytes 163872 | tf_op jit(solution)/shard_map/ppermute | solution.py:874
  78.8 11.9 %carry.1 = (f32[80,512]{1,0:T(8,128)}, f32[64,8,384]{2,1,0:T(8,128)}, f32[64,8,384]{2,1,0:T(8,128)}, f32[64,8,384]{2,1,0:T(8,128)}, f32[512,384]{1,0:T(8,128)}, /*index=5*/f32[4,24,384]{2,1,0:T(8,128)}) custom-call(s32[7]{0:T(128)} %pad_add_fusion.1.sc, f32[80,512]{1,0:T(8,128)} %copy-done.12, f32[80,512]{1,0:T(8,128)} %copy-done.27, ...), custom_call_target="tpu_custom_call" | custom-call | tf_op jit(solution)/shard_map/carry/pallas_call | solution.py:1033
  91.6 1.9 collective-permute-start.16
  93.5 2.5 collective-permute-start.17
  96.6 2.7 collective-permute-done.17.rest_2_
  99.9 26.7 %scan.1 = (bf16[512,384]{1,0:T(8,128)(2,1)}, bf16[512,384]{1,0:T(8,128)(2,1)}, f32[512,384]{1,0:T(8,128)}, bf16[512,384]{1,0:T(8,128)(2,1)}, f32[80,512]{1,0:T(8...) custom-call(s32[7]{0:T(128)} %pad_add_fusion.1.sc, ...), custom_call_target="tpu_custom_call" | custom-call | tf_op jit(solution)/shard_map/scan/pallas_call | solution.py:1037
  127.8 1.7 collective-permute-start.32
  132.0 4.8 %collective-permute-done.19.db_ = f32[80,512]{1,0:T(8,128)S(1)} collective-permute-done((f32[80,512]{1,0:T(8,128)S(1)}, f32[80,512]{1,0:T(8,128)S(1)}, u32[]{:S(2)}, u32[]{:S(2)}) %collective-permute-start.19) | collective-permute-done | bytes 163872 | tf_op jit(solution)/shard_map/ppermute | solution.py:874
  137.5 5.8 %back.1 = (f32[512,384]{1,0:T(8,128)}, f32[8,384]{1,0:T(8,128)}, bf16[384,896]{1,0:T(8,128)(2,1)}, f32[24,384]{1,0:T(8,128)}) custom-call(s32[7]{0:T(128)} %pad_add_fusion.1.sc, f32[80,512]{1,0:T(8,128)} %copy-done.11, f32[80,512]{1,0:T(8,128)} %copy-done.26, f32[512,384]{1,0:T(8,128)} %get-tuple-element.111.du1, f32[512,384]{1,0:T(8,128)} %get-tuple-element.112.v, ...), custom_call_target="tpu_custom_call" | custom-call | tf_op jit(solution)/shard_map/back/pallas_call | solution.py:1046
  144.8 1.7 constant_dynamic-slice_fusion.7
  146.9 2.1 collective-permute-done.20.spill
  149.7 5.7 %last.1 = (bf16[256,1536]{1,0:T(8,128)(2,1)}, bf16[256,1536]{1,0:T(8,128)(2,1)}, f32[1,768]{1,0:T(1,128)}) custom-call(f32[512,384]{1,0:T(8,128)} %get-tuple-element.117.dxu, f32[8,384]{1,0:T(8,128)} %copy-done.44, bf16[512,384]{1,0:T(8,128)(2,1)} %get-tuple-element.119.dz, bf16[384,768]{1,0:T(8,128)(2,1)} %get-tuple-element.120.wa, ...), custom_call_target="tpu_custom_call" | custom-call | tf_op jit(solution)/shard_map/last/pallas_call | solution.py:1051
  160.1 6.0 %collective-permute-done.30 = bf16[2,1,48,896]{3,2,1,0:T(8,128)(2,1)S(1)} collective-permute-done((bf16[2,1,48,896]{3,2,1,0:T(8,128)(2,1)S(1)}, bf16[2,1,48,896]{3,2,1,0:T(8,128)(2,1)S(1)}, u32[]{:S(2)}, u32[]{:S(2)}) %collective-permute-start.30) | collective-permute-done | bytes 172064 | tf_op jit(solution)/shard_map/ppermute | solution.py:874
  166.3 3.4 %collective-permute-done.33 = bf16[2,1,48,1536]{3,2,1,0:T(8,128)(2,1)S(1)} collective-permute-done((bf16[2,1,48,1536]{3,2,1,0:T(8,128)(2,1)S(1)}, bf16[2,1,48,1536]{3,2,1,0:T(8,128)(2,1)S(1)}, u32[]{:S(2)}, u32[]{:S(2)}) %collective-permute-start.33) | collective-permute-done | bytes 294944 | tf_op jit(solution)/shard_map/ppermute | solution.py:874
  169.9 4.4 %collective-permute-done.31 = bf16[1,1,48,896]{3,2,1,0:T(8,128)(2,1)S(1)} collective-permute-done((bf16[1,1,48,896]{3,2,1,0:T(8,128)(2,1)S(1)}, bf16[1,1,48,896]{3,2,1,0:T(8,128)(2,1)S(1)}, u32[]{:S(2)}, u32[]{:S(2)}) %collective-permute-start.31) | collective-permute-done | bytes 86048 | tf_op jit(solution)/shard_map/ppermute | solution.py:874
  174.9 3.1 collective-permute-done.34
  178.8 3.0 gram_out.1
  181.8 5.8 %gram_in.1 = (f32[48,2,768]{2,1,0:T(2,128)}, f32[48,2,768]{2,1,0:T(2,128)}, f32[48,80]{1,0:T(8,128)}, f32[48,80]{1,0:T(8,128)}, f32[48,48]{1,0:T(8,128)}, /*inde...) custom-call(s32[2]{0:T(128)} %pad_add_fusion.rsc.place, ...), custom_call_target="tpu_custom_call" | custom-call | tf_op jit(solution)/shard_map/gram_in/pallas_call | solution.py:1072
  188.1 4.5 %collective-permute-done.21.got = bf16[256,1536]{1,0:T(8,128)(2,1)S(1)} collective-permute-done((bf16[256,1536]{1,0:T(8,128)(2,1)S(1)}, bf16[256,1536]{1,0:T(8,128)(2,1)S(1)}, u32[]{:S(2)}, u32[]{:S(2)}) %collective-permute-start.21) | collective-permute-done | bytes 786464 | tf_op jit(solution)/shard_map/ppermute | solution.py:874
  197.7 7.2 %collective-permute-done.22.far = bf16[128,1536]{1,0:T(8,128)(2,1)S(1)} collective-permute-done((bf16[128,1536]{1,0:T(8,128)(2,1)}, bf16[128,1536]{1,0:T(8,128)(2,1)S(1)}, u32[]{:S(2)}, u32[]{:S(2)}) %collective-permute-start.22) | collective-permute-done | bytes 393248 | tf_op jit(solution)/shard_map/ppermute | solution.py:874
  205.7 2.7 norm_back.1
  208.3 1.7 add.157
  212.4 1.7 collective-permute-start.25
  214.1 2.7 collective-permute-start.23
  216.9 4.8 %collective-permute-done.43 = f32[288,384]{1,0:T(8,128)S(1)} collective-permute-done((f32[288,384]{1,0:T(8,128)S(1)}, f32[288,384]{1,0:T(8,128)S(1)}, u32[]{:S(2)}, u32[]{:S(2)}) %collective-permute-start.43) | collective-permute-done | bytes 442400 | tf_op jit(solution)/shard_map/ppermute | solution.py:874
  223.9 3.8 %collective-permute-done.44 = f32[144,384]{1,0:T(8,128)S(1)} collective-permute-done((f32[144,384]{1,0:T(8,128)S(1)}, f32[144,384]{1,0:T(8,128)S(1)}, u32[]{:S(2)}, u32[]{:S(2)}) %collective-permute-start.44) | collective-permute-done | bytes 221216 | tf_op jit(solution)/shard_map/ppermute | solution.py:874
  230.0 2.6 collective-permute-done.45
  232.7 2.6 collective-permute-done.38
  236.0 4.8 %collective-permute-done.46 = f32[72,384]{1,0:T(8,128)S(1)} collective-permute-done((f32[72,384]{1,0:T(8,128)S(1)}, f32[72,384]{1,0:T(8,128)S(1)}, u32[]{:S(2)}, u32[]{:S(2)}) %collective-permute-start.46) | collective-permute-done | bytes 110624 | tf_op jit(solution)/shard_map/ppermute | solution.py:874
  243.6 2.1 collective-permute-done.47
  248.1 5.1 %collective-permute-done.48 = f32[144,384]{1,0:T(8,128)S(1)} collective-permute-done((f32[144,384]{1,0:T(8,128)S(1)}, f32[144,384]{1,0:T(8,128)S(1)}, u32[]{:S(2)}, u32[]{:S(2)}) %collective-permute-start.48) | collective-permute-done | bytes 221216 | tf_op jit(solution)/shard_map/ppermute | solution.py:874
  261.7 2.0 collective-permute-done.42
  269.2 4.3 %final.1 = (bf16[512,768]{1,0:T(8,128)(2,1)}, bf16[512,768]{1,0:T(8,128)(2,1)}) custom-call(bf16[512,512]{1,0:T(8,128)(2,1)} %get-tuple-element.91.fin, bf16[128,1536]{1,0:T(8,128)(2,1)} %copy-done.5, bf16[128,1536]{1,0:T(8,128)(2,1)} %copy-done.16, bf16[128,1536]{1,0:T(8,128)(2,1)} %copy-done.15, bf16[128,1536]{1,0:T(8,128)(2,1)} %copy-done.18), custom_call_target="tpu_custom_call" | custom-call | tf_op jit(solution)/shard_map/final/pallas_call | solution.py:1060
  273.5 33.7 %muon.1 = (f32[96,768]{1,0:T(8,128)}, f32[96,768]{1,0:T(8,128)}) custom-call(s32[2]{0:T(128)} %pad_add_fusion.rsc.place, f32[576,768]{1,0:T(8,128)} %copy-done, f32[96,768]{1,0:T(8,128)} %get-tuple-element.140.um, f32[96,768]{1,0:T(8,128)} %collective-permute-done.51.ua), custom_call_target="tpu_custom_call" | custom-call | tf_op jit(solution)/shard_map/muon/pallas_call | solution.py:1076
  309.0 1.7 multiply_subtract_fusion
  315.3 2.2 finish.1
  (272 shorter events, 77.7 us)
Async XLA Ops:
  6.3 19.7 %collective-permute-start.2 = (bf16[32,1536]{1,0:T(8,128)(2,1)S(1)}, bf16[32,1536]{1,0:T(8,128)(2,1)S(1)}, u32[]{:S(2)}, u32[]{:S(2)}) collective-permute-start(bf16[32,1536]{1,0:T(8,128)(2,1)S(1)} %get-tuple-element.170), channel_id=1, source_target_pairs={{0,12},{4,8},{8,4},{12,0},{1,13},{5,9},{9,5},{13,1},{2,14},{6,10},... | collective-permute-start | bytes 294920 | tf_op jit(solution)/shard_map/ppermute | solution.py:874
  11.5 14.5 %collective-permute-start.1 = (bf16[32,1536]{1,0:T(8,128)(2,1)S(1)}, bf16[32,1536]{1,0:T(8,128)(2,1)S(1)}, u32[]{:S(2)}, u32[]{:S(2)}) collective-permute-start(bf16[32,1536]{1,0:T(8,128)(2,1)S(1)} %get-tuple-element.171), channel_id=1, source_target_pairs={{0,8},{4,12},{8,0},{12,4},{1,9},{5,13},{9,1},{13,5},{2,10},{6,14},... | collective-permute-start | bytes 294920 | tf_op jit(solution)/shard_map/ppermute | solution.py:874
  11.5 14.5 %collective-permute-start = (bf16[32,1536]{1,0:T(8,128)(2,1)S(1)}, bf16[32,1536]{1,0:T(8,128)(2,1)S(1)}, u32[]{:S(2)}, u32[]{:S(2)}) collective-permute-start(bf16[32,1536]{1,0:T(8,128)(2,1)S(1)} %get-tuple-element.172), channel_id=1, source_target_pairs={{0,4},{4,0},{8,12},{12,8},{1,5},{5,1},{9,13},{13,9},{2,6},{6,2},{1... | collective-permute-start | bytes 294920 | tf_op jit(solution)/shard_map/ppermute | solution.py:874
  16.0 7.3 %collective-permute-start.10 = (bf16[48,1664]{1,0:T(8,128)(2,1)}, bf16[48,1664]{1,0:T(8,128)(2,1)S(1)}, u32[]{:S(2)}, u32[]{:S(2)}) collective-permute-start(bf16[48,1664]{1,0:T(8,128)(2,1)} %get-tuple-element.97), channel_id=1, source_target_pairs={{0,4},{4,0},{8,12},{12,8},{1,5},{5,1},{9,13},{13,9},{2,6},{6,2},{1... | collective-permute-start | bytes 479240 | tf_op jit(solution)/shard_map/ppermute | solution.py:874
  19.8 25.1 %collective-permute-start.8 = (bf16[96,768]{1,0:T(8,128)(2,1)S(1)}, bf16[96,768]{1,0:T(8,128)(2,1)S(1)}, u32[]{:S(2)}, u32[]{:S(2)}) collective-permute-start(bf16[96,768]{1,0:T(8,128)(2,1)S(1)} %pad_maximum_fusion.7), channel_id=1, source_target_pairs={{0,4},{4,0},{8,12},{12,8},{1,5},{5,1},{9,13},{13,9},{2,6},{6,2},{1... | collective-permute-start | bytes 442376 | tf_op jit(solution)/shard_map/ppermute | solution.py:874
  24.2 16.2 %collective-permute-start.11 = (bf16[96,1664]{1,0:T(8,128)(2,1)S(1)}, bf16[96,1664]{1,0:T(8,128)(2,1)S(1)}, u32[]{:S(2)}, u32[]{:S(2)}) collective-permute-start(bf16[96,1664]{1,0:T(8,128)(2,1)S(1)} %pad_maximum_fusion.4), channel_id=1, source_target_pairs={{0,8},{4,12},{8,0},{12,4},{1,9},{5,13},{9,1},{13,5},{2,10},{6,14},... | collective-permute-start | bytes 958472 | tf_op jit(solution)/shard_map/ppermute | solution.py:874
  26.0 18.3 %collective-permute-start.4 = (bf16[128,1536]{1,0:T(8,128)(2,1)S(1)}, bf16[128,1536]{1,0:T(8,128)(2,1)S(1)}, u32[]{:S(2)}, u32[]{:S(2)}) collective-permute-start(bf16[128,1536]{1,0:T(8,128)(2,1)S(1)} %pad_maximum_fusion.2.rest_0_.own), channel_id=1, source_target_pairs={{0,2},{1,3},{2,0},{3,1},{4,6},{5,7},{6,4},{7,5},{8,10},{9,11},{10,... | collective-permute-start | bytes 1179656 | tf_op jit(solution)/shard_map/ppermute | solution.py:874
  40.4 20.7 %collective-permute-start.12 = (bf16[192,1664]{1,0:T(8,128)(2,1)S(1)}, bf16[192,1664]{1,0:T(8,128)(2,1)S(1)}, u32[]{:S(2)}, u32[]{:S(2)}) collective-permute-start(bf16[192,1664]{1,0:T(8,128)(2,1)S(1)} %constant_dynamic-update-slice_fusion.3.r0), channel_id=1, source_target_pairs={{0,16},{16,0},{1,17},{17,1},{2,18},{18,2},{3,19},{19,3},{4,20},{20... | collective-permute-start | bytes 1916936 | tf_op jit(solution)/shard_map/ppermute | solution.py:874
  44.9 16.3 %collective-permute-start.9 = (bf16[192,768]{1,0:T(8,128)(2,1)S(1)}, bf16[192,768]{1,0:T(8,128)(2,1)S(1)}, u32[]{:S(2)}, u32[]{:S(2)}) collective-permute-start(bf16[192,768]{1,0:T(8,128)(2,1)S(1)} %constant_dynamic-update-slice_fusion.a0), channel_id=1, source_target_pairs={{0,8},{4,12},{8,0},{12,4},{1,9},{5,13},{9,1},{13,5},{2,10},{6,14},... | collective-permute-start | bytes 884744 | tf_op jit(solution)/shard_map/ppermute | solution.py:874
  52.7 8.4 %collective-permute-start.6 = (bf16[8,768]{1,0:T(8,128)(2,1)S(1)}, bf16[8,768]{1,0:T(8,128)(2,1)S(1)}, u32[]{:S(2)}, u32[]{:S(2)}) collective-permute-start(bf16[8,768]{1,0:T(8,128)(2,1)S(1)} %slice.105), channel_id=1, source_target_pairs={{0,4},{4,8},{8,12},{1,5},{5,9},{9,13},{2,6},{6,10},{10,14},{3,7},{... | collective-permute-start | bytes 36872 | tf_op jit(solution)/shard_map/ppermute | solution.py:869
  71.8 6.3 %collective-permute-start.14 = (f32[80,512]{1,0:T(8,128)S(1)}, f32[80,512]{1,0:T(8,128)S(1)}, u32[]{:S(2)}, u32[]{:S(2)}) collective-permute-start(f32[80,512]{1,0:T(8,128)S(1)} %add.143.pa), channel_id=1, source_target_pairs={{0,2},{1,3},{2,0},{3,1},{4,6},{5,7},{6,4},{7,5},{8,10},{9,11},{10,... | collective-permute-start | bytes 491528 | tf_op jit(solution)/shard_map/ppermute | solution.py:874
  91.5 5.1 %collective-permute-start.15 = (f32[24,384]{1,0:T(8,128)S(1)}, f32[24,384]{1,0:T(8,128)S(1)}, u32[]{:S(2)}, u32[]{:S(2)}) collective-permute-start(f32[24,384]{1,0:T(8,128)S(1)} %get-tuple-element.185), channel_id=1, source_target_pairs={{0,4},{4,0},{8,12},{12,8},{1,5},{5,1},{9,13},{13,9},{2,6},{6,2},{1... | collective-permute-start | bytes 110600 | tf_op jit(solution)/shard_map/ppermute | solution.py:874
  91.6 5.0 %collective-permute-start.16 = (f32[24,384]{1,0:T(8,128)S(1)}, f32[24,384]{1,0:T(8,128)S(1)}, u32[]{:S(2)}, u32[]{:S(2)}) collective-permute-start(f32[24,384]{1,0:T(8,128)S(1)} %get-tuple-element.184), channel_id=1, source_target_pairs={{0,8},{4,12},{8,0},{12,4},{1,9},{5,13},{9,1},{13,5},{2,10},{6,14},... | collective-permute-start | bytes 110600 | tf_op jit(solution)/shard_map/ppermute | solution.py:874
  93.5 5.8 %collective-permute-start.17 = (f32[24,384]{1,0:T(8,128)S(1)}, f32[24,384]{1,0:T(8,128)S(1)}, u32[]{:S(2)}, u32[]{:S(2)}) collective-permute-start(f32[24,384]{1,0:T(8,128)S(1)} %get-tuple-element.183), channel_id=1, source_target_pairs={{0,12},{4,8},{8,4},{12,0},{1,13},{5,9},{9,5},{13,1},{2,14},{6,10},... | collective-permute-start | bytes 110600 | tf_op jit(solution)/shard_map/ppermute | solution.py:874
  127.8 29.8 %collective-permute-start.32 = (bf16[1,1,192,1536]{3,2,1,0:T(8,128)(2,1)S(1)}, bf16[1,1,192,1536]{3,2,1,0:T(8,128)(2,1)S(1)}, u32[]{:S(2)}, u32[]{:S(2)}) collective-permute-start(bf16[1,1,192,1536]{3,2,1,0:T(8,128)(2,1)S(1)} %constant_dynamic-slice_fusion.6), channel_id=1, source_target_pairs={{0,16},{16,0},{1,17},{17,1},{2,18},{18,2},{3,19},{19,3},{4,20},{20... | collective-permute-start | bytes 1769480 | tf_op jit(solution)/shard_map/ppermute | solution.py:874
  130.4 6.4 %collective-permute-start.19 = (f32[80,512]{1,0:T(8,128)S(1)}, f32[80,512]{1,0:T(8,128)S(1)}, u32[]{:S(2)}, u32[]{:S(2)}) collective-permute-start(f32[80,512]{1,0:T(8,128)S(1)} %add.144.da_), channel_id=1, source_target_pairs={{0,2},{1,3},{2,0},{3,1},{4,6},{5,7},{6,4},{7,5},{8,10},{9,11},{10,... | collective-permute-start | bytes 491528 | tf_op jit(solution)/shard_map/ppermute | solution.py:874
  143.3 5.8 %collective-permute-start.20 = (f32[8,384]{1,0:T(8,128)}, f32[8,384]{1,0:T(8,128)S(1)}, u32[]{:S(2)}, u32[]{:S(2)}) collective-permute-start(f32[8,384]{1,0:T(8,128)} %get-tuple-element.118), channel_id=1, source_target_pairs={{4,0},{8,4},{12,8},{5,1},{9,5},{13,9},{6,2},{10,6},{14,10},{7,3},{... | collective-permute-start | bytes 36872 | tf_op jit(solution)/shard_map/ppermute | solution.py:869
  146.5 11.2 %collective-permute-start.29 = (bf16[1,1,192,896]{3,2,1,0:T(8,128)(2,1)}, bf16[1,1,192,896]{3,2,1,0:T(8,128)(2,1)S(1)}, u32[]{:S(2)}, u32[]{:S(2)}) collective-permute-start(bf16[1,1,192,896]{3,2,1,0:T(8,128)(2,1)} %constant_dynamic-slice_fusion.7), channel_id=1, source_target_pairs={{0,16},{16,0},{1,17},{17,1},{2,18},{18,2},{3,19},{19,3},{4,20},{20... | collective-permute-start | bytes 1032200 | tf_op jit(solution)/shard_map/ppermute | solution.py:874
  157.9 8.2 %collective-permute-start.30 = (bf16[2,1,48,896]{3,2,1,0:T(8,128)(2,1)S(1)}, bf16[2,1,48,896]{3,2,1,0:T(8,128)(2,1)S(1)}, u32[]{:S(2)}, u32[]{:S(2)}) collective-permute-start(bf16[2,1,48,896]{3,2,1,0:T(8,128)(2,1)S(1)} %dynamic-slice_convert_fusion.1), channel_id=1, source_target_pairs={{0,4},{4,0},{8,12},{12,8},{1,5},{5,1},{9,13},{13,9},{2,6},{6,2},{1... | collective-permute-start | bytes 516104 | tf_op jit(solution)/shard_map/ppermute | solution.py:874
  158.6 11.1 %collective-permute-start.33 = (bf16[2,1,48,1536]{3,2,1,0:T(8,128)(2,1)S(1)}, bf16[2,1,48,1536]{3,2,1,0:T(8,128)(2,1)S(1)}, u32[]{:S(2)}, u32[]{:S(2)}) collective-permute-start(bf16[2,1,48,1536]{3,2,1,0:T(8,128)(2,1)S(1)} %dynamic-slice_convert_fusion), channel_id=1, source_target_pairs={{0,4},{4,0},{8,12},{12,8},{1,5},{5,1},{9,13},{13,9},{2,6},{6,2},{1... | collective-permute-start | bytes 884744 | tf_op jit(solution)/shard_map/ppermute | solution.py:874
  166.2 8.0 %collective-permute-start.31 = (bf16[1,1,48,896]{3,2,1,0:T(8,128)(2,1)S(1)}, bf16[1,1,48,896]{3,2,1,0:T(8,128)(2,1)S(1)}, u32[]{:S(2)}, u32[]{:S(2)}) collective-permute-start(bf16[1,1,48,896]{3,2,1,0:T(8,128)(2,1)S(1)} %dynamic-slice_convert_fusion.3), channel_id=1, source_target_pairs={{0,8},{4,12},{8,0},{12,4},{1,9},{5,13},{9,1},{13,5},{2,10},{6,14},... | collective-permute-start | bytes 258056 | tf_op jit(solution)/shard_map/ppermute | solution.py:874
  169.8 8.3 %collective-permute-start.34 = (bf16[1,1,48,1536]{3,2,1,0:T(8,128)(2,1)S(1)}, bf16[1,1,48,1536]{3,2,1,0:T(8,128)(2,1)S(1)}, u32[]{:S(2)}, u32[]{:S(2)}) collective-permute-start(bf16[1,1,48,1536]{3,2,1,0:T(8,128)(2,1)S(1)} %dynamic-slice_convert_fusion.2), channel_id=1, source_target_pairs={{0,8},{4,12},{8,0},{12,4},{1,9},{5,13},{9,1},{13,5},{2,10},{6,14},... | collective-permute-start | bytes 442376 | tf_op jit(solution)/shard_map/ppermute | solution.py:874
  187.6 20.8 %collective-permute-start.35 = (f32[576,768]{1,0:T(8,128)}, f32[576,768]{1,0:T(8,128)}, u32[]{:S(2)}, u32[]{:S(2)}) collective-permute-start(f32[576,768]{1,0:T(8,128)} %get-tuple-element.135), channel_id=1, source_target_pairs={{0,1},{1,0},{2,3},{3,2},{4,5},{5,4},{6,7},{7,6},{8,9},{9,8},{10,11... | collective-permute-start | bytes 5308424 | tf_op jit(solution)/shard_map/ppermute | solution.py:874
  187.6 5.0 %collective-permute-start.21 = (bf16[256,1536]{1,0:T(8,128)(2,1)S(1)}, bf16[256,1536]{1,0:T(8,128)(2,1)S(1)}, u32[]{:S(2)}, u32[]{:S(2)}) collective-permute-start(bf16[256,1536]{1,0:T(8,128)(2,1)S(1)} %copy-done.46), channel_id=1, source_target_pairs={{0,1},{1,0},{2,3},{3,2},{4,5},{5,4},{6,7},{7,6},{8,9},{9,8},{10,11... | collective-permute-start | bytes 2359304 | tf_op jit(solution)/shard_map/ppermute | solution.py:874
  193.5 11.4 %collective-permute-start.22 = (bf16[128,1536]{1,0:T(8,128)(2,1)}, bf16[128,1536]{1,0:T(8,128)(2,1)S(1)}, u32[]{:S(2)}, u32[]{:S(2)}) collective-permute-start(bf16[128,1536]{1,0:T(8,128)(2,1)} %add_convert_fusion), channel_id=1, source_target_pairs={{0,2},{1,3},{2,0},{3,1},{4,6},{5,7},{6,4},{7,5},{8,10},{9,11},{10,... | collective-permute-start | bytes 1179656 | tf_op jit(solution)/shard_map/ppermute | solution.py:874
  210.2 11.4 %collective-permute-start.43 = (f32[288,384]{1,0:T(8,128)S(1)}, f32[288,384]{1,0:T(8,128)S(1)}, u32[]{:S(2)}, u32[]{:S(2)}) collective-permute-start(f32[288,384]{1,0:T(8,128)S(1)} %constant_dynamic-slice_fusion.2), channel_id=1, source_target_pairs={{0,16},{16,0},{1,17},{17,1},{2,18},{18,2},{3,19},{19,3},{4,20},{20... | collective-permute-start | bytes 1327112 | tf_op jit(solution)/shard_map/ppermute | solution.py:874
  211.5 11.7 %collective-permute-start.36 = (f32[288,384]{1,0:T(8,128)S(1)}, f32[288,384]{1,0:T(8,128)S(1)}, u32[]{:S(2)}, u32[]{:S(2)}) collective-permute-start(f32[288,384]{1,0:T(8,128)S(1)} %constant_dynamic-slice_fusion.5), channel_id=1, source_target_pairs={{0,2},{1,3},{2,0},{3,1},{4,6},{5,7},{6,4},{7,5},{8,10},{9,11},{10,... | collective-permute-start | bytes 1327112 | tf_op jit(solution)/shard_map/ppermute | solution.py:874
  212.4 28.5 %collective-permute-start.25 = (bf16[32,1536]{1,0:T(8,128)(2,1)S(1)}, bf16[32,1536]{1,0:T(8,128)(2,1)S(1)}, u32[]{:S(2)}, u32[]{:S(2)}) collective-permute-start(bf16[32,1536]{1,0:T(8,128)(2,1)S(1)} %get-tuple-element.166), channel_id=1, source_target_pairs={{0,12},{4,8},{8,4},{12,0},{1,13},{5,9},{9,5},{13,1},{2,14},{6,10},... | collective-permute-start | bytes 294920 | tf_op jit(solution)/shard_map/ppermute | solution.py:874
  214.1 26.8 %collective-permute-start.24 = (bf16[32,1536]{1,0:T(8,128)(2,1)S(1)}, bf16[32,1536]{1,0:T(8,128)(2,1)S(1)}, u32[]{:S(2)}, u32[]{:S(2)}) collective-permute-start(bf16[32,1536]{1,0:T(8,128)(2,1)S(1)} %get-tuple-element.167), channel_id=1, source_target_pairs={{0,8},{4,12},{8,0},{12,4},{1,9},{5,13},{9,1},{13,5},{2,10},{6,14},... | collective-permute-start | bytes 294920 | tf_op jit(solution)/shard_map/ppermute | solution.py:874
  214.1 26.8 %collective-permute-start.23 = (bf16[32,1536]{1,0:T(8,128)(2,1)S(1)}, bf16[32,1536]{1,0:T(8,128)(2,1)S(1)}, u32[]{:S(2)}, u32[]{:S(2)}) collective-permute-start(bf16[32,1536]{1,0:T(8,128)(2,1)S(1)} %get-tuple-element.168), channel_id=1, source_target_pairs={{0,4},{4,0},{8,12},{12,8},{1,5},{5,1},{9,13},{13,9},{2,6},{6,2},{1... | collective-permute-start | bytes 294920 | tf_op jit(solution)/shard_map/ppermute | solution.py:874
  221.7 6.0 %collective-permute-start.44 = (f32[144,384]{1,0:T(8,128)S(1)}, f32[144,384]{1,0:T(8,128)S(1)}, u32[]{:S(2)}, u32[]{:S(2)}) collective-permute-start(f32[144,384]{1,0:T(8,128)S(1)} %constant_dynamic-slice_fusion.1), channel_id=1, source_target_pairs={{0,2},{1,3},{2,0},{3,1},{4,6},{5,7},{6,4},{7,5},{8,10},{9,11},{10,... | collective-permute-start | bytes 663560 | tf_op jit(solution)/shard_map/ppermute | solution.py:874
  223.3 6.0 %collective-permute-start.37 = (f32[144,384]{1,0:T(8,128)S(1)}, f32[144,384]{1,0:T(8,128)S(1)}, u32[]{:S(2)}, u32[]{:S(2)}) collective-permute-start(f32[144,384]{1,0:T(8,128)S(1)} %constant_dynamic-slice_fusion.4), channel_id=1, source_target_pairs={{0,16},{16,0},{1,17},{17,1},{2,18},{18,2},{3,19},{19,3},{4,20},{20... | collective-permute-start | bytes 663560 | tf_op jit(solution)/shard_map/ppermute | solution.py:874
  227.8 4.8 %collective-permute-start.45 = (f32[72,384]{1,0:T(8,128)S(1)}, f32[72,384]{1,0:T(8,128)S(1)}, u32[]{:S(2)}, u32[]{:S(2)}) collective-permute-start(f32[72,384]{1,0:T(8,128)S(1)} %constant_dynamic-slice_fusion), channel_id=1, source_target_pairs={{0,4},{4,0},{8,12},{12,8},{1,5},{5,1},{9,13},{13,9},{2,6},{6,2},{1... | collective-permute-start | bytes 331784 | tf_op jit(solution)/shard_map/ppermute | solution.py:874
  229.4 5.9 %collective-permute-start.38 = (f32[72,384]{1,0:T(8,128)S(1)}, f32[72,384]{1,0:T(8,128)S(1)}, u32[]{:S(2)}, u32[]{:S(2)}) collective-permute-start(f32[72,384]{1,0:T(8,128)S(1)} %constant_dynamic-slice_fusion.3), channel_id=1, source_target_pairs={{0,4},{4,0},{8,12},{12,8},{1,5},{5,1},{9,13},{13,9},{2,6},{6,2},{1... | collective-permute-start | bytes 331784 | tf_op jit(solution)/shard_map/ppermute | solution.py:874
  232.6 8.2 %collective-permute-start.46 = (f32[72,384]{1,0:T(8,128)S(1)}, f32[72,384]{1,0:T(8,128)S(1)}, u32[]{:S(2)}, u32[]{:S(2)}) collective-permute-start(f32[72,384]{1,0:T(8,128)S(1)} %dynamic-slice_add_fusion.4), channel_id=1, source_target_pairs={{0,8},{4,12},{8,0},{12,4},{1,9},{5,13},{9,1},{13,5},{2,10},{6,14},... | collective-permute-start | bytes 331784 | tf_op jit(solution)/shard_map/ppermute | solution.py:874
  235.3 6.7 %collective-permute-start.39 = (f32[72,384]{1,0:T(8,128)S(1)}, f32[72,384]{1,0:T(8,128)S(1)}, u32[]{:S(2)}, u32[]{:S(2)}) collective-permute-start(f32[72,384]{1,0:T(8,128)S(1)} %dynamic-slice_add_fusion.5), channel_id=1, source_target_pairs={{0,8},{4,12},{8,0},{12,4},{1,9},{5,13},{9,1},{13,5},{2,10},{6,14},... | collective-permute-start | bytes 331784 | tf_op jit(solution)/shard_map/ppermute | solution.py:874
  240.9 4.8 %collective-permute-start.47 = (f32[72,384]{1,0:T(8,128)S(1)}, f32[72,384]{1,0:T(8,128)S(1)}, u32[]{:S(2)}, u32[]{:S(2)}) collective-permute-start(f32[72,384]{1,0:T(8,128)S(1)} %add.175), channel_id=1, source_target_pairs={{0,4},{4,0},{8,12},{12,8},{1,5},{5,1},{9,13},{13,9},{2,6},{6,2},{1... | collective-permute-start | bytes 331784 | tf_op jit(solution)/shard_map/ppermute | solution.py:874
  241.0 18.9 %collective-permute-start.27 = (bf16[128,1536]{1,0:T(8,128)(2,1)S(1)}, bf16[128,1536]{1,0:T(8,128)(2,1)S(1)}, u32[]{:S(2)}, u32[]{:S(2)}) collective-permute-start(bf16[128,1536]{1,0:T(8,128)(2,1)S(1)} %pad_maximum_fusion.3.rest_0_), channel_id=1, source_target_pairs={{0,2},{1,3},{2,0},{3,1},{4,6},{5,7},{6,4},{7,5},{8,10},{9,11},{10,... | collective-permute-start | bytes 1179656 | tf_op jit(solution)/shard_map/ppermute | solution.py:874
  242.0 4.8 %collective-permute-start.40 = (f32[72,384]{1,0:T(8,128)S(1)}, f32[72,384]{1,0:T(8,128)S(1)}, u32[]{:S(2)}, u32[]{:S(2)}) collective-permute-start(f32[72,384]{1,0:T(8,128)S(1)} %add.167), channel_id=1, source_target_pairs={{0,4},{4,0},{8,12},{12,8},{1,5},{5,1},{9,13},{13,9},{2,6},{6,2},{1... | collective-permute-start | bytes 331784 | tf_op jit(solution)/shard_map/ppermute | solution.py:874
  245.7 7.5 %collective-permute-start.48 = (f32[144,384]{1,0:T(8,128)S(1)}, f32[144,384]{1,0:T(8,128)S(1)}, u32[]{:S(2)}, u32[]{:S(2)}) collective-permute-start(f32[144,384]{1,0:T(8,128)S(1)} %pad_maximum_fusion.6), channel_id=1, source_target_pairs={{0,2},{1,3},{2,0},{3,1},{4,6},{5,7},{6,4},{7,5},{8,10},{9,11},{10,... | collective-permute-start | bytes 663560 | tf_op jit(solution)/shard_map/ppermute | solution.py:874
  246.9 8.4 %collective-permute-start.41 = (f32[144,384]{1,0:T(8,128)S(1)}, f32[144,384]{1,0:T(8,128)S(1)}, u32[]{:S(2)}, u32[]{:S(2)}) collective-permute-start(f32[144,384]{1,0:T(8,128)S(1)} %pad_maximum_fusion.5), channel_id=1, source_target_pairs={{0,16},{16,0},{1,17},{17,1},{2,18},{18,2},{3,19},{19,3},{4,20},{20... | collective-permute-start | bytes 663560 | tf_op jit(solution)/shard_map/ppermute | solution.py:874
  253.3 8.4 %collective-permute-start.49 = (f32[288,384]{1,0:T(8,128)S(1)}, f32[288,384]{1,0:T(8,128)S(1)}, u32[]{:S(2)}, u32[]{:S(2)}) collective-permute-start(f32[288,384]{1,0:T(8,128)S(1)} %pad_maximum_fusion.1), channel_id=1, source_target_pairs={{0,16},{16,0},{1,17},{17,1},{2,18},{18,2},{3,19},{19,3},{4,20},{20... | collective-permute-start | bytes 1327112 | tf_op jit(solution)/shard_map/ppermute | solution.py:874
  255.4 8.4 %collective-permute-start.42 = (f32[288,384]{1,0:T(8,128)S(1)}, f32[288,384]{1,0:T(8,128)S(1)}, u32[]{:S(2)}, u32[]{:S(2)}) collective-permute-start(f32[288,384]{1,0:T(8,128)S(1)} %pad_maximum_fusion), channel_id=1, source_target_pairs={{0,2},{1,3},{2,0},{3,1},{4,6},{5,7},{6,4},{7,5},{8,10},{9,11},{10,... | collective-permute-start | bytes 1327112 | tf_op jit(solution)/shard_map/ppermute | solution.py:874
  259.4 14.0 %collective-permute-start.51 = (f32[96,768]{1,0:T(8,128)}, f32[96,768]{1,0:T(8,128)}, u32[]{:S(2)}, u32[]{:S(2)}) collective-permute-start(f32[96,768]{1,0:T(8,128)} %get-tuple-element.141), channel_id=1, source_target_pairs={{0,1},{1,0},{2,3},{3,2},{4,5},{5,4},{6,7},{7,6},{8,9},{9,8},{10,11... | collective-permute-start | bytes 884744 | tf_op jit(solution)/shard_map/ppermute | solution.py:874
  259.4 8.8 %collective-permute-start.26 = (bf16[128,1536]{1,0:T(8,128)(2,1)S(1)}, bf16[128,1536]{1,0:T(8,128)(2,1)S(1)}, u32[]{:S(2)}, u32[]{:S(2)}) collective-permute-start(bf16[128,1536]{1,0:T(8,128)(2,1)S(1)} %pad_maximum_fusion.3.rest_0_), channel_id=1, source_target_pairs={{0,1},{1,0},{2,3},{3,2},{4,5},{5,4},{6,7},{7,6},{8,9},{9,8},{10,11... | collective-permute-start | bytes 1179656 | tf_op jit(solution)/shard_map/ppermute | solution.py:874
  260.0 8.3 %collective-permute-start.28 = (bf16[128,1536]{1,0:T(8,128)(2,1)S(1)}, bf16[128,1536]{1,0:T(8,128)(2,1)S(1)}, u32[]{:S(2)}, u32[]{:S(2)}) collective-permute-start(bf16[128,1536]{1,0:T(8,128)(2,1)S(1)} %collective-permute-done.27.rest_2_), channel_id=1, source_target_pairs={{0,1},{1,0},{2,3},{3,2},{4,5},{5,4},{6,7},{7,6},{8,9},{9,8},{10,11... | collective-permute-start | bytes 1179656 | tf_op jit(solution)/shard_map/ppermute | solution.py:874
  264.7 43.1 %collective-permute-start.50 = (f32[48,768]{1,0:T(8,128)}, f32[48,768]{1,0:T(8,128)}, u32[]{:S(2)}, u32[]{:S(2)}) collective-permute-start(f32[48,768]{1,0:T(8,128)} %slice.139), channel_id=1, source_target_pairs={{0,1},{1,0},{2,3},{3,2},{4,5},{5,4},{6,7},{7,6},{8,9},{9,8},{10,11... | collective-permute-start | bytes 442376 | tf_op jit(solution)/shard_map/ppermute | solution.py:874
  307.2 7.3 %collective-permute-start.52 = (f32[96,768]{1,0:T(8,128)}, f32[96,768]{1,0:T(8,128)S(1)}, u32[]{:S(2)}, u32[]{:S(2)}) collective-permute-start(f32[96,768]{1,0:T(8,128)} %get-tuple-element.143), channel_id=1, source_target_pairs={{0,1},{1,0},{2,3},{3,2},{4,5},{5,4},{6,7},{7,6},{8,9},{9,8},{10,11... | collective-permute-start | bytes 884744 | tf_op jit(solution)/shard_map/ppermute | solution.py:874
  (52 other events, 503.2 us)

commit v3 on v2

--- a/solution.py
+++ b/solution.py
@@ -917,9 +917,8 @@
     return jnp.concatenate(done, axis=1)
 
 
-def to_owners(grads, rows):
-    steps = [("fsdp", b) for b in bits_of("fsdp")[::-1]] + [("ctx", b) for b in bits_of("ctx")]
-    value = grads
+def to_owners(value, rows, axes=("fsdp", "ctx")):
+    steps = [(a, b) for a in axes for b in bits_of(a)[:: -1 if a == "fsdp" else 1]]
     for axis, bit in steps:
         if axis == "fsdp":
             value = value.reshape(1, 2, value.shape[0] // 2, value.shape[1])
@@ -1047,14 +1046,17 @@
         scal, dp_pair, swap(dp_pair, "tp", 2), du_one, conv_out, conv_act, conv_in, x_halo, w_turn, conv_weight,
         vec_part, part_dt, normed, halo,
     )
-    got_two = to_owners(grads_two, own_rows)
+    two = to_owners(grads_two, own_rows, ("fsdp",))
     keep, away, g_gain = make_last(tokens, channels, width, quarter)(
         d_conv_in, shifted(spill, "ctx", -1), d_gate, w_in, w_rest, mix_part, stream_x, route
     )
 
     near = swap(away, "tp", 1)
     cross = (keep[quarter:].astype(F32) + near[quarter:].astype(F32)).astype(BF)
+    two, cross = lax.optimization_barrier((two, cross))
+    got_two = to_owners(two, own_rows, ("ctx",))
     back = make_norm_back(quarter, width)(keep, near, swap(cross, "tp", 2), own, gain_row)[0]
+    got_two, back = lax.optimization_barrier((got_two, back))
     home = over_ctx(back)
     home_far = swap(home, "tp", 2)
     block_out, input_grad = make_final(tokens, width, tp_count)(

time: 319 us -> 314 us (0.984)
  waiting for transfers between devices: 97.5 us -> 82.1 us
  starting transfers between devices: 51.5 us -> 57.2 us
    ppermute x51, waiting for transfers between devices: 95.3 us -> 80 us  [swap(): return lax.ppermute(value, axis, [(i, i ^ bit) for i in range(devices)])]
    ppermute x51, starting transfers between devices: 46 us -> 51.7 us  [swap(): return lax.ppermute(value, axis, [(i, i ^ bit) for i in range(devices)])]
    unnamed x108 -> x102, local copies, waits for them, and re-layouts: 14.6 us -> 14.6 us
  transfers between devices with their start and end apart: 53 -> 53, of which waited for: 30 -> 27; matrix products, arithmetic and copies ran while one was open for 10% -> 11% of each run, Pallas kernels for 18% -> 18%
where the time goes in v3:
time: 314 us; the launch traced here: 312 us
  Pallas kernels  121 us (39%)
  waiting for transfers between devices  82.1 us (26%)
  starting transfers between devices  57.2 us (18%)
  local copies, waits for them, and re-layouts  32.5 us (10%)
  other arithmetic  17 us (5%)
    ppermute x51, waiting for transfers between devices, swap(): return lax.ppermute(value, axis, [(i, i ^ bit) for i in range(devices)])  80 us
    ppermute x51, starting transfers between devices, swap(): return lax.ppermute(value, axis, [(i, i ^ bit) for i in range(devices)])  51.7 us
    pallas_call x1, Pallas kernels, on_device(): make_muon(width, own_rows, xw, rank, pack, full)  33.7 us
    pallas_call x1, Pallas kernels, on_device(): make_scan(tokens, channels, width, docs, xw, rank, states, ctx_count)  26.7 us
    unnamed x102, local copies, waits for them, and re-layouts  14.6 us
    pallas_call x1, Pallas kernels, on_device(): make_carry(tokens, channels, docs, xw, rank, states, ctx_count)  11.9 us
    pallas_call x1, Pallas kernels, on_device(): make_front(tokens, channels, width, docs, xw, rank, ctx_count, fsdp_count...  7.1 us
  transfers between devices with their start and end apart: 53, of which 27 were waited for; matrix products, arithmetic and copies ran while one was open for 11% of the time, Pallas kernels for 18%

profile of v3, /device:TPU:0, one launch (start us, length us, event | category | flops | bytes accessed | tf_op | source)
XLA Modules:
  0.0 312.2 jit_solution(12577521683662358322)
XLA Ops:
  2.6 2.7 send.1
  6.3 5.1 %collective-permute-start.2 = (bf16[32,1536]{1,0:T(8,128)(2,1)S(1)}, bf16[32,1536]{1,0:T(8,128)(2,1)S(1)}, u32[]{:S(2)}, u32[]{:S(2)}) collective-permute-start(bf16[32,1536]{1,0:T(8,128)(2,1)S(1)} %get-tuple-element.178), channel_id=1, source_target_pairs={{0,12},{4,8},{8,4},{12,0},{1,13},{5,9},{9,5},{13,1},{2,14},{6,10},... | collective-permute-start | bytes 294920 | tf_op jit(solution)/shard_map/ppermute | solution.py:874
  12.1 2.2 pack.1
  14.3 1.7 collective-permute-start.7
  21.2 2.0 collective-permute-done.10
  24.2 1.8 collective-permute-start.11
  27.6 12.8 %collective-permute-done.11 = bf16[96,1664]{1,0:T(8,128)(2,1)S(1)} collective-permute-done((bf16[96,1664]{1,0:T(8,128)(2,1)S(1)}, bf16[96,1664]{1,0:T(8,128)(2,1)S(1)}, u32[]{:S(2)}, u32[]{:S(2)}) %collective-permute-start.11) | collective-permute-done | bytes 319520 | tf_op jit(solution)/shard_map/ppermute | solution.py:874
  40.9 2.7 plan.1
  47.4 4.6 %recv.1 = (bf16[512,768]{1,0:T(8,128)(2,1)}, bf16[512,768]{1,0:T(8,128)(2,1)}, bf16[512,768]{1,0:T(8,128)(2,1)}) custom-call(bf16[512,512]{1,0:T(8,128)(2,1)} %get-tuple-element.96.rt, f32[1,768]{1,0:T(1,128)} %reshape.170.gain, bf16[128,1536]{1,0:T(8,128)(2,1)} %copy-done.1, bf16[128,1536]{1,0:T(8,128)(2,1)} %copy-done.17, bf16[128,1536]{1,0:T(8,128)(2,1)} %copy-done.15, ...), custom_call_target="tpu_custom_call" | custom-call | tf_op jit(solution)/shard_map/recv/pallas_call | solution.py:1023
  52.7 4.1 %collective-permute-start.6 = (bf16[8,768]{1,0:T(8,128)(2,1)S(1)}, bf16[8,768]{1,0:T(8,128)(2,1)S(1)}, u32[]{:S(2)}, u32[]{:S(2)}) collective-permute-start(bf16[8,768]{1,0:T(8,128)(2,1)S(1)} %slice.105), channel_id=1, source_target_pairs={{0,4},{4,8},{8,12},{1,5},{5,9},{9,13},{2,6},{6,10},{10,14},{3,7},{... | collective-permute-start | bytes 36872 | tf_op jit(solution)/shard_map/ppermute | solution.py:869
  58.0 3.2 %collective-permute-done.9.a1 = bf16[192,768]{1,0:T(8,128)(2,1)S(1)} collective-permute-done((bf16[192,768]{1,0:T(8,128)(2,1)S(1)}, bf16[192,768]{1,0:T(8,128)(2,1)S(1)}, u32[]{:S(2)}, u32[]{:S(2)}) %collective-permute-start.9) | collective-permute-done | bytes 294944 | tf_op jit(solution)/shard_map/ppermute | solution.py:874
  62.1 7.1 %front.1 = (bf16[384,768]{1,0:T(8,128)(2,1)}, bf16[384,1664]{1,0:T(8,128)(2,1)}, bf16[512,384]{1,0:T(8,128)(2,1)}, bf16[512,384]{1,0:T(8,128)(2,1)}, bf16[512,38...) custom-call(s32[7]{0:T(128)} %pad_add_fusion.1.sc, ...), custom_call_target="tpu_custom_call" | custom-call | tf_op jit(solution)/shard_map/front/pallas_call | solution.py:1028
  73.9 4.2 %collective-permute-done.14.pb = f32[80,512]{1,0:T(8,128)S(1)} collective-permute-done((f32[80,512]{1,0:T(8,128)S(1)}, f32[80,512]{1,0:T(8,128)S(1)}, u32[]{:S(2)}, u32[]{:S(2)}) %collective-permute-start.14) | collective-permute-done | bytes 163872 | tf_op jit(solution)/shard_map/ppermute | solution.py:874
  78.8 11.9 %carry.1 = (f32[80,512]{1,0:T(8,128)}, f32[64,8,384]{2,1,0:T(8,128)}, f32[64,8,384]{2,1,0:T(8,128)}, f32[64,8,384]{2,1,0:T(8,128)}, f32[512,384]{1,0:T(8,128)}, /*index=5*/f32[4,24,384]{2,1,0:T(8,128)}) custom-call(s32[7]{0:T(128)} %pad_add_fusion.1.sc, f32[80,512]{1,0:T(8,128)} %copy-done.10, f32[80,512]{1,0:T(8,128)} %copy-done.25, ...), custom_call_target="tpu_custom_call" | custom-call | tf_op jit(solution)/shard_map/carry/pallas_call | solution.py:1032
  91.6 1.9 collective-permute-start.16
  93.5 2.5 collective-permute-start.17
  96.6 2.7 collective-permute-done.17.rest_2_
  99.9 26.7 %scan.1 = (bf16[512,384]{1,0:T(8,128)(2,1)}, bf16[512,384]{1,0:T(8,128)(2,1)}, f32[512,384]{1,0:T(8,128)}, bf16[512,384]{1,0:T(8,128)(2,1)}, f32[80,512]{1,0:T(8...) custom-call(s32[7]{0:T(128)} %pad_add_fusion.1.sc, ...), custom_call_target="tpu_custom_call" | custom-call | tf_op jit(solution)/shard_map/scan/pallas_call | solution.py:1036
  127.7 1.7 collective-permute-start.32
  133.5 4.8 %collective-permute-done.19.db_ = f32[80,512]{1,0:T(8,128)S(1)} collective-permute-done((f32[80,512]{1,0:T(8,128)S(1)}, f32[80,512]{1,0:T(8,128)S(1)}, u32[]{:S(2)}, u32[]{:S(2)}) %collective-permute-start.19) | collective-permute-done | bytes 163872 | tf_op jit(solution)/shard_map/ppermute | solution.py:874
  139.0 5.7 %back.1 = (f32[512,384]{1,0:T(8,128)}, f32[8,384]{1,0:T(8,128)}, bf16[384,896]{1,0:T(8,128)(2,1)}, f32[24,384]{1,0:T(8,128)}) custom-call(s32[7]{0:T(128)} %pad_add_fusion.1.sc, f32[80,512]{1,0:T(8,128)} %copy-done.9, f32[80,512]{1,0:T(8,128)} %copy-done.24, f32[512,384]{1,0:T(8,128)} %get-tuple-element.115.du1, f32[512,384]{1,0:T(8,128)} %get-tuple-element.116.v, ...), custom_call_target="tpu_custom_call" | custom-call | tf_op jit(solution)/shard_map/back/pallas_call | solution.py:1045
  146.2 1.7 constant_dynamic-slice_fusion.7
  148.3 2.2 collective-permute-done.21.spill
  151.1 5.5 %last.1 = (bf16[256,1536]{1,0:T(8,128)(2,1)}, bf16[256,1536]{1,0:T(8,128)(2,1)}, f32[1,768]{1,0:T(1,128)}) custom-call(f32[512,384]{1,0:T(8,128)} %get-tuple-element.122.dxu, f32[8,384]{1,0:T(8,128)} %copy-done.42, bf16[512,384]{1,0:T(8,128)(2,1)} %get-tuple-element.124.dz, bf16[384,768]{1,0:T(8,128)(2,1)} %get-tuple-element.125.wa, ...), custom_call_target="tpu_custom_call" | custom-call | tf_op jit(solution)/shard_map/last/pallas_call | solution.py:1050
  163.9 5.8 %collective-permute-done.33 = bf16[2,1,48,1536]{3,2,1,0:T(8,128)(2,1)} collective-permute-done((bf16[2,1,48,1536]{3,2,1,0:T(8,128)(2,1)}, bf16[2,1,48,1536]{3,2,1,0:T(8,128)(2,1)}, u32[]{:S(2)}, u32[]{:S(2)}) %collective-permute-start.33) | collective-permute-done | bytes 294944 | tf_op jit(solution)/shard_map/ppermute | solution.py:874
  173.4 5.0 %collective-permute-done.23 = bf16[2,1,48,896]{3,2,1,0:T(8,128)(2,1)S(1)} collective-permute-done((bf16[2,1,48,896]{3,2,1,0:T(8,128)(2,1)S(1)}, bf16[2,1,48,896]{3,2,1,0:T(8,128)(2,1)S(1)}, u32[]{:S(2)}, u32[]{:S(2)}) %collective-permute-start.23) | collective-permute-done | bytes 172064 | tf_op jit(solution)/shard_map/ppermute | solution.py:874
  178.6 3.8 %collective-permute-done.34 = bf16[1,1,48,1536]{3,2,1,0:T(8,128)(2,1)S(1)} collective-permute-done((bf16[1,1,48,1536]{3,2,1,0:T(8,128)(2,1)S(1)}, bf16[1,1,48,1536]{3,2,1,0:T(8,128)(2,1)S(1)}, u32[]{:S(2)}, u32[]{:S(2)}) %collective-permute-start.34) | collective-permute-done | bytes 147488 | tf_op jit(solution)/shard_map/ppermute | solution.py:874
  183.2 3.0 gram_out.1
  187.6 2.7 norm_back.1
  190.3 5.8 %gram_in.1 = (f32[48,2,768]{2,1,0:T(2,128)}, f32[48,2,768]{2,1,0:T(2,128)}, f32[48,80]{1,0:T(8,128)}, f32[48,80]{1,0:T(8,128)}, f32[48,48]{1,0:T(8,128)}, /*inde...) custom-call(s32[2]{0:T(128)} %pad_add_fusion.rsc.place, ...), custom_call_target="tpu_custom_call" | custom-call | tf_op jit(solution)/shard_map/gram_in/pallas_call | solution.py:1074
  200.0 1.7 add.157
  205.3 4.2 %collective-permute-start.26 = (bf16[32,1536]{1,0:T(8,128)(2,1)S(1)}, bf16[32,1536]{1,0:T(8,128)(2,1)S(1)}, u32[]{:S(2)}, u32[]{:S(2)}) collective-permute-start(bf16[32,1536]{1,0:T(8,128)(2,1)S(1)} %get-tuple-element.176), channel_id=1, source_target_pairs={{0,4},{4,0},{8,12},{12,8},{1,5},{5,1},{9,13},{13,9},{2,6},{6,2},{1... | collective-permute-start | bytes 294920 | tf_op jit(solution)/shard_map/ppermute | solution.py:874
  209.6 4.5 %collective-permute-done.43 = f32[288,384]{1,0:T(8,128)S(1)} collective-permute-done((f32[288,384]{1,0:T(8,128)S(1)}, f32[288,384]{1,0:T(8,128)S(1)}, u32[]{:S(2)}, u32[]{:S(2)}) %collective-permute-start.43) | collective-permute-done | bytes 442400 | tf_op jit(solution)/shard_map/ppermute | solution.py:874
  215.7 1.8 collective-permute-start.37
  217.5 3.4 %collective-permute-done.44 = f32[144,384]{1,0:T(8,128)S(1)} collective-permute-done((f32[144,384]{1,0:T(8,128)S(1)}, f32[144,384]{1,0:T(8,128)S(1)}, u32[]{:S(2)}, u32[]{:S(2)}) %collective-permute-start.44) | collective-permute-done | bytes 221216 | tf_op jit(solution)/shard_map/ppermute | solution.py:874
  223.2 2.6 collective-permute-done.45
  228.9 5.9 %collective-permute-done.46 = f32[72,384]{1,0:T(8,128)S(1)} collective-permute-done((f32[72,384]{1,0:T(8,128)S(1)}, f32[72,384]{1,0:T(8,128)S(1)}, u32[]{:S(2)}, u32[]{:S(2)}) %collective-permute-start.46) | collective-permute-done | bytes 110624 | tf_op jit(solution)/shard_map/ppermute | solution.py:874
  234.9 1.6 collective-permute-start.30
  236.6 2.1 collective-permute-start.40
  239.7 1.7 collective-permute-start.48
  243.0 3.4 %collective-permute-done.48 = f32[144,384]{1,0:T(8,128)S(1)} collective-permute-done((f32[144,384]{1,0:T(8,128)S(1)}, f32[144,384]{1,0:T(8,128)S(1)}, u32[]{:S(2)}, u32[]{:S(2)}) %collective-permute-start.48) | collective-permute-done | bytes 221216 | tf_op jit(solution)/shard_map/ppermute | solution.py:874
  246.5 1.6 collective-permute-start.49
  248.1 1.8 collective-permute-done.41
  255.8 2.5 collective-permute-done.42
  263.7 4.3 %final.1 = (bf16[512,768]{1,0:T(8,128)(2,1)}, bf16[512,768]{1,0:T(8,128)(2,1)}) custom-call(bf16[512,512]{1,0:T(8,128)(2,1)} %get-tuple-element.95.fin, bf16[128,1536]{1,0:T(8,128)(2,1)} %copy-done.4, bf16[128,1536]{1,0:T(8,128)(2,1)} %copy-done.14, bf16[128,1536]{1,0:T(8,128)(2,1)} %copy-done.13, bf16[128,1536]{1,0:T(8,128)(2,1)} %copy-done.16), custom_call_target="tpu_custom_call" | custom-call | tf_op jit(solution)/shard_map/final/pallas_call | solution.py:1062
  268.1 33.7 %muon.1 = (f32[96,768]{1,0:T(8,128)}, f32[96,768]{1,0:T(8,128)}) custom-call(s32[2]{0:T(128)} %pad_add_fusion.rsc.place, f32[576,768]{1,0:T(8,128)} %copy-done, f32[96,768]{1,0:T(8,128)} %get-tuple-element.148.um, f32[96,768]{1,0:T(8,128)} %collective-permute-done.51.ua), custom_call_target="tpu_custom_call" | custom-call | tf_op jit(solution)/shard_map/muon/pallas_call | solution.py:1078
  303.6 1.7 multiply_subtract_fusion
  309.8 2.2 finish.1
  (266 shorter events, 81.5 us)
Async XLA Ops:
  6.3 19.7 %collective-permute-start.2 = (bf16[32,1536]{1,0:T(8,128)(2,1)S(1)}, bf16[32,1536]{1,0:T(8,128)(2,1)S(1)}, u32[]{:S(2)}, u32[]{:S(2)}) collective-permute-start(bf16[32,1536]{1,0:T(8,128)(2,1)S(1)} %get-tuple-element.178), channel_id=1, source_target_pairs={{0,12},{4,8},{8,4},{12,0},{1,13},{5,9},{9,5},{13,1},{2,14},{6,10},... | collective-permute-start | bytes 294920 | tf_op jit(solution)/shard_map/ppermute | solution.py:874
  11.5 14.5 %collective-permute-start.1 = (bf16[32,1536]{1,0:T(8,128)(2,1)S(1)}, bf16[32,1536]{1,0:T(8,128)(2,1)S(1)}, u32[]{:S(2)}, u32[]{:S(2)}) collective-permute-start(bf16[32,1536]{1,0:T(8,128)(2,1)S(1)} %get-tuple-element.179), channel_id=1, source_target_pairs={{0,8},{4,12},{8,0},{12,4},{1,9},{5,13},{9,1},{13,5},{2,10},{6,14},... | collective-permute-start | bytes 294920 | tf_op jit(solution)/shard_map/ppermute | solution.py:874
  11.5 14.5 %collective-permute-start = (bf16[32,1536]{1,0:T(8,128)(2,1)S(1)}, bf16[32,1536]{1,0:T(8,128)(2,1)S(1)}, u32[]{:S(2)}, u32[]{:S(2)}) collective-permute-start(bf16[32,1536]{1,0:T(8,128)(2,1)S(1)} %get-tuple-element.180), channel_id=1, source_target_pairs={{0,4},{4,0},{8,12},{12,8},{1,5},{5,1},{9,13},{13,9},{2,6},{6,2},{1... | collective-permute-start | bytes 294920 | tf_op jit(solution)/shard_map/ppermute | solution.py:874
  14.3 4.6 %collective-permute-start.7 = (bf16[48,768]{1,0:T(8,128)(2,1)}, bf16[48,768]{1,0:T(8,128)(2,1)S(1)}, u32[]{:S(2)}, u32[]{:S(2)}) collective-permute-start(bf16[48,768]{1,0:T(8,128)(2,1)} %get-tuple-element.100), channel_id=1, source_target_pairs={{0,16},{16,0},{1,17},{17,1},{2,18},{18,2},{3,19},{19,3},{4,20},{20... | collective-permute-start | bytes 221192 | tf_op jit(solution)/shard_map/ppermute | solution.py:874
  16.0 7.3 %collective-permute-start.10 = (bf16[48,1664]{1,0:T(8,128)(2,1)}, bf16[48,1664]{1,0:T(8,128)(2,1)S(1)}, u32[]{:S(2)}, u32[]{:S(2)}) collective-permute-start(bf16[48,1664]{1,0:T(8,128)(2,1)} %get-tuple-element.101), channel_id=1, source_target_pairs={{0,4},{4,0},{8,12},{12,8},{1,5},{5,1},{9,13},{13,9},{2,6},{6,2},{1... | collective-permute-start | bytes 479240 | tf_op jit(solution)/shard_map/ppermute | solution.py:874
  19.8 25.1 %collective-permute-start.8 = (bf16[96,768]{1,0:T(8,128)(2,1)S(1)}, bf16[96,768]{1,0:T(8,128)(2,1)S(1)}, u32[]{:S(2)}, u32[]{:S(2)}) collective-permute-start(bf16[96,768]{1,0:T(8,128)(2,1)S(1)} %pad_maximum_fusion.7), channel_id=1, source_target_pairs={{0,4},{4,0},{8,12},{12,8},{1,5},{5,1},{9,13},{13,9},{2,6},{6,2},{1... | collective-permute-start | bytes 442376 | tf_op jit(solution)/shard_map/ppermute | solution.py:874
  24.2 16.2 %collective-permute-start.11 = (bf16[96,1664]{1,0:T(8,128)(2,1)S(1)}, bf16[96,1664]{1,0:T(8,128)(2,1)S(1)}, u32[]{:S(2)}, u32[]{:S(2)}) collective-permute-start(bf16[96,1664]{1,0:T(8,128)(2,1)S(1)} %pad_maximum_fusion.4), channel_id=1, source_target_pairs={{0,8},{4,12},{8,0},{12,4},{1,9},{5,13},{9,1},{13,5},{2,10},{6,14},... | collective-permute-start | bytes 958472 | tf_op jit(solution)/shard_map/ppermute | solution.py:874
  26.0 18.3 %collective-permute-start.4 = (bf16[128,1536]{1,0:T(8,128)(2,1)S(1)}, bf16[128,1536]{1,0:T(8,128)(2,1)S(1)}, u32[]{:S(2)}, u32[]{:S(2)}) collective-permute-start(bf16[128,1536]{1,0:T(8,128)(2,1)S(1)} %pad_maximum_fusion.2.rest_0_.own), channel_id=1, source_target_pairs={{0,2},{1,3},{2,0},{3,1},{4,6},{5,7},{6,4},{7,5},{8,10},{9,11},{10,... | collective-permute-start | bytes 1179656 | tf_op jit(solution)/shard_map/ppermute | solution.py:874
  40.4 20.7 %collective-permute-start.12 = (bf16[192,1664]{1,0:T(8,128)(2,1)S(1)}, bf16[192,1664]{1,0:T(8,128)(2,1)S(1)}, u32[]{:S(2)}, u32[]{:S(2)}) collective-permute-start(bf16[192,1664]{1,0:T(8,128)(2,1)S(1)} %constant_dynamic-update-slice_fusion.3.r0), channel_id=1, source_target_pairs={{0,16},{16,0},{1,17},{17,1},{2,18},{18,2},{3,19},{19,3},{4,20},{20... | collective-permute-start | bytes 1916936 | tf_op jit(solution)/shard_map/ppermute | solution.py:874
  44.9 16.3 %collective-permute-start.9 = (bf16[192,768]{1,0:T(8,128)(2,1)S(1)}, bf16[192,768]{1,0:T(8,128)(2,1)S(1)}, u32[]{:S(2)}, u32[]{:S(2)}) collective-permute-start(bf16[192,768]{1,0:T(8,128)(2,1)S(1)} %constant_dynamic-update-slice_fusion.a0), channel_id=1, source_target_pairs={{0,8},{4,12},{8,0},{12,4},{1,9},{5,13},{9,1},{13,5},{2,10},{6,14},... | collective-permute-start | bytes 884744 | tf_op jit(solution)/shard_map/ppermute | solution.py:874
  52.7 8.4 %collective-permute-start.6 = (bf16[8,768]{1,0:T(8,128)(2,1)S(1)}, bf16[8,768]{1,0:T(8,128)(2,1)S(1)}, u32[]{:S(2)}, u32[]{:S(2)}) collective-permute-start(bf16[8,768]{1,0:T(8,128)(2,1)S(1)} %slice.105), channel_id=1, source_target_pairs={{0,4},{4,8},{8,12},{1,5},{5,9},{9,13},{2,6},{6,10},{10,14},{3,7},{... | collective-permute-start | bytes 36872 | tf_op jit(solution)/shard_map/ppermute | solution.py:869
  71.8 6.3 %collective-permute-start.14 = (f32[80,512]{1,0:T(8,128)S(1)}, f32[80,512]{1,0:T(8,128)S(1)}, u32[]{:S(2)}, u32[]{:S(2)}) collective-permute-start(f32[80,512]{1,0:T(8,128)S(1)} %add.143.pa), channel_id=1, source_target_pairs={{0,2},{1,3},{2,0},{3,1},{4,6},{5,7},{6,4},{7,5},{8,10},{9,11},{10,... | collective-permute-start | bytes 491528 | tf_op jit(solution)/shard_map/ppermute | solution.py:874
  91.6 5.1 %collective-permute-start.15 = (f32[24,384]{1,0:T(8,128)S(1)}, f32[24,384]{1,0:T(8,128)S(1)}, u32[]{:S(2)}, u32[]{:S(2)}) collective-permute-start(f32[24,384]{1,0:T(8,128)S(1)} %get-tuple-element.193), channel_id=1, source_target_pairs={{0,4},{4,0},{8,12},{12,8},{1,5},{5,1},{9,13},{13,9},{2,6},{6,2},{1... | collective-permute-start | bytes 110600 | tf_op jit(solution)/shard_map/ppermute | solution.py:874
  91.6 5.0 %collective-permute-start.16 = (f32[24,384]{1,0:T(8,128)S(1)}, f32[24,384]{1,0:T(8,128)S(1)}, u32[]{:S(2)}, u32[]{:S(2)}) collective-permute-start(f32[24,384]{1,0:T(8,128)S(1)} %get-tuple-element.192), channel_id=1, source_target_pairs={{0,8},{4,12},{8,0},{12,4},{1,9},{5,13},{9,1},{13,5},{2,10},{6,14},... | collective-permute-start | bytes 110600 | tf_op jit(solution)/shard_map/ppermute | solution.py:874
  93.5 5.8 %collective-permute-start.17 = (f32[24,384]{1,0:T(8,128)S(1)}, f32[24,384]{1,0:T(8,128)S(1)}, u32[]{:S(2)}, u32[]{:S(2)}) collective-permute-start(f32[24,384]{1,0:T(8,128)S(1)} %get-tuple-element.191), channel_id=1, source_target_pairs={{0,12},{4,8},{8,4},{12,0},{1,13},{5,9},{9,5},{13,1},{2,14},{6,10},... | collective-permute-start | bytes 110600 | tf_op jit(solution)/shard_map/ppermute | solution.py:874
  127.7 30.4 %collective-permute-start.32 = (bf16[1,1,192,1536]{3,2,1,0:T(8,128)(2,1)S(1)}, bf16[1,1,192,1536]{3,2,1,0:T(8,128)(2,1)S(1)}, u32[]{:S(2)}, u32[]{:S(2)}) collective-permute-start(bf16[1,1,192,1536]{3,2,1,0:T(8,128)(2,1)S(1)} %constant_dynamic-slice_fusion.6), channel_id=1, source_target_pairs={{0,16},{16,0},{1,17},{17,1},{2,18},{18,2},{3,19},{19,3},{4,20},{20... | collective-permute-start | bytes 1769480 | tf_op jit(solution)/shard_map/ppermute | solution.py:874
  132.0 6.3 %collective-permute-start.19 = (f32[80,512]{1,0:T(8,128)S(1)}, f32[80,512]{1,0:T(8,128)S(1)}, u32[]{:S(2)}, u32[]{:S(2)}) collective-permute-start(f32[80,512]{1,0:T(8,128)S(1)} %add.144.da_), channel_id=1, source_target_pairs={{0,2},{1,3},{2,0},{3,1},{4,6},{5,7},{6,4},{7,5},{8,10},{9,11},{10,... | collective-permute-start | bytes 491528 | tf_op jit(solution)/shard_map/ppermute | solution.py:874
  144.7 5.8 %collective-permute-start.21 = (f32[8,384]{1,0:T(8,128)}, f32[8,384]{1,0:T(8,128)S(1)}, u32[]{:S(2)}, u32[]{:S(2)}) collective-permute-start(f32[8,384]{1,0:T(8,128)} %get-tuple-element.123), channel_id=1, source_target_pairs={{4,0},{8,4},{12,8},{5,1},{9,5},{13,9},{6,2},{10,6},{14,10},{7,3},{... | collective-permute-start | bytes 36872 | tf_op jit(solution)/shard_map/ppermute | solution.py:869
  148.0 14.9 %collective-permute-start.20 = (bf16[1,1,192,896]{3,2,1,0:T(8,128)(2,1)}, bf16[1,1,192,896]{3,2,1,0:T(8,128)(2,1)}, u32[]{:S(2)}, u32[]{:S(2)}) collective-permute-start(bf16[1,1,192,896]{3,2,1,0:T(8,128)(2,1)} %constant_dynamic-slice_fusion.7), channel_id=1, source_target_pairs={{0,16},{16,0},{1,17},{17,1},{2,18},{18,2},{3,19},{19,3},{4,20},{20... | collective-permute-start | bytes 1032200 | tf_op jit(solution)/shard_map/ppermute | solution.py:874
  156.6 14.2 %collective-permute-start.22 = (bf16[256,1536]{1,0:T(8,128)(2,1)}, bf16[256,1536]{1,0:T(8,128)(2,1)S(1)}, u32[]{:S(2)}, u32[]{:S(2)}) collective-permute-start(bf16[256,1536]{1,0:T(8,128)(2,1)} %get-tuple-element.129), channel_id=1, source_target_pairs={{0,1},{1,0},{2,3},{3,2},{4,5},{5,4},{6,7},{7,6},{8,9},{9,8},{10,11... | collective-permute-start | bytes 2359304 | tf_op jit(solution)/shard_map/ppermute | solution.py:874
  160.1 9.7 %collective-permute-start.33 = (bf16[2,1,48,1536]{3,2,1,0:T(8,128)(2,1)}, bf16[2,1,48,1536]{3,2,1,0:T(8,128)(2,1)}, u32[]{:S(2)}, u32[]{:S(2)}) collective-permute-start(bf16[2,1,48,1536]{3,2,1,0:T(8,128)(2,1)} %dynamic-slice_convert_fusion), channel_id=1, source_target_pairs={{0,4},{4,0},{8,12},{12,8},{1,5},{5,1},{9,13},{13,9},{2,6},{6,2},{1... | collective-permute-start | bytes 884744 | tf_op jit(solution)/shard_map/ppermute | solution.py:874
  171.0 7.4 %collective-permute-start.23 = (bf16[2,1,48,896]{3,2,1,0:T(8,128)(2,1)S(1)}, bf16[2,1,48,896]{3,2,1,0:T(8,128)(2,1)S(1)}, u32[]{:S(2)}, u32[]{:S(2)}) collective-permute-start(bf16[2,1,48,896]{3,2,1,0:T(8,128)(2,1)S(1)} %dynamic-slice_convert_fusion.1), channel_id=1, source_target_pairs={{0,4},{4,0},{8,12},{12,8},{1,5},{5,1},{9,13},{13,9},{2,6},{6,2},{1... | collective-permute-start | bytes 516104 | tf_op jit(solution)/shard_map/ppermute | solution.py:874
  171.5 10.9 %collective-permute-start.34 = (bf16[1,1,48,1536]{3,2,1,0:T(8,128)(2,1)S(1)}, bf16[1,1,48,1536]{3,2,1,0:T(8,128)(2,1)S(1)}, u32[]{:S(2)}, u32[]{:S(2)}) collective-permute-start(bf16[1,1,48,1536]{3,2,1,0:T(8,128)(2,1)S(1)} %dynamic-slice_convert_fusion.2), channel_id=1, source_target_pairs={{0,8},{4,12},{8,0},{12,4},{1,9},{5,13},{9,1},{13,5},{2,10},{6,14},... | collective-permute-start | bytes 442376 | tf_op jit(solution)/shard_map/ppermute | solution.py:874
  172.0 14.9 %collective-permute-start.25 = (bf16[128,1536]{1,0:T(8,128)(2,1)S(1)}, bf16[128,1536]{1,0:T(8,128)(2,1)S(1)}, u32[]{:S(2)}, u32[]{:S(2)}) collective-permute-start(bf16[128,1536]{1,0:T(8,128)(2,1)S(1)} %add_convert_fusion), channel_id=1, source_target_pairs={{0,2},{1,3},{2,0},{3,1},{4,6},{5,7},{6,4},{7,5},{8,10},{9,11},{10,... | collective-permute-start | bytes 1179656 | tf_op jit(solution)/shard_map/ppermute | solution.py:874
  178.5 7.7 %collective-permute-start.24 = (bf16[1,1,48,896]{3,2,1,0:T(8,128)(2,1)S(1)}, bf16[1,1,48,896]{3,2,1,0:T(8,128)(2,1)S(1)}, u32[]{:S(2)}, u32[]{:S(2)}) collective-permute-start(bf16[1,1,48,896]{3,2,1,0:T(8,128)(2,1)S(1)} %dynamic-slice_convert_fusion.3), channel_id=1, source_target_pairs={{0,8},{4,12},{8,0},{12,4},{1,9},{5,13},{9,1},{13,5},{2,10},{6,14},... | collective-permute-start | bytes 258056 | tf_op jit(solution)/shard_map/ppermute | solution.py:874
  201.8 12.3 %collective-permute-start.43 = (f32[288,384]{1,0:T(8,128)S(1)}, f32[288,384]{1,0:T(8,128)S(1)}, u32[]{:S(2)}, u32[]{:S(2)}) collective-permute-start(f32[288,384]{1,0:T(8,128)S(1)} %constant_dynamic-slice_fusion.2), channel_id=1, source_target_pairs={{0,16},{16,0},{1,17},{17,1},{2,18},{18,2},{3,19},{19,3},{4,20},{20... | collective-permute-start | bytes 1327112 | tf_op jit(solution)/shard_map/ppermute | solution.py:874
  203.5 12.1 %collective-permute-start.36 = (f32[288,384]{1,0:T(8,128)S(1)}, f32[288,384]{1,0:T(8,128)S(1)}, u32[]{:S(2)}, u32[]{:S(2)}) collective-permute-start(f32[288,384]{1,0:T(8,128)S(1)} %constant_dynamic-slice_fusion.5), channel_id=1, source_target_pairs={{0,2},{1,3},{2,0},{3,1},{4,6},{5,7},{6,4},{7,5},{8,10},{9,11},{10,... | collective-permute-start | bytes 1327112 | tf_op jit(solution)/shard_map/ppermute | solution.py:874
  205.1 29.8 %collective-permute-start.28 = (bf16[32,1536]{1,0:T(8,128)(2,1)S(1)}, bf16[32,1536]{1,0:T(8,128)(2,1)S(1)}, u32[]{:S(2)}, u32[]{:S(2)}) collective-permute-start(bf16[32,1536]{1,0:T(8,128)(2,1)S(1)} %get-tuple-element.174), channel_id=1, source_target_pairs={{0,12},{4,8},{8,4},{12,0},{1,13},{5,9},{9,5},{13,1},{2,14},{6,10},... | collective-permute-start | bytes 294920 | tf_op jit(solution)/shard_map/ppermute | solution.py:874
  205.2 29.7 %collective-permute-start.27 = (bf16[32,1536]{1,0:T(8,128)(2,1)S(1)}, bf16[32,1536]{1,0:T(8,128)(2,1)S(1)}, u32[]{:S(2)}, u32[]{:S(2)}) collective-permute-start(bf16[32,1536]{1,0:T(8,128)(2,1)S(1)} %get-tuple-element.175), channel_id=1, source_target_pairs={{0,8},{4,12},{8,0},{12,4},{1,9},{5,13},{9,1},{13,5},{2,10},{6,14},... | collective-permute-start | bytes 294920 | tf_op jit(solution)/shard_map/ppermute | solution.py:874
  205.3 29.5 %collective-permute-start.26 = (bf16[32,1536]{1,0:T(8,128)(2,1)S(1)}, bf16[32,1536]{1,0:T(8,128)(2,1)S(1)}, u32[]{:S(2)}, u32[]{:S(2)}) collective-permute-start(bf16[32,1536]{1,0:T(8,128)(2,1)S(1)} %get-tuple-element.176), channel_id=1, source_target_pairs={{0,4},{4,0},{8,12},{12,8},{1,5},{5,1},{9,13},{13,9},{2,6},{6,2},{1... | collective-permute-start | bytes 294920 | tf_op jit(solution)/shard_map/ppermute | solution.py:874
  214.2 6.7 %collective-permute-start.44 = (f32[144,384]{1,0:T(8,128)S(1)}, f32[144,384]{1,0:T(8,128)S(1)}, u32[]{:S(2)}, u32[]{:S(2)}) collective-permute-start(f32[144,384]{1,0:T(8,128)S(1)} %constant_dynamic-slice_fusion.1), channel_id=1, source_target_pairs={{0,2},{1,3},{2,0},{3,1},{4,6},{5,7},{6,4},{7,5},{8,10},{9,11},{10,... | collective-permute-start | bytes 663560 | tf_op jit(solution)/shard_map/ppermute | solution.py:874
  215.7 6.5 %collective-permute-start.37 = (f32[144,384]{1,0:T(8,128)S(1)}, f32[144,384]{1,0:T(8,128)S(1)}, u32[]{:S(2)}, u32[]{:S(2)}) collective-permute-start(f32[144,384]{1,0:T(8,128)S(1)} %constant_dynamic-slice_fusion.4), channel_id=1, source_target_pairs={{0,16},{16,0},{1,17},{17,1},{2,18},{18,2},{3,19},{19,3},{4,20},{20... | collective-permute-start | bytes 663560 | tf_op jit(solution)/shard_map/ppermute | solution.py:874
  221.0 4.8 %collective-permute-start.45 = (f32[72,384]{1,0:T(8,128)S(1)}, f32[72,384]{1,0:T(8,128)S(1)}, u32[]{:S(2)}, u32[]{:S(2)}) collective-permute-start(f32[72,384]{1,0:T(8,128)S(1)} %constant_dynamic-slice_fusion), channel_id=1, source_target_pairs={{0,4},{4,0},{8,12},{12,8},{1,5},{5,1},{9,13},{13,9},{2,6},{6,2},{1... | collective-permute-start | bytes 331784 | tf_op jit(solution)/shard_map/ppermute | solution.py:874
  222.3 5.2 %collective-permute-start.38 = (f32[72,384]{1,0:T(8,128)S(1)}, f32[72,384]{1,0:T(8,128)S(1)}, u32[]{:S(2)}, u32[]{:S(2)}) collective-permute-start(f32[72,384]{1,0:T(8,128)S(1)} %constant_dynamic-slice_fusion.3), channel_id=1, source_target_pairs={{0,4},{4,0},{8,12},{12,8},{1,5},{5,1},{9,13},{13,9},{2,6},{6,2},{1... | collective-permute-start | bytes 331784 | tf_op jit(solution)/shard_map/ppermute | solution.py:874
  225.8 9.0 %collective-permute-start.46 = (f32[72,384]{1,0:T(8,128)S(1)}, f32[72,384]{1,0:T(8,128)S(1)}, u32[]{:S(2)}, u32[]{:S(2)}) collective-permute-start(f32[72,384]{1,0:T(8,128)S(1)} %dynamic-slice_add_fusion.4), channel_id=1, source_target_pairs={{0,8},{4,12},{8,0},{12,4},{1,9},{5,13},{9,1},{13,5},{2,10},{6,14},... | collective-permute-start | bytes 331784 | tf_op jit(solution)/shard_map/ppermute | solution.py:874
  227.5 9.1 %collective-permute-start.39 = (f32[72,384]{1,0:T(8,128)S(1)}, f32[72,384]{1,0:T(8,128)S(1)}, u32[]{:S(2)}, u32[]{:S(2)}) collective-permute-start(f32[72,384]{1,0:T(8,128)S(1)} %dynamic-slice_add_fusion.5), channel_id=1, source_target_pairs={{0,8},{4,12},{8,0},{12,4},{1,9},{5,13},{9,1},{13,5},{2,10},{6,14},... | collective-permute-start | bytes 331784 | tf_op jit(solution)/shard_map/ppermute | solution.py:874
  234.8 4.9 %collective-permute-start.47 = (f32[72,384]{1,0:T(8,128)S(1)}, f32[72,384]{1,0:T(8,128)S(1)}, u32[]{:S(2)}, u32[]{:S(2)}) collective-permute-start(f32[72,384]{1,0:T(8,128)S(1)} %add.175), channel_id=1, source_target_pairs={{0,4},{4,0},{8,12},{12,8},{1,5},{5,1},{9,13},{13,9},{2,6},{6,2},{1... | collective-permute-start | bytes 331784 | tf_op jit(solution)/shard_map/ppermute | solution.py:874
  234.9 19.3 %collective-permute-start.30 = (bf16[128,1536]{1,0:T(8,128)(2,1)S(1)}, bf16[128,1536]{1,0:T(8,128)(2,1)S(1)}, u32[]{:S(2)}, u32[]{:S(2)}) collective-permute-start(bf16[128,1536]{1,0:T(8,128)(2,1)S(1)} %pad_maximum_fusion.3.rest_0_), channel_id=1, source_target_pairs={{0,2},{1,3},{2,0},{3,1},{4,6},{5,7},{6,4},{7,5},{8,10},{9,11},{10,... | collective-permute-start | bytes 1179656 | tf_op jit(solution)/shard_map/ppermute | solution.py:874
  236.6 4.8 %collective-permute-start.40 = (f32[72,384]{1,0:T(8,128)S(1)}, f32[72,384]{1,0:T(8,128)S(1)}, u32[]{:S(2)}, u32[]{:S(2)}) collective-permute-start(f32[72,384]{1,0:T(8,128)S(1)} %add.167), channel_id=1, source_target_pairs={{0,4},{4,0},{8,12},{12,8},{1,5},{5,1},{9,13},{13,9},{2,6},{6,2},{1... | collective-permute-start | bytes 331784 | tf_op jit(solution)/shard_map/ppermute | solution.py:874
  239.7 6.7 %collective-permute-start.48 = (f32[144,384]{1,0:T(8,128)S(1)}, f32[144,384]{1,0:T(8,128)S(1)}, u32[]{:S(2)}, u32[]{:S(2)}) collective-permute-start(f32[144,384]{1,0:T(8,128)S(1)} %pad_maximum_fusion.6), channel_id=1, source_target_pairs={{0,2},{1,3},{2,0},{3,1},{4,6},{5,7},{6,4},{7,5},{8,10},{9,11},{10,... | collective-permute-start | bytes 663560 | tf_op jit(solution)/shard_map/ppermute | solution.py:874
  241.5 8.4 %collective-permute-start.41 = (f32[144,384]{1,0:T(8,128)S(1)}, f32[144,384]{1,0:T(8,128)S(1)}, u32[]{:S(2)}, u32[]{:S(2)}) collective-permute-start(f32[144,384]{1,0:T(8,128)S(1)} %pad_maximum_fusion.5), channel_id=1, source_target_pairs={{0,16},{16,0},{1,17},{17,1},{2,18},{18,2},{3,19},{19,3},{4,20},{20... | collective-permute-start | bytes 663560 | tf_op jit(solution)/shard_map/ppermute | solution.py:874
  246.5 9.3 %collective-permute-start.49 = (f32[288,384]{1,0:T(8,128)S(1)}, f32[288,384]{1,0:T(8,128)S(1)}, u32[]{:S(2)}, u32[]{:S(2)}) collective-permute-start(f32[288,384]{1,0:T(8,128)S(1)} %pad_maximum_fusion.1), channel_id=1, source_target_pairs={{0,16},{16,0},{1,17},{17,1},{2,18},{18,2},{3,19},{19,3},{4,20},{20... | collective-permute-start | bytes 1327112 | tf_op jit(solution)/shard_map/ppermute | solution.py:874
  249.9 8.4 %collective-permute-start.42 = (f32[288,384]{1,0:T(8,128)S(1)}, f32[288,384]{1,0:T(8,128)S(1)}, u32[]{:S(2)}, u32[]{:S(2)}) collective-permute-start(f32[288,384]{1,0:T(8,128)S(1)} %pad_maximum_fusion), channel_id=1, source_target_pairs={{0,2},{1,3},{2,0},{3,1},{4,6},{5,7},{6,4},{7,5},{8,10},{9,11},{10,... | collective-permute-start | bytes 1327112 | tf_op jit(solution)/shard_map/ppermute | solution.py:874
  253.7 14.4 %collective-permute-start.51 = (f32[96,768]{1,0:T(8,128)}, f32[96,768]{1,0:T(8,128)}, u32[]{:S(2)}, u32[]{:S(2)}) collective-permute-start(f32[96,768]{1,0:T(8,128)} %get-tuple-element.149), channel_id=1, source_target_pairs={{0,1},{1,0},{2,3},{3,2},{4,5},{5,4},{6,7},{7,6},{8,9},{9,8},{10,11... | collective-permute-start | bytes 884744 | tf_op jit(solution)/shard_map/ppermute | solution.py:874
  253.7 9.2 %collective-permute-start.29 = (bf16[128,1536]{1,0:T(8,128)(2,1)S(1)}, bf16[128,1536]{1,0:T(8,128)(2,1)S(1)}, u32[]{:S(2)}, u32[]{:S(2)}) collective-permute-start(bf16[128,1536]{1,0:T(8,128)(2,1)S(1)} %pad_maximum_fusion.3.rest_0_), channel_id=1, source_target_pairs={{0,1},{1,0},{2,3},{3,2},{4,5},{5,4},{6,7},{7,6},{8,9},{9,8},{10,11... | collective-permute-start | bytes 1179656 | tf_op jit(solution)/shard_map/ppermute | solution.py:874
  254.2 8.6 %collective-permute-start.31 = (bf16[128,1536]{1,0:T(8,128)(2,1)S(1)}, bf16[128,1536]{1,0:T(8,128)(2,1)S(1)}, u32[]{:S(2)}, u32[]{:S(2)}) collective-permute-start(bf16[128,1536]{1,0:T(8,128)(2,1)S(1)} %collective-permute-done.30.rest_2_), channel_id=1, source_target_pairs={{0,1},{1,0},{2,3},{3,2},{4,5},{5,4},{6,7},{7,6},{8,9},{9,8},{10,11... | collective-permute-start | bytes 1179656 | tf_op jit(solution)/shard_map/ppermute | solution.py:874
  259.2 43.1 %collective-permute-start.50 = (f32[48,768]{1,0:T(8,128)}, f32[48,768]{1,0:T(8,128)}, u32[]{:S(2)}, u32[]{:S(2)}) collective-permute-start(f32[48,768]{1,0:T(8,128)} %slice.135), channel_id=1, source_target_pairs={{0,1},{1,0},{2,3},{3,2},{4,5},{5,4},{6,7},{7,6},{8,9},{9,8},{10,11... | collective-permute-start | bytes 442376 | tf_op jit(solution)/shard_map/ppermute | solution.py:874
  301.8 7.3 %collective-permute-start.52 = (f32[96,768]{1,0:T(8,128)}, f32[96,768]{1,0:T(8,128)S(1)}, u32[]{:S(2)}, u32[]{:S(2)}) collective-permute-start(f32[96,768]{1,0:T(8,128)} %get-tuple-element.151), channel_id=1, source_target_pairs={{0,1},{1,0},{2,3},{3,2},{4,5},{5,4},{6,7},{7,6},{8,9},{9,8},{10,11... | collective-permute-start | bytes 884744 | tf_op jit(solution)/shard_map/ppermute | solution.py:874
  (49 other events, 448.8 us)

commit v4 on v3

--- a/solution.py
+++ b/solution.py
@@ -768,7 +768,7 @@
             self.acc[self.at(i), i * b : n] = a
             self.put(i, a, self.ah, self.al)
 
-    def apply(self):
+    def factor(self):
         for i in range(self.blocks):
             tail = slice(i * self.nbk, self.n)
             a2 = mul3(self.ah[self.at(i), :], self.al[self.at(i), :], self.ah[:, tail], self.al[:, tail])
@@ -776,14 +776,26 @@
             c = lax.broadcasted_iota(jnp.int32, a2.shape, 1)
             q = jnp.where(r == c, NS_A, 0.0) + (NS_B * self.acc[self.at(i), tail] + NS_C * a2)
             self.put(i, q, self.qh, self.ql)
+
+    def apply(self):
+        self.factor()
         h, l = halves(self.xs[...])
         self.xs[...] = mul3(h, l, self.qh[...], self.ql[...])
 
     def advance(self):
+        self.factor()
         for src, dst in (((self.ah, self.al), (self.th, self.tl)), ((self.th, self.tl), (self.ah, self.al))):
             for i in range(self.blocks):
                 tail = slice(i * self.nbk, self.n)
-                a = mul3(src[0][self.at(i), :], src[1][self.at(i), :], self.qh[:, tail], self.ql[:, tail])
+                h, l = src[0][self.at(i), :], src[1][self.at(i), :]
+                joined = i == 0 and src[0] is self.ah
+                if joined:
+                    xh, xl = halves(self.xs[...])
+                    h, l = jnp.concatenate([h, xh], axis=0), jnp.concatenate([l, xl], axis=0)
+                a = mul3(h, l, self.qh[:, tail], self.ql[:, tail])
+                if joined:
+                    self.xs[...] = a[self.nbk :]
+                    a = a[0 : self.nbk]
                 if dst[0] is self.ah:
                     self.acc[self.at(i), tail] = a
                 self.put(i, a, *dst)
@@ -811,8 +823,6 @@
         s.start([small], jnp.concatenate([um[rows:, 0:LANES], ua[rows:, 0:LANES]], axis=0))
 
         def step(k, c):
-            p.apply()
-            s.apply()
             p.advance()
             s.advance()
             return c

time: 314 us -> 313 us (level)
  no operation moved by 1% of the time
where the time goes in v4:
time: 313 us; the launch traced here: 312 us
  Pallas kernels  121 us (39%)
  waiting for transfers between devices  82.1 us (26%)
  starting transfers between devices  57.2 us (18%)
  local copies, waits for them, and re-layouts  32.5 us (10%)
  other arithmetic  17 us (5%)
    ppermute x51, waiting for transfers between devices, swap(): return lax.ppermute(value, axis, [(i, i ^ bit) for i in range(devices)])  80 us
    ppermute x51, starting transfers between devices, swap(): return lax.ppermute(value, axis, [(i, i ^ bit) for i in range(devices)])  51.7 us
    pallas_call x1, Pallas kernels, on_device(): make_muon(width, own_rows, xw, rank, pack, full)  33.5 us
    pallas_call x1, Pallas kernels, on_device(): make_scan(tokens, channels, width, docs, xw, rank, states, ctx_count)  26.7 us
    unnamed x102, local copies, waits for them, and re-layouts  14.6 us
    pallas_call x1, Pallas kernels, on_device(): make_carry(tokens, channels, docs, xw, rank, states, ctx_count)  11.9 us
    pallas_call x1, Pallas kernels, on_device(): make_front(tokens, channels, width, docs, xw, rank, ctx_count, fsdp_count...  7.1 us
  transfers between devices with their start and end apart: 53, of which 27 were waited for; matrix products, arithmetic and copies ran while one was open for 11% of the time, Pallas kernels for 18%

profile of v4, /device:TPU:0, one launch (start us, length us, event | category | flops | bytes accessed | tf_op | source)
XLA Modules:
  0.0 312.0 jit_solution(13913566594423590351)
XLA Ops:
  2.6 2.7 send.1
  6.3 5.1 %collective-permute-start.2 = (bf16[32,1536]{1,0:T(8,128)(2,1)S(1)}, bf16[32,1536]{1,0:T(8,128)(2,1)S(1)}, u32[]{:S(2)}, u32[]{:S(2)}) collective-permute-start(bf16[32,1536]{1,0:T(8,128)(2,1)S(1)} %get-tuple-element.178), channel_id=1, source_target_pairs={{0,12},{4,8},{8,4},{12,0},{1,13},{5,9},{9,5},{13,1},{2,14},{6,10},... | collective-permute-start | bytes 294920 | tf_op jit(solution)/shard_map/ppermute | solution.py:884
  12.1 2.2 pack.1
  14.3 1.7 collective-permute-start.7
  21.2 2.0 collective-permute-done.10
  24.2 1.8 collective-permute-start.11
  27.6 12.8 %collective-permute-done.11 = bf16[96,1664]{1,0:T(8,128)(2,1)S(1)} collective-permute-done((bf16[96,1664]{1,0:T(8,128)(2,1)S(1)}, bf16[96,1664]{1,0:T(8,128)(2,1)S(1)}, u32[]{:S(2)}, u32[]{:S(2)}) %collective-permute-start.11) | collective-permute-done | bytes 319520 | tf_op jit(solution)/shard_map/ppermute | solution.py:884
  40.9 2.7 plan.1
  47.4 4.6 %recv.1 = (bf16[512,768]{1,0:T(8,128)(2,1)}, bf16[512,768]{1,0:T(8,128)(2,1)}, bf16[512,768]{1,0:T(8,128)(2,1)}) custom-call(bf16[512,512]{1,0:T(8,128)(2,1)} %get-tuple-element.96.rt, f32[1,768]{1,0:T(1,128)} %reshape.170.gain, bf16[128,1536]{1,0:T(8,128)(2,1)} %copy-done.1, bf16[128,1536]{1,0:T(8,128)(2,1)} %copy-done.17, bf16[128,1536]{1,0:T(8,128)(2,1)} %copy-done.15, ...), custom_call_target="tpu_custom_call" | custom-call | tf_op jit(solution)/shard_map/recv/pallas_call | solution.py:1033
  52.7 4.1 %collective-permute-start.6 = (bf16[8,768]{1,0:T(8,128)(2,1)S(1)}, bf16[8,768]{1,0:T(8,128)(2,1)S(1)}, u32[]{:S(2)}, u32[]{:S(2)}) collective-permute-start(bf16[8,768]{1,0:T(8,128)(2,1)S(1)} %slice.105), channel_id=1, source_target_pairs={{0,4},{4,8},{8,12},{1,5},{5,9},{9,13},{2,6},{6,10},{10,14},{3,7},{... | collective-permute-start | bytes 36872 | tf_op jit(solution)/shard_map/ppermute | solution.py:879
  58.0 3.2 %collective-permute-done.9.a1 = bf16[192,768]{1,0:T(8,128)(2,1)S(1)} collective-permute-done((bf16[192,768]{1,0:T(8,128)(2,1)S(1)}, bf16[192,768]{1,0:T(8,128)(2,1)S(1)}, u32[]{:S(2)}, u32[]{:S(2)}) %collective-permute-start.9) | collective-permute-done | bytes 294944 | tf_op jit(solution)/shard_map/ppermute | solution.py:884
  62.1 7.1 %front.1 = (bf16[384,768]{1,0:T(8,128)(2,1)}, bf16[384,1664]{1,0:T(8,128)(2,1)}, bf16[512,384]{1,0:T(8,128)(2,1)}, bf16[512,384]{1,0:T(8,128)(2,1)}, bf16[512,38...) custom-call(s32[7]{0:T(128)} %pad_add_fusion.1.sc, ...), custom_call_target="tpu_custom_call" | custom-call | tf_op jit(solution)/shard_map/front/pallas_call | solution.py:1038
  73.9 4.2 %collective-permute-done.14.pb = f32[80,512]{1,0:T(8,128)S(1)} collective-permute-done((f32[80,512]{1,0:T(8,128)S(1)}, f32[80,512]{1,0:T(8,128)S(1)}, u32[]{:S(2)}, u32[]{:S(2)}) %collective-permute-start.14) | collective-permute-done | bytes 163872 | tf_op jit(solution)/shard_map/ppermute | solution.py:884
  78.8 11.9 %carry.1 = (f32[80,512]{1,0:T(8,128)}, f32[64,8,384]{2,1,0:T(8,128)}, f32[64,8,384]{2,1,0:T(8,128)}, f32[64,8,384]{2,1,0:T(8,128)}, f32[512,384]{1,0:T(8,128)}, /*index=5*/f32[4,24,384]{2,1,0:T(8,128)}) custom-call(s32[7]{0:T(128)} %pad_add_fusion.1.sc, f32[80,512]{1,0:T(8,128)} %copy-done.10, f32[80,512]{1,0:T(8,128)} %copy-done.25, ...), custom_call_target="tpu_custom_call" | custom-call | tf_op jit(solution)/shard_map/carry/pallas_call | solution.py:1042
  91.6 1.9 collective-permute-start.16
  93.5 2.5 collective-permute-start.17
  96.6 2.7 collective-permute-done.17.rest_2_
  99.9 26.7 %scan.1 = (bf16[512,384]{1,0:T(8,128)(2,1)}, bf16[512,384]{1,0:T(8,128)(2,1)}, f32[512,384]{1,0:T(8,128)}, bf16[512,384]{1,0:T(8,128)(2,1)}, f32[80,512]{1,0:T(8...) custom-call(s32[7]{0:T(128)} %pad_add_fusion.1.sc, ...), custom_call_target="tpu_custom_call" | custom-call | tf_op jit(solution)/shard_map/scan/pallas_call | solution.py:1046
  127.7 1.7 collective-permute-start.32
  133.5 4.8 %collective-permute-done.19.db_ = f32[80,512]{1,0:T(8,128)S(1)} collective-permute-done((f32[80,512]{1,0:T(8,128)S(1)}, f32[80,512]{1,0:T(8,128)S(1)}, u32[]{:S(2)}, u32[]{:S(2)}) %collective-permute-start.19) | collective-permute-done | bytes 163872 | tf_op jit(solution)/shard_map/ppermute | solution.py:884
  139.0 5.7 %back.1 = (f32[512,384]{1,0:T(8,128)}, f32[8,384]{1,0:T(8,128)}, bf16[384,896]{1,0:T(8,128)(2,1)}, f32[24,384]{1,0:T(8,128)}) custom-call(s32[7]{0:T(128)} %pad_add_fusion.1.sc, f32[80,512]{1,0:T(8,128)} %copy-done.9, f32[80,512]{1,0:T(8,128)} %copy-done.24, f32[512,384]{1,0:T(8,128)} %get-tuple-element.115.du1, f32[512,384]{1,0:T(8,128)} %get-tuple-element.116.v, ...), custom_call_target="tpu_custom_call" | custom-call | tf_op jit(solution)/shard_map/back/pallas_call | solution.py:1055
  146.2 1.7 constant_dynamic-slice_fusion.7
  148.3 2.2 collective-permute-done.21.spill
  151.1 5.5 %last.1 = (bf16[256,1536]{1,0:T(8,128)(2,1)}, bf16[256,1536]{1,0:T(8,128)(2,1)}, f32[1,768]{1,0:T(1,128)}) custom-call(f32[512,384]{1,0:T(8,128)} %get-tuple-element.122.dxu, f32[8,384]{1,0:T(8,128)} %copy-done.42, bf16[512,384]{1,0:T(8,128)(2,1)} %get-tuple-element.124.dz, bf16[384,768]{1,0:T(8,128)(2,1)} %get-tuple-element.125.wa, ...), custom_call_target="tpu_custom_call" | custom-call | tf_op jit(solution)/shard_map/last/pallas_call | solution.py:1060
  163.9 5.8 %collective-permute-done.33 = bf16[2,1,48,1536]{3,2,1,0:T(8,128)(2,1)} collective-permute-done((bf16[2,1,48,1536]{3,2,1,0:T(8,128)(2,1)}, bf16[2,1,48,1536]{3,2,1,0:T(8,128)(2,1)}, u32[]{:S(2)}, u32[]{:S(2)}) %collective-permute-start.33) | collective-permute-done | bytes 294944 | tf_op jit(solution)/shard_map/ppermute | solution.py:884
  173.4 5.0 %collective-permute-done.23 = bf16[2,1,48,896]{3,2,1,0:T(8,128)(2,1)S(1)} collective-permute-done((bf16[2,1,48,896]{3,2,1,0:T(8,128)(2,1)S(1)}, bf16[2,1,48,896]{3,2,1,0:T(8,128)(2,1)S(1)}, u32[]{:S(2)}, u32[]{:S(2)}) %collective-permute-start.23) | collective-permute-done | bytes 172064 | tf_op jit(solution)/shard_map/ppermute | solution.py:884
  178.6 3.8 %collective-permute-done.34 = bf16[1,1,48,1536]{3,2,1,0:T(8,128)(2,1)S(1)} collective-permute-done((bf16[1,1,48,1536]{3,2,1,0:T(8,128)(2,1)S(1)}, bf16[1,1,48,1536]{3,2,1,0:T(8,128)(2,1)S(1)}, u32[]{:S(2)}, u32[]{:S(2)}) %collective-permute-start.34) | collective-permute-done | bytes 147488 | tf_op jit(solution)/shard_map/ppermute | solution.py:884
  183.2 3.0 gram_out.1
  187.6 2.7 norm_back.1
  190.3 5.8 %gram_in.1 = (f32[48,2,768]{2,1,0:T(2,128)}, f32[48,2,768]{2,1,0:T(2,128)}, f32[48,80]{1,0:T(8,128)}, f32[48,80]{1,0:T(8,128)}, f32[48,48]{1,0:T(8,128)}, /*inde...) custom-call(s32[2]{0:T(128)} %pad_add_fusion.rsc.place, ...), custom_call_target="tpu_custom_call" | custom-call | tf_op jit(solution)/shard_map/gram_in/pallas_call | solution.py:1084
  200.0 1.7 add.157
  205.3 4.2 %collective-permute-start.26 = (bf16[32,1536]{1,0:T(8,128)(2,1)S(1)}, bf16[32,1536]{1,0:T(8,128)(2,1)S(1)}, u32[]{:S(2)}, u32[]{:S(2)}) collective-permute-start(bf16[32,1536]{1,0:T(8,128)(2,1)S(1)} %get-tuple-element.176), channel_id=1, source_target_pairs={{0,4},{4,0},{8,12},{12,8},{1,5},{5,1},{9,13},{13,9},{2,6},{6,2},{1... | collective-permute-start | bytes 294920 | tf_op jit(solution)/shard_map/ppermute | solution.py:884
  209.6 4.5 %collective-permute-done.43 = f32[288,384]{1,0:T(8,128)S(1)} collective-permute-done((f32[288,384]{1,0:T(8,128)S(1)}, f32[288,384]{1,0:T(8,128)S(1)}, u32[]{:S(2)}, u32[]{:S(2)}) %collective-permute-start.43) | collective-permute-done | bytes 442400 | tf_op jit(solution)/shard_map/ppermute | solution.py:884
  215.7 1.8 collective-permute-start.37
  217.5 3.4 %collective-permute-done.44 = f32[144,384]{1,0:T(8,128)S(1)} collective-permute-done((f32[144,384]{1,0:T(8,128)S(1)}, f32[144,384]{1,0:T(8,128)S(1)}, u32[]{:S(2)}, u32[]{:S(2)}) %collective-permute-start.44) | collective-permute-done | bytes 221216 | tf_op jit(solution)/shard_map/ppermute | solution.py:884
  223.2 2.6 collective-permute-done.45
  228.9 5.9 %collective-permute-done.46 = f32[72,384]{1,0:T(8,128)S(1)} collective-permute-done((f32[72,384]{1,0:T(8,128)S(1)}, f32[72,384]{1,0:T(8,128)S(1)}, u32[]{:S(2)}, u32[]{:S(2)}) %collective-permute-start.46) | collective-permute-done | bytes 110624 | tf_op jit(solution)/shard_map/ppermute | solution.py:884
  234.9 1.6 collective-permute-start.30
  236.6 2.1 collective-permute-start.40
  239.7 1.7 collective-permute-start.48
  243.0 3.4 %collective-permute-done.48 = f32[144,384]{1,0:T(8,128)S(1)} collective-permute-done((f32[144,384]{1,0:T(8,128)S(1)}, f32[144,384]{1,0:T(8,128)S(1)}, u32[]{:S(2)}, u32[]{:S(2)}) %collective-permute-start.48) | collective-permute-done | bytes 221216 | tf_op jit(solution)/shard_map/ppermute | solution.py:884
  246.5 1.6 collective-permute-start.49
  248.1 1.8 collective-permute-done.41
  255.8 2.5 collective-permute-done.42
  263.7 4.3 %final.1 = (bf16[512,768]{1,0:T(8,128)(2,1)}, bf16[512,768]{1,0:T(8,128)(2,1)}) custom-call(bf16[512,512]{1,0:T(8,128)(2,1)} %get-tuple-element.95.fin, bf16[128,1536]{1,0:T(8,128)(2,1)} %copy-done.4, bf16[128,1536]{1,0:T(8,128)(2,1)} %copy-done.14, bf16[128,1536]{1,0:T(8,128)(2,1)} %copy-done.13, bf16[128,1536]{1,0:T(8,128)(2,1)} %copy-done.16), custom_call_target="tpu_custom_call" | custom-call | tf_op jit(solution)/shard_map/final/pallas_call | solution.py:1072
  268.1 33.5 %muon.1 = (f32[96,768]{1,0:T(8,128)}, f32[96,768]{1,0:T(8,128)}) custom-call(s32[2]{0:T(128)} %pad_add_fusion.rsc.place, f32[576,768]{1,0:T(8,128)} %copy-done, f32[96,768]{1,0:T(8,128)} %get-tuple-element.148.um, f32[96,768]{1,0:T(8,128)} %collective-permute-done.51.ua), custom_call_target="tpu_custom_call" | custom-call | tf_op jit(solution)/shard_map/muon/pallas_call | solution.py:1088
  303.3 1.7 multiply_subtract_fusion
  309.6 2.2 finish.1
  (266 shorter events, 81.5 us)
Async XLA Ops:
  6.3 19.7 %collective-permute-start.2 = (bf16[32,1536]{1,0:T(8,128)(2,1)S(1)}, bf16[32,1536]{1,0:T(8,128)(2,1)S(1)}, u32[]{:S(2)}, u32[]{:S(2)}) collective-permute-start(bf16[32,1536]{1,0:T(8,128)(2,1)S(1)} %get-tuple-element.178), channel_id=1, source_target_pairs={{0,12},{4,8},{8,4},{12,0},{1,13},{5,9},{9,5},{13,1},{2,14},{6,10},... | collective-permute-start | bytes 294920 | tf_op jit(solution)/shard_map/ppermute | solution.py:884
  11.5 14.5 %collective-permute-start.1 = (bf16[32,1536]{1,0:T(8,128)(2,1)S(1)}, bf16[32,1536]{1,0:T(8,128)(2,1)S(1)}, u32[]{:S(2)}, u32[]{:S(2)}) collective-permute-start(bf16[32,1536]{1,0:T(8,128)(2,1)S(1)} %get-tuple-element.179), channel_id=1, source_target_pairs={{0,8},{4,12},{8,0},{12,4},{1,9},{5,13},{9,1},{13,5},{2,10},{6,14},... | collective-permute-start | bytes 294920 | tf_op jit(solution)/shard_map/ppermute | solution.py:884
  11.5 14.5 %collective-permute-start = (bf16[32,1536]{1,0:T(8,128)(2,1)S(1)}, bf16[32,1536]{1,0:T(8,128)(2,1)S(1)}, u32[]{:S(2)}, u32[]{:S(2)}) collective-permute-start(bf16[32,1536]{1,0:T(8,128)(2,1)S(1)} %get-tuple-element.180), channel_id=1, source_target_pairs={{0,4},{4,0},{8,12},{12,8},{1,5},{5,1},{9,13},{13,9},{2,6},{6,2},{1... | collective-permute-start | bytes 294920 | tf_op jit(solution)/shard_map/ppermute | solution.py:884
  14.3 4.6 %collective-permute-start.7 = (bf16[48,768]{1,0:T(8,128)(2,1)}, bf16[48,768]{1,0:T(8,128)(2,1)S(1)}, u32[]{:S(2)}, u32[]{:S(2)}) collective-permute-start(bf16[48,768]{1,0:T(8,128)(2,1)} %get-tuple-element.100), channel_id=1, source_target_pairs={{0,16},{16,0},{1,17},{17,1},{2,18},{18,2},{3,19},{19,3},{4,20},{20... | collective-permute-start | bytes 221192 | tf_op jit(solution)/shard_map/ppermute | solution.py:884
  16.0 7.3 %collective-permute-start.10 = (bf16[48,1664]{1,0:T(8,128)(2,1)}, bf16[48,1664]{1,0:T(8,128)(2,1)S(1)}, u32[]{:S(2)}, u32[]{:S(2)}) collective-permute-start(bf16[48,1664]{1,0:T(8,128)(2,1)} %get-tuple-element.101), channel_id=1, source_target_pairs={{0,4},{4,0},{8,12},{12,8},{1,5},{5,1},{9,13},{13,9},{2,6},{6,2},{1... | collective-permute-start | bytes 479240 | tf_op jit(solution)/shard_map/ppermute | solution.py:884
  19.8 25.1 %collective-permute-start.8 = (bf16[96,768]{1,0:T(8,128)(2,1)S(1)}, bf16[96,768]{1,0:T(8,128)(2,1)S(1)}, u32[]{:S(2)}, u32[]{:S(2)}) collective-permute-start(bf16[96,768]{1,0:T(8,128)(2,1)S(1)} %pad_maximum_fusion.7), channel_id=1, source_target_pairs={{0,4},{4,0},{8,12},{12,8},{1,5},{5,1},{9,13},{13,9},{2,6},{6,2},{1... | collective-permute-start | bytes 442376 | tf_op jit(solution)/shard_map/ppermute | solution.py:884
  24.2 16.2 %collective-permute-start.11 = (bf16[96,1664]{1,0:T(8,128)(2,1)S(1)}, bf16[96,1664]{1,0:T(8,128)(2,1)S(1)}, u32[]{:S(2)}, u32[]{:S(2)}) collective-permute-start(bf16[96,1664]{1,0:T(8,128)(2,1)S(1)} %pad_maximum_fusion.4), channel_id=1, source_target_pairs={{0,8},{4,12},{8,0},{12,4},{1,9},{5,13},{9,1},{13,5},{2,10},{6,14},... | collective-permute-start | bytes 958472 | tf_op jit(solution)/shard_map/ppermute | solution.py:884
  26.0 18.3 %collective-permute-start.4 = (bf16[128,1536]{1,0:T(8,128)(2,1)S(1)}, bf16[128,1536]{1,0:T(8,128)(2,1)S(1)}, u32[]{:S(2)}, u32[]{:S(2)}) collective-permute-start(bf16[128,1536]{1,0:T(8,128)(2,1)S(1)} %pad_maximum_fusion.2.rest_0_.own), channel_id=1, source_target_pairs={{0,2},{1,3},{2,0},{3,1},{4,6},{5,7},{6,4},{7,5},{8,10},{9,11},{10,... | collective-permute-start | bytes 1179656 | tf_op jit(solution)/shard_map/ppermute | solution.py:884
  40.4 20.7 %collective-permute-start.12 = (bf16[192,1664]{1,0:T(8,128)(2,1)S(1)}, bf16[192,1664]{1,0:T(8,128)(2,1)S(1)}, u32[]{:S(2)}, u32[]{:S(2)}) collective-permute-start(bf16[192,1664]{1,0:T(8,128)(2,1)S(1)} %constant_dynamic-update-slice_fusion.3.r0), channel_id=1, source_target_pairs={{0,16},{16,0},{1,17},{17,1},{2,18},{18,2},{3,19},{19,3},{4,20},{20... | collective-permute-start | bytes 1916936 | tf_op jit(solution)/shard_map/ppermute | solution.py:884
  44.9 16.3 %collective-permute-start.9 = (bf16[192,768]{1,0:T(8,128)(2,1)S(1)}, bf16[192,768]{1,0:T(8,128)(2,1)S(1)}, u32[]{:S(2)}, u32[]{:S(2)}) collective-permute-start(bf16[192,768]{1,0:T(8,128)(2,1)S(1)} %constant_dynamic-update-slice_fusion.a0), channel_id=1, source_target_pairs={{0,8},{4,12},{8,0},{12,4},{1,9},{5,13},{9,1},{13,5},{2,10},{6,14},... | collective-permute-start | bytes 884744 | tf_op jit(solution)/shard_map/ppermute | solution.py:884
  52.7 8.4 %collective-permute-start.6 = (bf16[8,768]{1,0:T(8,128)(2,1)S(1)}, bf16[8,768]{1,0:T(8,128)(2,1)S(1)}, u32[]{:S(2)}, u32[]{:S(2)}) collective-permute-start(bf16[8,768]{1,0:T(8,128)(2,1)S(1)} %slice.105), channel_id=1, source_target_pairs={{0,4},{4,8},{8,12},{1,5},{5,9},{9,13},{2,6},{6,10},{10,14},{3,7},{... | collective-permute-start | bytes 36872 | tf_op jit(solution)/shard_map/ppermute | solution.py:879
  71.8 6.3 %collective-permute-start.14 = (f32[80,512]{1,0:T(8,128)S(1)}, f32[80,512]{1,0:T(8,128)S(1)}, u32[]{:S(2)}, u32[]{:S(2)}) collective-permute-start(f32[80,512]{1,0:T(8,128)S(1)} %add.143.pa), channel_id=1, source_target_pairs={{0,2},{1,3},{2,0},{3,1},{4,6},{5,7},{6,4},{7,5},{8,10},{9,11},{10,... | collective-permute-start | bytes 491528 | tf_op jit(solution)/shard_map/ppermute | solution.py:884
  91.6 5.1 %collective-permute-start.15 = (f32[24,384]{1,0:T(8,128)S(1)}, f32[24,384]{1,0:T(8,128)S(1)}, u32[]{:S(2)}, u32[]{:S(2)}) collective-permute-start(f32[24,384]{1,0:T(8,128)S(1)} %get-tuple-element.193), channel_id=1, source_target_pairs={{0,4},{4,0},{8,12},{12,8},{1,5},{5,1},{9,13},{13,9},{2,6},{6,2},{1... | collective-permute-start | bytes 110600 | tf_op jit(solution)/shard_map/ppermute | solution.py:884
  91.6 5.0 %collective-permute-start.16 = (f32[24,384]{1,0:T(8,128)S(1)}, f32[24,384]{1,0:T(8,128)S(1)}, u32[]{:S(2)}, u32[]{:S(2)}) collective-permute-start(f32[24,384]{1,0:T(8,128)S(1)} %get-tuple-element.192), channel_id=1, source_target_pairs={{0,8},{4,12},{8,0},{12,4},{1,9},{5,13},{9,1},{13,5},{2,10},{6,14},... | collective-permute-start | bytes 110600 | tf_op jit(solution)/shard_map/ppermute | solution.py:884
  93.5 5.8 %collective-permute-start.17 = (f32[24,384]{1,0:T(8,128)S(1)}, f32[24,384]{1,0:T(8,128)S(1)}, u32[]{:S(2)}, u32[]{:S(2)}) collective-permute-start(f32[24,384]{1,0:T(8,128)S(1)} %get-tuple-element.191), channel_id=1, source_target_pairs={{0,12},{4,8},{8,4},{12,0},{1,13},{5,9},{9,5},{13,1},{2,14},{6,10},... | collective-permute-start | bytes 110600 | tf_op jit(solution)/shard_map/ppermute | solution.py:884
  127.7 30.4 %collective-permute-start.32 = (bf16[1,1,192,1536]{3,2,1,0:T(8,128)(2,1)S(1)}, bf16[1,1,192,1536]{3,2,1,0:T(8,128)(2,1)S(1)}, u32[]{:S(2)}, u32[]{:S(2)}) collective-permute-start(bf16[1,1,192,1536]{3,2,1,0:T(8,128)(2,1)S(1)} %constant_dynamic-slice_fusion.6), channel_id=1, source_target_pairs={{0,16},{16,0},{1,17},{17,1},{2,18},{18,2},{3,19},{19,3},{4,20},{20... | collective-permute-start | bytes 1769480 | tf_op jit(solution)/shard_map/ppermute | solution.py:884
  132.0 6.3 %collective-permute-start.19 = (f32[80,512]{1,0:T(8,128)S(1)}, f32[80,512]{1,0:T(8,128)S(1)}, u32[]{:S(2)}, u32[]{:S(2)}) collective-permute-start(f32[80,512]{1,0:T(8,128)S(1)} %add.144.da_), channel_id=1, source_target_pairs={{0,2},{1,3},{2,0},{3,1},{4,6},{5,7},{6,4},{7,5},{8,10},{9,11},{10,... | collective-permute-start | bytes 491528 | tf_op jit(solution)/shard_map/ppermute | solution.py:884
  144.7 5.8 %collective-permute-start.21 = (f32[8,384]{1,0:T(8,128)}, f32[8,384]{1,0:T(8,128)S(1)}, u32[]{:S(2)}, u32[]{:S(2)}) collective-permute-start(f32[8,384]{1,0:T(8,128)} %get-tuple-element.123), channel_id=1, source_target_pairs={{4,0},{8,4},{12,8},{5,1},{9,5},{13,9},{6,2},{10,6},{14,10},{7,3},{... | collective-permute-start | bytes 36872 | tf_op jit(solution)/shard_map/ppermute | solution.py:879
  148.0 14.9 %collective-permute-start.20 = (bf16[1,1,192,896]{3,2,1,0:T(8,128)(2,1)}, bf16[1,1,192,896]{3,2,1,0:T(8,128)(2,1)}, u32[]{:S(2)}, u32[]{:S(2)}) collective-permute-start(bf16[1,1,192,896]{3,2,1,0:T(8,128)(2,1)} %constant_dynamic-slice_fusion.7), channel_id=1, source_target_pairs={{0,16},{16,0},{1,17},{17,1},{2,18},{18,2},{3,19},{19,3},{4,20},{20... | collective-permute-start | bytes 1032200 | tf_op jit(solution)/shard_map/ppermute | solution.py:884
  156.6 14.2 %collective-permute-start.22 = (bf16[256,1536]{1,0:T(8,128)(2,1)}, bf16[256,1536]{1,0:T(8,128)(2,1)S(1)}, u32[]{:S(2)}, u32[]{:S(2)}) collective-permute-start(bf16[256,1536]{1,0:T(8,128)(2,1)} %get-tuple-element.129), channel_id=1, source_target_pairs={{0,1},{1,0},{2,3},{3,2},{4,5},{5,4},{6,7},{7,6},{8,9},{9,8},{10,11... | collective-permute-start | bytes 2359304 | tf_op jit(solution)/shard_map/ppermute | solution.py:884
  160.1 9.7 %collective-permute-start.33 = (bf16[2,1,48,1536]{3,2,1,0:T(8,128)(2,1)}, bf16[2,1,48,1536]{3,2,1,0:T(8,128)(2,1)}, u32[]{:S(2)}, u32[]{:S(2)}) collective-permute-start(bf16[2,1,48,1536]{3,2,1,0:T(8,128)(2,1)} %dynamic-slice_convert_fusion), channel_id=1, source_target_pairs={{0,4},{4,0},{8,12},{12,8},{1,5},{5,1},{9,13},{13,9},{2,6},{6,2},{1... | collective-permute-start | bytes 884744 | tf_op jit(solution)/shard_map/ppermute | solution.py:884
  171.0 7.4 %collective-permute-start.23 = (bf16[2,1,48,896]{3,2,1,0:T(8,128)(2,1)S(1)}, bf16[2,1,48,896]{3,2,1,0:T(8,128)(2,1)S(1)}, u32[]{:S(2)}, u32[]{:S(2)}) collective-permute-start(bf16[2,1,48,896]{3,2,1,0:T(8,128)(2,1)S(1)} %dynamic-slice_convert_fusion.1), channel_id=1, source_target_pairs={{0,4},{4,0},{8,12},{12,8},{1,5},{5,1},{9,13},{13,9},{2,6},{6,2},{1... | collective-permute-start | bytes 516104 | tf_op jit(solution)/shard_map/ppermute | solution.py:884
  171.5 10.9 %collective-permute-start.34 = (bf16[1,1,48,1536]{3,2,1,0:T(8,128)(2,1)S(1)}, bf16[1,1,48,1536]{3,2,1,0:T(8,128)(2,1)S(1)}, u32[]{:S(2)}, u32[]{:S(2)}) collective-permute-start(bf16[1,1,48,1536]{3,2,1,0:T(8,128)(2,1)S(1)} %dynamic-slice_convert_fusion.2), channel_id=1, source_target_pairs={{0,8},{4,12},{8,0},{12,4},{1,9},{5,13},{9,1},{13,5},{2,10},{6,14},... | collective-permute-start | bytes 442376 | tf_op jit(solution)/shard_map/ppermute | solution.py:884
  172.0 14.9 %collective-permute-start.25 = (bf16[128,1536]{1,0:T(8,128)(2,1)S(1)}, bf16[128,1536]{1,0:T(8,128)(2,1)S(1)}, u32[]{:S(2)}, u32[]{:S(2)}) collective-permute-start(bf16[128,1536]{1,0:T(8,128)(2,1)S(1)} %add_convert_fusion), channel_id=1, source_target_pairs={{0,2},{1,3},{2,0},{3,1},{4,6},{5,7},{6,4},{7,5},{8,10},{9,11},{10,... | collective-permute-start | bytes 1179656 | tf_op jit(solution)/shard_map/ppermute | solution.py:884
  178.5 7.7 %collective-permute-start.24 = (bf16[1,1,48,896]{3,2,1,0:T(8,128)(2,1)S(1)}, bf16[1,1,48,896]{3,2,1,0:T(8,128)(2,1)S(1)}, u32[]{:S(2)}, u32[]{:S(2)}) collective-permute-start(bf16[1,1,48,896]{3,2,1,0:T(8,128)(2,1)S(1)} %dynamic-slice_convert_fusion.3), channel_id=1, source_target_pairs={{0,8},{4,12},{8,0},{12,4},{1,9},{5,13},{9,1},{13,5},{2,10},{6,14},... | collective-permute-start | bytes 258056 | tf_op jit(solution)/shard_map/ppermute | solution.py:884
  201.8 12.3 %collective-permute-start.43 = (f32[288,384]{1,0:T(8,128)S(1)}, f32[288,384]{1,0:T(8,128)S(1)}, u32[]{:S(2)}, u32[]{:S(2)}) collective-permute-start(f32[288,384]{1,0:T(8,128)S(1)} %constant_dynamic-slice_fusion.2), channel_id=1, source_target_pairs={{0,16},{16,0},{1,17},{17,1},{2,18},{18,2},{3,19},{19,3},{4,20},{20... | collective-permute-start | bytes 1327112 | tf_op jit(solution)/shard_map/ppermute | solution.py:884
  203.5 12.1 %collective-permute-start.36 = (f32[288,384]{1,0:T(8,128)S(1)}, f32[288,384]{1,0:T(8,128)S(1)}, u32[]{:S(2)}, u32[]{:S(2)}) collective-permute-start(f32[288,384]{1,0:T(8,128)S(1)} %constant_dynamic-slice_fusion.5), channel_id=1, source_target_pairs={{0,2},{1,3},{2,0},{3,1},{4,6},{5,7},{6,4},{7,5},{8,10},{9,11},{10,... | collective-permute-start | bytes 1327112 | tf_op jit(solution)/shard_map/ppermute | solution.py:884
  205.1 29.8 %collective-permute-start.28 = (bf16[32,1536]{1,0:T(8,128)(2,1)S(1)}, bf16[32,1536]{1,0:T(8,128)(2,1)S(1)}, u32[]{:S(2)}, u32[]{:S(2)}) collective-permute-start(bf16[32,1536]{1,0:T(8,128)(2,1)S(1)} %get-tuple-element.174), channel_id=1, source_target_pairs={{0,12},{4,8},{8,4},{12,0},{1,13},{5,9},{9,5},{13,1},{2,14},{6,10},... | collective-permute-start | bytes 294920 | tf_op jit(solution)/shard_map/ppermute | solution.py:884
  205.2 29.7 %collective-permute-start.27 = (bf16[32,1536]{1,0:T(8,128)(2,1)S(1)}, bf16[32,1536]{1,0:T(8,128)(2,1)S(1)}, u32[]{:S(2)}, u32[]{:S(2)}) collective-permute-start(bf16[32,1536]{1,0:T(8,128)(2,1)S(1)} %get-tuple-element.175), channel_id=1, source_target_pairs={{0,8},{4,12},{8,0},{12,4},{1,9},{5,13},{9,1},{13,5},{2,10},{6,14},... | collective-permute-start | bytes 294920 | tf_op jit(solution)/shard_map/ppermute | solution.py:884
  205.3 29.5 %collective-permute-start.26 = (bf16[32,1536]{1,0:T(8,128)(2,1)S(1)}, bf16[32,1536]{1,0:T(8,128)(2,1)S(1)}, u32[]{:S(2)}, u32[]{:S(2)}) collective-permute-start(bf16[32,1536]{1,0:T(8,128)(2,1)S(1)} %get-tuple-element.176), channel_id=1, source_target_pairs={{0,4},{4,0},{8,12},{12,8},{1,5},{5,1},{9,13},{13,9},{2,6},{6,2},{1... | collective-permute-start | bytes 294920 | tf_op jit(solution)/shard_map/ppermute | solution.py:884
  214.2 6.7 %collective-permute-start.44 = (f32[144,384]{1,0:T(8,128)S(1)}, f32[144,384]{1,0:T(8,128)S(1)}, u32[]{:S(2)}, u32[]{:S(2)}) collective-permute-start(f32[144,384]{1,0:T(8,128)S(1)} %constant_dynamic-slice_fusion.1), channel_id=1, source_target_pairs={{0,2},{1,3},{2,0},{3,1},{4,6},{5,7},{6,4},{7,5},{8,10},{9,11},{10,... | collective-permute-start | bytes 663560 | tf_op jit(solution)/shard_map/ppermute | solution.py:884
  215.7 6.5 %collective-permute-start.37 = (f32[144,384]{1,0:T(8,128)S(1)}, f32[144,384]{1,0:T(8,128)S(1)}, u32[]{:S(2)}, u32[]{:S(2)}) collective-permute-start(f32[144,384]{1,0:T(8,128)S(1)} %constant_dynamic-slice_fusion.4), channel_id=1, source_target_pairs={{0,16},{16,0},{1,17},{17,1},{2,18},{18,2},{3,19},{19,3},{4,20},{20... | collective-permute-start | bytes 663560 | tf_op jit(solution)/shard_map/ppermute | solution.py:884
  221.0 4.8 %collective-permute-start.45 = (f32[72,384]{1,0:T(8,128)S(1)}, f32[72,384]{1,0:T(8,128)S(1)}, u32[]{:S(2)}, u32[]{:S(2)}) collective-permute-start(f32[72,384]{1,0:T(8,128)S(1)} %constant_dynamic-slice_fusion), channel_id=1, source_target_pairs={{0,4},{4,0},{8,12},{12,8},{1,5},{5,1},{9,13},{13,9},{2,6},{6,2},{1... | collective-permute-start | bytes 331784 | tf_op jit(solution)/shard_map/ppermute | solution.py:884
  222.3 5.2 %collective-permute-start.38 = (f32[72,384]{1,0:T(8,128)S(1)}, f32[72,384]{1,0:T(8,128)S(1)}, u32[]{:S(2)}, u32[]{:S(2)}) collective-permute-start(f32[72,384]{1,0:T(8,128)S(1)} %constant_dynamic-slice_fusion.3), channel_id=1, source_target_pairs={{0,4},{4,0},{8,12},{12,8},{1,5},{5,1},{9,13},{13,9},{2,6},{6,2},{1... | collective-permute-start | bytes 331784 | tf_op jit(solution)/shard_map/ppermute | solution.py:884
  225.8 9.0 %collective-permute-start.46 = (f32[72,384]{1,0:T(8,128)S(1)}, f32[72,384]{1,0:T(8,128)S(1)}, u32[]{:S(2)}, u32[]{:S(2)}) collective-permute-start(f32[72,384]{1,0:T(8,128)S(1)} %dynamic-slice_add_fusion.4), channel_id=1, source_target_pairs={{0,8},{4,12},{8,0},{12,4},{1,9},{5,13},{9,1},{13,5},{2,10},{6,14},... | collective-permute-start | bytes 331784 | tf_op jit(solution)/shard_map/ppermute | solution.py:884
  227.5 9.1 %collective-permute-start.39 = (f32[72,384]{1,0:T(8,128)S(1)}, f32[72,384]{1,0:T(8,128)S(1)}, u32[]{:S(2)}, u32[]{:S(2)}) collective-permute-start(f32[72,384]{1,0:T(8,128)S(1)} %dynamic-slice_add_fusion.5), channel_id=1, source_target_pairs={{0,8},{4,12},{8,0},{12,4},{1,9},{5,13},{9,1},{13,5},{2,10},{6,14},... | collective-permute-start | bytes 331784 | tf_op jit(solution)/shard_map/ppermute | solution.py:884
  234.8 4.9 %collective-permute-start.47 = (f32[72,384]{1,0:T(8,128)S(1)}, f32[72,384]{1,0:T(8,128)S(1)}, u32[]{:S(2)}, u32[]{:S(2)}) collective-permute-start(f32[72,384]{1,0:T(8,128)S(1)} %add.175), channel_id=1, source_target_pairs={{0,4},{4,0},{8,12},{12,8},{1,5},{5,1},{9,13},{13,9},{2,6},{6,2},{1... | collective-permute-start | bytes 331784 | tf_op jit(solution)/shard_map/ppermute | solution.py:884
  234.9 19.3 %collective-permute-start.30 = (bf16[128,1536]{1,0:T(8,128)(2,1)S(1)}, bf16[128,1536]{1,0:T(8,128)(2,1)S(1)}, u32[]{:S(2)}, u32[]{:S(2)}) collective-permute-start(bf16[128,1536]{1,0:T(8,128)(2,1)S(1)} %pad_maximum_fusion.3.rest_0_), channel_id=1, source_target_pairs={{0,2},{1,3},{2,0},{3,1},{4,6},{5,7},{6,4},{7,5},{8,10},{9,11},{10,... | collective-permute-start | bytes 1179656 | tf_op jit(solution)/shard_map/ppermute | solution.py:884
  236.6 4.8 %collective-permute-start.40 = (f32[72,384]{1,0:T(8,128)S(1)}, f32[72,384]{1,0:T(8,128)S(1)}, u32[]{:S(2)}, u32[]{:S(2)}) collective-permute-start(f32[72,384]{1,0:T(8,128)S(1)} %add.167), channel_id=1, source_target_pairs={{0,4},{4,0},{8,12},{12,8},{1,5},{5,1},{9,13},{13,9},{2,6},{6,2},{1... | collective-permute-start | bytes 331784 | tf_op jit(solution)/shard_map/ppermute | solution.py:884
  239.7 6.7 %collective-permute-start.48 = (f32[144,384]{1,0:T(8,128)S(1)}, f32[144,384]{1,0:T(8,128)S(1)}, u32[]{:S(2)}, u32[]{:S(2)}) collective-permute-start(f32[144,384]{1,0:T(8,128)S(1)} %pad_maximum_fusion.6), channel_id=1, source_target_pairs={{0,2},{1,3},{2,0},{3,1},{4,6},{5,7},{6,4},{7,5},{8,10},{9,11},{10,... | collective-permute-start | bytes 663560 | tf_op jit(solution)/shard_map/ppermute | solution.py:884
  241.5 8.4 %collective-permute-start.41 = (f32[144,384]{1,0:T(8,128)S(1)}, f32[144,384]{1,0:T(8,128)S(1)}, u32[]{:S(2)}, u32[]{:S(2)}) collective-permute-start(f32[144,384]{1,0:T(8,128)S(1)} %pad_maximum_fusion.5), channel_id=1, source_target_pairs={{0,16},{16,0},{1,17},{17,1},{2,18},{18,2},{3,19},{19,3},{4,20},{20... | collective-permute-start | bytes 663560 | tf_op jit(solution)/shard_map/ppermute | solution.py:884
  246.5 9.3 %collective-permute-start.49 = (f32[288,384]{1,0:T(8,128)S(1)}, f32[288,384]{1,0:T(8,128)S(1)}, u32[]{:S(2)}, u32[]{:S(2)}) collective-permute-start(f32[288,384]{1,0:T(8,128)S(1)} %pad_maximum_fusion.1), channel_id=1, source_target_pairs={{0,16},{16,0},{1,17},{17,1},{2,18},{18,2},{3,19},{19,3},{4,20},{20... | collective-permute-start | bytes 1327112 | tf_op jit(solution)/shard_map/ppermute | solution.py:884
  249.9 8.4 %collective-permute-start.42 = (f32[288,384]{1,0:T(8,128)S(1)}, f32[288,384]{1,0:T(8,128)S(1)}, u32[]{:S(2)}, u32[]{:S(2)}) collective-permute-start(f32[288,384]{1,0:T(8,128)S(1)} %pad_maximum_fusion), channel_id=1, source_target_pairs={{0,2},{1,3},{2,0},{3,1},{4,6},{5,7},{6,4},{7,5},{8,10},{9,11},{10,... | collective-permute-start | bytes 1327112 | tf_op jit(solution)/shard_map/ppermute | solution.py:884
  253.7 14.4 %collective-permute-start.51 = (f32[96,768]{1,0:T(8,128)}, f32[96,768]{1,0:T(8,128)}, u32[]{:S(2)}, u32[]{:S(2)}) collective-permute-start(f32[96,768]{1,0:T(8,128)} %get-tuple-element.149), channel_id=1, source_target_pairs={{0,1},{1,0},{2,3},{3,2},{4,5},{5,4},{6,7},{7,6},{8,9},{9,8},{10,11... | collective-permute-start | bytes 884744 | tf_op jit(solution)/shard_map/ppermute | solution.py:884
  253.7 9.2 %collective-permute-start.29 = (bf16[128,1536]{1,0:T(8,128)(2,1)S(1)}, bf16[128,1536]{1,0:T(8,128)(2,1)S(1)}, u32[]{:S(2)}, u32[]{:S(2)}) collective-permute-start(bf16[128,1536]{1,0:T(8,128)(2,1)S(1)} %pad_maximum_fusion.3.rest_0_), channel_id=1, source_target_pairs={{0,1},{1,0},{2,3},{3,2},{4,5},{5,4},{6,7},{7,6},{8,9},{9,8},{10,11... | collective-permute-start | bytes 1179656 | tf_op jit(solution)/shard_map/ppermute | solution.py:884
  254.2 8.6 %collective-permute-start.31 = (bf16[128,1536]{1,0:T(8,128)(2,1)S(1)}, bf16[128,1536]{1,0:T(8,128)(2,1)S(1)}, u32[]{:S(2)}, u32[]{:S(2)}) collective-permute-start(bf16[128,1536]{1,0:T(8,128)(2,1)S(1)} %collective-permute-done.30.rest_2_), channel_id=1, source_target_pairs={{0,1},{1,0},{2,3},{3,2},{4,5},{5,4},{6,7},{7,6},{8,9},{9,8},{10,11... | collective-permute-start | bytes 1179656 | tf_op jit(solution)/shard_map/ppermute | solution.py:884
  259.2 42.8 %collective-permute-start.50 = (f32[48,768]{1,0:T(8,128)}, f32[48,768]{1,0:T(8,128)}, u32[]{:S(2)}, u32[]{:S(2)}) collective-permute-start(f32[48,768]{1,0:T(8,128)} %slice.135), channel_id=1, source_target_pairs={{0,1},{1,0},{2,3},{3,2},{4,5},{5,4},{6,7},{7,6},{8,9},{9,8},{10,11... | collective-permute-start | bytes 442376 | tf_op jit(solution)/shard_map/ppermute | solution.py:884
  301.5 7.3 %collective-permute-start.52 = (f32[96,768]{1,0:T(8,128)}, f32[96,768]{1,0:T(8,128)S(1)}, u32[]{:S(2)}, u32[]{:S(2)}) collective-permute-start(f32[96,768]{1,0:T(8,128)} %get-tuple-element.151), channel_id=1, source_target_pairs={{0,1},{1,0},{2,3},{3,2},{4,5},{5,4},{6,7},{7,6},{8,9},{9,8},{10,11... | collective-permute-start | bytes 884744 | tf_op jit(solution)/shard_map/ppermute | solution.py:884
  (49 other events, 448.3 us)
